TPU v7x, 32 devices: a whole 2x2x4 slice. The times are simulated.
32 devices in a mesh: dp: 16 (over z, y, x), mp: 2 (over core).
Axes of the slice: x: 2, y: 2, z: 4, core: 2. Of those that a mesh axis runs over, the one named last changes fastest.
Arguments:
- tokens: bfloat16 [16, 1024, 1024], P('dp'), may hold values from -6 to 6
- doc_lengths: int32 [16, 8], P('dp'), may hold values from 1 to 384, 1024 in all within a row
- pad_counts: int32 [16], P('dp'), may hold values from 0 to 255
- norm_gain: float32 [4, 1024], replicated, may hold values from 0.5 to 1.5
- norm_bias: float32 [4, 1024], replicated, may hold values from -1.5 to 1.5
- qkv_weight: bfloat16 [1024, 3, 1024], P(None, None, 'mp'), may hold values from -0.1875 to 0.1875
- out_weight: bfloat16 [1024, 1024], P('mp'), may hold values from -0.1875 to 0.1875
- up_weight: bfloat16 [1024, 4096], P(None, 'mp'), may hold values from -0.1875 to 0.1875
- down_weight: bfloat16 [4096, 1024], P('mp'), may hold values from -0.09375 to 0.09375
- cotangent: bfloat16 [16, 1024, 1024], P('dp'), may hold values from -6 to 6
Outputs:
- out_tokens: bfloat16 [16, 1024, 1024], P('dp')
- input_grad: bfloat16 [16, 1024, 1024], P('dp')
- gain_grad: float32 [4, 1024], replicated
- bias_grad: float32 [4, 1024], replicated
- qkv_grad: float32 [1024, 3, 1024], P(None, None, 'mp')
- out_grad: float32 [1024, 1024], P('mp')
- up_grad: float32 [1024, 4096], P(None, 'mp')
- down_grad: float32 [4096, 1024], P('mp')
Inputs may be any that keep to these rules, and one draw needn't show every extreme that they name: `doc_lengths`: the 8 document lengths of a row add up to 1024; the last pad_counts positions of a row are padding, whatever document they fall in.
All inputs are finite; a program needn't handle non-finite values.
Results may differ from a plain program's by a relative error of at most 0.02.
Values may be sent and summed in bfloat16 or wider, within the bound.
No kernel may reach another device: no remote copies, remote signals or barrier semaphores. Data moves between devices by JAX's collectives and lax.ppermute only.
A program may use at most 192 MiB of HBM per device.

v0:
```python
import math

import jax
import jax.numpy as jnp
from jax import lax
from jax.sharding import PartitionSpec as P

HEAD_DIM = 64


EPSILON = 1e-05
NEGATIVE = -1e30
GELU_SCALE = 0.7978845608028654


def normalize(values_in, gain_vec, shift_vec):
    mean_vals = jnp.mean(values_in, axis=-1, keepdims=True)
    centred = values_in - mean_vals
    spread = jnp.mean(centred * centred, axis=-1, keepdims=True)
    return centred * lax.rsqrt(spread + EPSILON) * gain_vec + shift_vec


def gelu_tanh(hidden):
    return (
        0.5 * hidden * (1.0 + jnp.tanh(GELU_SCALE * (hidden + 0.044715 * hidden * hidden * hidden)))
    )


def rotate(field_in, cosine, sine_vals):
    half_dim = field_in.shape[-1] // 2
    first_half = field_in[..., :half_dim]
    second_half = field_in[..., half_dim:]
    return jnp.concatenate(
        [
            first_half * cosine - second_half * sine_vals,
            second_half * cosine + first_half * sine_vals,
        ],
        axis=-1,
    )


def rotate_back(grad_in, cosine, sine_vals):
    half_dim = grad_in.shape[-1] // 2
    first_half = grad_in[..., :half_dim]
    second_half = grad_in[..., half_dim:]
    return jnp.concatenate(
        [
            first_half * cosine + second_half * sine_vals,
            second_half * cosine - first_half * sine_vals,
        ],
        axis=-1,
    )


def row_layout(lengths, pad_count, seq_len, half_dim):
    position = jnp.arange(seq_len, dtype=jnp.int32)
    doc_ends = jnp.cumsum(lengths)
    passed = position[:, None] >= doc_ends[None, :]
    segment = jnp.sum(passed.astype(jnp.int32), axis=1)
    start_at = jnp.sum(jnp.where(passed, lengths[None, :], 0), axis=1)
    pad_start = seq_len - pad_count
    is_live = position < pad_start
    segment = jnp.where(is_live, segment, lengths.shape[0])
    start_at = jnp.where(is_live, start_at, pad_start)
    offset = (position - start_at).astype(jnp.float32)
    frequencies = jnp.exp(-math.log(10000.0) * jnp.arange(half_dim, dtype=jnp.float32) / half_dim)
    angles = offset[:, None] * frequencies[None, :]
    return (segment, position, jnp.cos(angles), jnp.sin(angles))


def first_norm(rows_in, gain_all, shift_all):
    return normalize(rows_in, gain_all[0], shift_all[0])


def middle(att_rows, resid_rows, gain_all, shift_all):
    middle_rows = resid_rows + normalize(att_rows, gain_all[1], shift_all[1])
    return (middle_rows, normalize(middle_rows, gain_all[2], shift_all[2]))


def finish(mlp_rows, middle_rows, gain_all, shift_all):
    return middle_rows + normalize(mlp_rows, gain_all[3], shift_all[3])


def contract_rows(left_side, right_side):
    return lax.dot_general(
        left_side, right_side, (((0,), (0,)), ((), ())), preferred_element_type=jnp.float32
    )


def contract_cols(left_side, right_side):
    return lax.dot_general(
        left_side, right_side, (((1,), (1,)), ((), ())), preferred_element_type=jnp.float32
    )


def block_scores(query_blk, key_row, seg_query, pos_query, seg_row, pos_row, score_scale):
    raw_scores = (
        jnp.einsum("qhd,khd->hqk", query_blk, key_row, preferred_element_type=jnp.float32)
        * score_scale
    )
    allowed = (seg_query[:, None] == seg_row[None, :]) & (pos_row[None, :] <= pos_query[:, None])
    return jnp.where(allowed[None], raw_scores, NEGATIVE)


def attention_forward(query_low, key_low, value_low, segment, position):
    row_count, seq_len, head_count, head_size = query_low.shape
    block_len = min(512, seq_len)
    block_count = seq_len // block_len
    score_scale = head_size ** (-0.5)

    def one_row(row_data):
        query_row, key_row, value_row, seg_row, pos_row = row_data

        def one_block(block_data):
            query_blk, seg_query, pos_query = block_data
            scores = block_scores(
                query_blk, key_row, seg_query, pos_query, seg_row, pos_row, score_scale
            )
            row_max = jnp.max(scores, axis=-1, keepdims=True)
            expo_vals = jnp.exp(scores - row_max)
            row_total = jnp.sum(expo_vals, axis=-1, keepdims=True)
            soft_low = (expo_vals / row_total).astype(jnp.bfloat16)
            attended = jnp.einsum(
                "hqk,khd->qhd", soft_low, value_row, preferred_element_type=jnp.float32
            )
            return (attended, (row_max + jnp.log(row_total))[..., 0])

        return lax.map(
            one_block,
            (
                query_row.reshape(block_count, block_len, head_count, head_size),
                seg_row.reshape(block_count, block_len),
                pos_row.reshape(block_count, block_len),
            ),
        )

    return lax.map(one_row, (query_low, key_low, value_low, segment, position))


def attention_backward(query_low, key_low, value_low, segment, position, log_total, grad_att):
    row_count, seq_len, head_count, head_size = query_low.shape
    block_len = min(512, seq_len)
    block_count = seq_len // block_len
    score_scale = head_size ** (-0.5)

    def one_row(row_data):
        query_row, key_row, value_row, seg_row, pos_row, log_row, grad_row = row_data

        def one_block(carried, block_data):
            key_acc, value_acc = carried
            query_blk, grad_blk, seg_query, pos_query, log_blk = block_data
            scores = block_scores(
                query_blk, key_row, seg_query, pos_query, seg_row, pos_row, score_scale
            )
            soft_vals = jnp.exp(scores - log_blk[:, :, None])
            grad_soft = jnp.einsum(
                "qhd,khd->hqk", grad_blk, value_row, preferred_element_type=jnp.float32
            )
            inner_sum = jnp.sum(soft_vals * grad_soft, axis=-1, keepdims=True)
            grad_scores = (soft_vals * (grad_soft - inner_sum)).astype(jnp.bfloat16)
            grad_query = (
                jnp.einsum("hqk,khd->qhd", grad_scores, key_row, preferred_element_type=jnp.float32)
                * score_scale
            )
            key_acc = (
                key_acc
                + jnp.einsum(
                    "hqk,qhd->khd", grad_scores, query_blk, preferred_element_type=jnp.float32
                )
                * score_scale
            )
            value_acc = value_acc + jnp.einsum(
                "hqk,qhd->khd",
                soft_vals.astype(jnp.bfloat16),
                grad_blk,
                preferred_element_type=jnp.float32,
            )
            return ((key_acc, value_acc), grad_query)

        zero_acc = jnp.zeros((seq_len, head_count, head_size), jnp.float32)
        (grad_key, grad_value), grad_query = lax.scan(
            one_block,
            (zero_acc, zero_acc),
            (
                query_row.reshape(block_count, block_len, head_count, head_size),
                grad_row.reshape(block_count, block_len, head_count, head_size),
                seg_row.reshape(block_count, block_len),
                pos_row.reshape(block_count, block_len),
                log_row,
            ),
        )
        return (grad_query.reshape(seq_len, head_count, head_size), grad_key, grad_value)

    return lax.map(one_row, (query_low, key_low, value_low, segment, position, log_total, grad_att))


def body(
    tokens,
    doc_lengths,
    pad_counts,
    norm_gain,
    norm_bias,
    qkv_weight,
    out_weight,
    up_weight,
    down_weight,
    cotangent,
):
    row_count, seq_len, width_all = tokens.shape
    token_count = row_count * seq_len
    inner_here = qkv_weight.shape[2]
    head_count = inner_here // HEAD_DIM
    layout = jax.vmap(row_layout, in_axes=(0, 0, None, None))
    segment, position, cosine, sine_vals = layout(doc_lengths, pad_counts, seq_len, HEAD_DIM // 2)
    cos_heads = cosine[:, :, None, :]
    sin_heads = sine_vals[:, :, None, :]

    def branch_sum(partial_sum):
        return lax.psum(partial_sum.astype(jnp.bfloat16), "mp").astype(jnp.float32)

    def grad_sum(partial_sum):
        return lax.psum(partial_sum.astype(jnp.bfloat16), "mp").astype(jnp.float32)

    residual = tokens.reshape(token_count, width_all).astype(jnp.float32)
    normed_low = first_norm(residual, norm_gain, norm_bias).astype(jnp.bfloat16)
    mixed_proj = jnp.einsum(
        "nd,dce->nce", normed_low, qkv_weight, preferred_element_type=jnp.float32
    )
    mixed_proj = mixed_proj.reshape(row_count, seq_len, 3, head_count, HEAD_DIM)
    query_low = rotate(mixed_proj[:, :, 0], cos_heads, sin_heads).astype(jnp.bfloat16)
    key_low = rotate(mixed_proj[:, :, 1], cos_heads, sin_heads).astype(jnp.bfloat16)
    value_low = mixed_proj[:, :, 2].astype(jnp.bfloat16)
    attended, log_total = attention_forward(query_low, key_low, value_low, segment, position)
    att_low = attended.reshape(token_count, inner_here).astype(jnp.bfloat16)
    att_sum = branch_sum(jnp.dot(att_low, out_weight, preferred_element_type=jnp.float32))
    middle_rows, mlp_norm = middle(att_sum, residual, norm_gain, norm_bias)
    mlp_low = mlp_norm.astype(jnp.bfloat16)
    hidden = jnp.dot(mlp_low, up_weight, preferred_element_type=jnp.float32)
    act_low = gelu_tanh(hidden).astype(jnp.bfloat16)
    mlp_sum = branch_sum(jnp.dot(act_low, down_weight, preferred_element_type=jnp.float32))
    output_rows = finish(mlp_sum, middle_rows, norm_gain, norm_bias)
    out_tokens = output_rows.astype(jnp.bfloat16).reshape(row_count, seq_len, width_all)
    grad_out = cotangent.reshape(token_count, width_all).astype(jnp.float32)
    _, finish_back = jax.vjp(finish, mlp_sum, middle_rows, norm_gain, norm_bias)
    grad_mlp_sum, grad_middle, gain_last, bias_last = finish_back(grad_out)
    grad_mlp_low = grad_mlp_sum.astype(jnp.bfloat16)
    down_grad = contract_rows(act_low, grad_mlp_low)
    grad_act = contract_cols(grad_mlp_low, down_weight)
    _, gelu_back = jax.vjp(gelu_tanh, hidden)
    grad_hidden = gelu_back(grad_act)[0].astype(jnp.bfloat16)
    up_grad = contract_rows(mlp_low, grad_hidden)
    grad_mlp_norm = grad_sum(contract_cols(grad_hidden, up_weight))
    _, middle_back = jax.vjp(middle, att_sum, residual, norm_gain, norm_bias)
    grad_att_sum, grad_resid_mid, gain_mid, bias_mid = middle_back((grad_middle, grad_mlp_norm))
    grad_att_low = grad_att_sum.astype(jnp.bfloat16)
    out_grad = contract_rows(att_low, grad_att_low)
    grad_attended = contract_cols(grad_att_low, out_weight).astype(jnp.bfloat16)
    grad_attended = grad_attended.reshape(row_count, seq_len, head_count, HEAD_DIM)
    grad_query, grad_key, grad_value = attention_backward(
        query_low, key_low, value_low, segment, position, log_total, grad_attended
    )
    grad_mixed = jnp.stack(
        [
            rotate_back(grad_query, cos_heads, sin_heads),
            rotate_back(grad_key, cos_heads, sin_heads),
            grad_value,
        ],
        axis=2,
    )
    grad_mixed = grad_mixed.astype(jnp.bfloat16).reshape(token_count, 3, inner_here)
    qkv_grad = jnp.einsum("nd,nce->dce", normed_low, grad_mixed, preferred_element_type=jnp.float32)
    grad_normed = grad_sum(
        jnp.einsum("nce,dce->nd", grad_mixed, qkv_weight, preferred_element_type=jnp.float32)
    )
    _, first_back = jax.vjp(first_norm, residual, norm_gain, norm_bias)
    grad_resid_first, gain_first, bias_first = first_back(grad_normed)
    input_grad = (
        (grad_resid_mid + grad_resid_first)
        .astype(jnp.bfloat16)
        .reshape(row_count, seq_len, width_all)
    )
    gain_grad = gain_last + gain_mid + gain_first
    bias_grad = bias_last + bias_mid + bias_first
    qkv_grad, out_grad, up_grad, down_grad, gain_grad, bias_grad = (
        lax.psum(qkv_grad.astype(jnp.bfloat16), "dp").astype(jnp.float32),
        lax.psum(out_grad.astype(jnp.bfloat16), "dp").astype(jnp.float32),
        lax.psum(up_grad.astype(jnp.bfloat16), "dp").astype(jnp.float32),
        lax.psum(down_grad.astype(jnp.bfloat16), "dp").astype(jnp.float32),
        lax.psum(gain_grad.astype(jnp.bfloat16), "dp").astype(jnp.float32),
        lax.psum(bias_grad.astype(jnp.bfloat16), "dp").astype(jnp.float32),
    )
    return (out_tokens, input_grad, gain_grad, bias_grad, qkv_grad, out_grad, up_grad, down_grad)


def solution(mesh):
    in_specs = (
        P("dp", None, None),
        P("dp", None),
        P("dp"),
        P(),
        P(),
        P(None, None, "mp"),
        P("mp", None),
        P(None, "mp"),
        P("mp", None),
        P("dp", None, None),
    )
    out_specs = (
        P("dp", None, None),
        P("dp", None, None),
        P(),
        P(),
        P(None, None, "mp"),
        P("mp", None),
        P(None, "mp"),
        P("mp", None),
    )
    return jax.shard_map(body, mesh=mesh, in_specs=in_specs, out_specs=out_specs, check_vma=False)
```

profile of v0, /device:TPU:0, one launch (start us, length us, event | category | flops | bytes accessed | tf_op | source)
XLA Modules:
  0.0 804.0 jit_solution(4252362378498883801)
XLA Ops:
  13.6 4.6 copy.38
  18.2 5.6 convolution_bitcast_fusion
  28.5 3.8 fusion.105
  39.9 30.8 %while.48 = (s32[]{:T(128)}, bf16[2,512,8,64]{1,3,2,0:T(8,128)(2,1)}, f32[2,8,512]{2,1,0:T(8,128)}, s32[2,512]{1,0:T(2,128)S(1)}, s32[1024]{0:T(1024)S(1)}, /*in...) while((s32[]{:T(128)}, ...), condition=%wide.region_8.9_spmd.clone, body=%wide.region_5.8_spmd.clone.sunk | while | flops 1125642240 | bytes 56247912 | solution.py:128
  40.7 4.1 fusion.164
  44.8 4.2 fusion.165
  49.6 5.8 fusion.166
  56.0 4.1 fusion.164
  60.1 4.2 fusion.165
  64.9 5.8 fusion.166
  77.0 24.1 %all-reduce.16.cloned.1.call-done = bf16[1024,1024]{1,0:T(8,128)(2,1)} async-done(((bf16[1024,1024]{1,0:T(8,128)(2,1)}), bf16[1024,1024]{1,0:T(8,128)(2,1)}) %all-reduce.16.cloned.1.call-update) | async-done | bytes 2097168 | tf_op jit(solution)/shard_map/psum | solution.py:219
  109.3 5.5 fusion.115
  118.2 6.3 convolution_convert_fusion.4
  124.6 22.6 %all-reduce.18.cloned.1.call-done = bf16[1024,1024]{1,0:T(8,128)(2,1)} async-done(((bf16[1024,1024]{1,0:T(8,128)(2,1)}), bf16[1024,1024]{1,0:T(8,128)(2,1)}) %all-reduce.18.cloned.1.call-update) | async-done | bytes 2097168 | tf_op jit(solution)/shard_map/psum | solution.py:219
  149.3 3.7 fusion.77
  156.6 14.1 %fusion.38 = bf16[1024,2048]{1,0:T(8,128)(2,1)S(1)} fusion(f32[1024,2048]{1,0:T(8,128)} %copy-done.82, bf16[2048,1024]{1,0:T(8,128)(2,1)S(1)} %copy-done.79, bf16[1024,1024]{1,0:T(8,128)(2,1)S(1)} %copy-done.19, bf16[1,1024,1024]{2,1,0:T(8,128)(2,1)S(1)} %copy-done.17, f32[1024]{0:T(1024)S(1)} %negate_multiply_fusion.3, f32[1024]{0:T(1024)S(1)} %get-tuple-element.390, ...), kind=kOutput, calls=%fused_computation.55 | convolution fusion | flops 4355784704 | bytes 20992000 | tf_op jit(solution)/shard_map/dot_general | solution.py:91
  172.7 5.7 convolution_convert_fusion.3
  178.9 13.6 %convolution_convert_fusion = bf16[2048,1024]{1,0:T(8,128)(2,1)} fusion(f32[1024,2048]{1,0:T(8,128)} %copy-done.82, bf16[1024,1024]{1,0:T(8,128)(2,1)} %all-reduce.18.cloned.1.call-done, bf16[1,1024,1024]{2,1,0:T(8,128)(2,1)} %param.23, f32[1024]{0:T(1024)S(1)} %negate_multiply_fusion.3, f32[1024]{0:T(1024)S(1)} %get-tuple-element.390, ...), kind=kOutput, calls=%fused_computation.131 | convolution fusion | flops 4326424576 | bytes 16797696 | tf_op jit(solution)/shard_map/dot_general | solution.py:85
  192.6 8.5 %all-reduce.20.cloned.1.call-done = bf16[1024,1024]{1,0:T(8,128)(2,1)} async-done(((bf16[1024,1024]{1,0:T(8,128)(2,1)}), bf16[1024,1024]{1,0:T(8,128)(2,1)}) %all-reduce.20.cloned.1.call-update) | async-done | bytes 2097168 | tf_op jit(solution)/shard_map/psum | solution.py:222
  201.0 6.0 convert_reduce_fusion.1
  207.0 4.5 fusion.86
  211.6 7.3 fusion.72
  225.3 3.9 reshape.665
  232.5 139.0 %while.49 = (s32[]{:T(128)}, f32[1024,8,64]{0,2,1:T(8,128)}, f32[1024,8,64]{0,2,1:T(8,128)}, f32[2,512,8,64]{1,0,3,2:T(2,128)}, bf16[2,512,8,64]{1,3,2,0:T(8,128...) while((s32[]{:T(128)}, f32[1024,8,64]{0,2,1:T(8,128)}, ...), condition=%wide.region_26.27_spmd.clone, body=%wide.region_24.26_spmd.clone.sunk | while | flops 2726555648 | bytes 183732096 | solution.py:181
  234.2 3.8 fusion.176
  238.0 11.0 %multiply_reduce_fusion.3 = (f32[8,512]{1,0:T(8,128)S(1)}, f32[8,512,1024]{2,1,0:T(8,128)}) fusion(f32[8,512,1024]{2,1,0:T(8,128)S(1)} %fusion.176, f32[8,512]{1,0:T(8,128)S(1)} %dynamic-slice_bitcast_fusion.2, bf16[1024,8,64]{0,2,1:T(8,128)(2,1)} %copy-done.2, bf16[2,512,8,64]{1,3,2,0:T(8,128)(2,1)} %get-tuple-element.602, s32[]{:T(128)} %get-tuple-element.584, ...), kind=kOutput, calls=%fused_computation.22.clone.1 | convolution fusion | flops 557838336 | bytes 35684864 | tf_op jit(solution)/shard_map/while/body/eval_jaxpr/while/body/eval_jaxpr/qhd,khd->hqk/dot_general | solution.py:98
  249.0 9.3 %multiply_convert_fusion.5 = bf16[8,512,1024]{2,1,0:T(8,128)(2,1)} fusion(f32[8,512,1024]{2,1,0:T(8,128)} %get-tuple-element.538, f32[8,512,1024]{2,1,0:T(8,128)S(1)} %fusion.176, f32[8,512]{1,0:T(8,128)S(1)} %get-tuple-element.539), kind=kLoop, calls=%fused_computation.21.clone.1 | loop fusion | flops 12582912 | bytes 41959424 | tf_op jit(solution)/shard_map/while/body/eval_jaxpr/while/body/eval_jaxpr/convert_element_type | solution.py:160
  258.3 6.3 fusion.178
  266.7 19.7 %dynamic_update_slice.34 = f32[2,512,8,64]{1,0,3,2:T(2,128)} dynamic-update-slice(f32[2,512,8,64]{1,0,3,2:T(2,128)} %get-tuple-element.587, f32[1,512,8,64]{1,0,3,2:T(1,128)} %copy.92, s32[]{:T(128)} %get-tuple-element.584, s32[]{:T(128)} %constant.120.clone.1..sunk, s32[]{:T(128)} %constant.120.clone.1..sunk, s32[]{:T(128)} %constant.120.clone.1..sunk) | dynamic-update-slice | bytes 2097156 | tf_op jit(solution)/shard_map/while/body/eval_jaxpr/while/body/jit(dynamic_update_index_in_dim)/dynamic_update_slice | solution.py:128
  286.3 5.4 bitcast_add_fusion.4
  293.1 8.8 %bitcast_add_fusion.5 = f32[1024,8,64]{0,2,1:T(8,128)} fusion(f32[1024,8,64]{0,2,1:T(8,128)} %get-tuple-element.586, f32[8,512,1024]{2,1,0:T(8,128)} %get-tuple-element.538, pred[]{:T(512)S(6)} %compare.11, bf16[2,512,8,64]{1,3,2,0:T(8,128)(2,1)S(1)} %copy-done.15, s32[]{:T(128)} %get-tuple-element.584), kind=kOutput, calls=%fused_computation.26.clone.1 | convolution fusion | flops 542113792 | bytes 21495812 | tf_op jit(solution)/shard_map/while/body/eval_jaxpr/while/body/eval_jaxpr/hqk,qhd->khd/dot_general | solution.py:172
  303.2 3.8 fusion.176
  307.0 11.0 %multiply_reduce_fusion.3 = (f32[8,512]{1,0:T(8,128)S(1)}, f32[8,512,1024]{2,1,0:T(8,128)}) fusion(f32[8,512,1024]{2,1,0:T(8,128)S(1)} %fusion.176, f32[8,512]{1,0:T(8,128)S(1)} %dynamic-slice_bitcast_fusion.2, bf16[1024,8,64]{0,2,1:T(8,128)(2,1)} %copy-done.2, bf16[2,512,8,64]{1,3,2,0:T(8,128)(2,1)} %get-tuple-element.602, s32[]{:T(128)} %get-tuple-element.584, ...), kind=kOutput, calls=%fused_computation.22.clone.1 | convolution fusion | flops 557838336 | bytes 35684864 | tf_op jit(solution)/shard_map/while/body/eval_jaxpr/while/body/eval_jaxpr/qhd,khd->hqk/dot_general | solution.py:98
  318.0 9.3 %multiply_convert_fusion.5 = bf16[8,512,1024]{2,1,0:T(8,128)(2,1)} fusion(f32[8,512,1024]{2,1,0:T(8,128)} %get-tuple-element.538, f32[8,512,1024]{2,1,0:T(8,128)S(1)} %fusion.176, f32[8,512]{1,0:T(8,128)S(1)} %get-tuple-element.539), kind=kLoop, calls=%fused_computation.21.clone.1 | loop fusion | flops 12582912 | bytes 41959424 | tf_op jit(solution)/shard_map/while/body/eval_jaxpr/while/body/eval_jaxpr/convert_element_type | solution.py:160
  327.3 6.3 fusion.178
  335.7 19.7 %dynamic_update_slice.34 = f32[2,512,8,64]{1,0,3,2:T(2,128)} dynamic-update-slice(f32[2,512,8,64]{1,0,3,2:T(2,128)} %get-tuple-element.587, f32[1,512,8,64]{1,0,3,2:T(1,128)} %copy.92, s32[]{:T(128)} %get-tuple-element.584, s32[]{:T(128)} %constant.120.clone.1..sunk, s32[]{:T(128)} %constant.120.clone.1..sunk, s32[]{:T(128)} %constant.120.clone.1..sunk) | dynamic-update-slice | bytes 2097156 | tf_op jit(solution)/shard_map/while/body/eval_jaxpr/while/body/jit(dynamic_update_index_in_dim)/dynamic_update_slice | solution.py:128
  355.3 5.4 bitcast_add_fusion.4
  362.1 9.4 %bitcast_add_fusion.5 = f32[1024,8,64]{0,2,1:T(8,128)} fusion(f32[1024,8,64]{0,2,1:T(8,128)} %get-tuple-element.586, f32[8,512,1024]{2,1,0:T(8,128)} %get-tuple-element.538, pred[]{:T(512)S(6)} %compare.11, bf16[2,512,8,64]{1,3,2,0:T(8,128)(2,1)S(1)} %copy-done.15, s32[]{:T(128)} %get-tuple-element.584), kind=kOutput, calls=%fused_computation.26.clone.1 | convolution fusion | flops 542113792 | bytes 21495812 | tf_op jit(solution)/shard_map/while/body/eval_jaxpr/while/body/eval_jaxpr/hqk,qhd->khd/dot_general | solution.py:172
  371.5 4.3 broadcast_in_dim.154
  385.0 7.7 bitcast_convert_fusion
  393.0 10.3 %convolution_convert_fusion.1 = bf16[1024,2048]{1,0:T(8,128)(2,1)} fusion(bf16[1024,2048]{1,0:T(8,128)(2,1)} %copy-done.83, f32[1024]{0:T(1024)S(1)} %bitcast.315, f32[1024]{0:T(1024)S(1)} %bitcast.297, f32[1024]{0:T(1024)S(1)} %copy-done.62, f32[1024]{0:T(1024)S(1)} %copy-done.51, bf16[1,1024,1024]{2,1,0:T(8,128)(2,1)S(1)} %copy-done.7, ...), kind=kOutput, calls=%fused_computation.132 | convolution fusion | flops 4309647360 | bytes 12615680 | tf_op jit(solution)/shard_map/dot_general | solution.py:85
  405.7 5.6 convolution_convert_fusion.2
  421.6 81.8 %all-reduce.8 = (bf16[4,1024]{1,0:T(4,128)(2,1)S(1)}, bf16[4,1024]{1,0:T(4,128)(2,1)S(1)}) all-reduce(bf16[4,1024]{1,0:T(4,128)(2,1)S(1)} %add_convert_fusion.9, bf16[4,1024]{1,0:T(4,128)(2,1)S(1)} %add_convert_fusion.8), channel_id=1, replica_groups=mesh['dp'=16,'mp'=2] {'dp'}, use_global_device_ids=true, to_apply=%region_34.35 | all-reduce | flops 8192 | bytes 32768 | tf_op jit(solution)/shard_map/psum | solution.py:289
  504.7 4.7 fusion.90
  509.3 271.4 %all-reduce.24.cloned.1.call-done = (bf16[1024,3,512]{2,0,1:T(8,128)(2,1)}, bf16[512,1024]{1,0:T(8,128)(2,1)}, bf16[1024,2048]{1,0:T(8,128)(2,1)}, bf16[2048,1024]{1,0:T(8,128)(2,1)}) async-done(((bf16[1024,3,512]{2,0,1:T(8,128)(2,1)}, bf16[512,1024]{1,0:T(8,128)(2,1)}, bf16[1024,2048]{1,0:T(8,128)(2,1)}, bf16[2048,1024]{1,0:T(8,128)(2,1)}), (bf16[1024,3,512]{2,0,1:T(8,128)(2,1)}, ...) | async-done | bytes 12582928 | tf_op jit(solution)/shard_map/psum | solution.py:285
  780.8 6.8 convert_element_type.193
  787.6 4.4 convert_element_type.195
  792.0 3.6 convert_element_type.189
  (275 shorter events, 89.8 us)
Async XLA Ops:
  7.2 67.1 %copy-start = (bf16[512,1024]{1,0:T(8,128)(2,1)S(1)}, bf16[512,1024]{1,0:T(8,128)(2,1)}, u32[]{:S(2)}) copy-start(bf16[512,1024]{1,0:T(8,128)(2,1)} %param.20) | copy-start | bytes 3145732
  7.2 93.9 %all-reduce.16.cloned.1.call-start = ((), (), s32[]{:S(2)}) async-start(), calls=%async_computation | async-start | bytes 4194304 | tf_op jit(solution)/shard_map/psum | solution.py:219
  9.3 8.9 %copy-start.48 = (f32[1024]{0:T(1024)}, f32[1024]{0:T(1024)S(1)}, u32[]{:S(2)}) copy-start(f32[1024]{0:T(1024)S(1)} %broadcast_multiply_fusion.3) | copy-start | bytes 12292
  9.3 8.9 %copy-start.4 = (bf16[1,1024,1024]{2,1,0:T(8,128)(2,1)S(1)}, bf16[1,1024,1024]{2,1,0:T(8,128)(2,1)}, u32[]{:S(2)}) copy-start(bf16[1,1024,1024]{2,1,0:T(8,128)(2,1)} %param.14) | copy-start | bytes 6291460
  12.3 11.4 %copy-start.59 = (f32[1024]{0:T(1024)}, f32[1024]{0:T(1024)S(1)}, u32[]{:S(2)}) copy-start(f32[1024]{0:T(1024)S(1)} %fusion.108) | copy-start | bytes 12292
  12.9 10.8 %copy-start.52 = (f32[1,1024]{1,0:T(1,128)}, f32[1,1024]{1,0:T(1,128)S(1)}, u32[]{:S(2)}) copy-start(f32[1,1024]{1,0:T(1,128)S(1)} %get-tuple-element.382) | copy-start | bytes 12292
  13.6 10.2 %copy-start.73 = (f32[1,1024]{1,0:T(1,128)}, f32[1,1024]{1,0:T(1,128)S(1)}, u32[]{:S(2)}) copy-start(f32[1,1024]{1,0:T(1,128)S(1)} %get-tuple-element.386) | copy-start | bytes 12292
  76.9 28.6 %copy-start.44 = (f32[1,1024]{1,0:T(1,128)S(1)}, f32[1,1024]{1,0:T(1,128)}, u32[]{:S(2)}) copy-start(f32[1,1024]{1,0:T(1,128)} %get-tuple-element.381) | copy-start | bytes 12292
  76.9 28.6 %copy-start.46 = (f32[1,1024]{1,0:T(1,128)S(1)}, f32[1,1024]{1,0:T(1,128)}, u32[]{:S(2)}) copy-start(f32[1,1024]{1,0:T(1,128)} %get-tuple-element.385) | copy-start | bytes 12292
  76.9 70.2 %all-reduce.18.cloned.1.call-start = ((), (), s32[]{:S(2)}) async-start(), calls=%async_computation.1 | async-start | bytes 4194304 | tf_op jit(solution)/shard_map/psum | solution.py:219
  103.2 115.8 %copy-start.39 = (f32[1024]{0:T(1024)}, f32[1024]{0:T(1024)S(1)}, u32[]{:S(2)}) copy-start(f32[1024]{0:T(1024)S(1)} %broadcast_multiply_fusion.2) | copy-start | bytes 12292
  105.5 113.5 %copy-start.42 = (f32[1024]{0:T(1024)}, f32[1024]{0:T(1024)S(1)}, u32[]{:S(2)}) copy-start(f32[1024]{0:T(1024)S(1)} %fusion.109) | copy-start | bytes 12292
  107.0 104.6 %copy-start.50 = (f32[1024]{0:T(1024)}, f32[1024]{0:T(1024)S(1)}, u32[]{:S(2)}) copy-start(f32[1024]{0:T(1024)S(1)} %broadcast_multiply_fusion.1) | copy-start | bytes 12292
  109.2 102.4 %copy-start.61 = (f32[1024]{0:T(1024)}, f32[1024]{0:T(1024)S(1)}, u32[]{:S(2)}) copy-start(f32[1024]{0:T(1024)S(1)} %fusion.110) | copy-start | bytes 12292
  109.3 8.9 %copy-start.78 = (bf16[2048,1024]{1,0:T(8,128)(2,1)S(1)}, bf16[2048,1024]{1,0:T(8,128)(2,1)}, u32[]{:S(2)}) copy-start(bf16[2048,1024]{1,0:T(8,128)(2,1)} %param.22) | copy-start | bytes 12582916
  124.5 24.8 %copy-start.56 = (f32[1,1024]{1,0:T(1,128)S(1)}, f32[1,1024]{1,0:T(1,128)}, u32[]{:S(2)}) copy-start(f32[1,1024]{1,0:T(1,128)} %get-tuple-element.380) | copy-start | bytes 12292
  124.5 76.5 %all-reduce.20.cloned.1.call-start = ((), (), s32[]{:S(2)}) async-start(), calls=%async_computation.2 | async-start | bytes 4194304 | tf_op jit(solution)/shard_map/psum | solution.py:222
  149.3 7.3 copy-start.79
  156.6 16.1 %copy-start.81 = (bf16[1024,2048]{1,0:T(8,128)(2,1)S(1)}, bf16[1024,2048]{1,0:T(8,128)(2,1)}, u32[]{:S(2)}) copy-start(bf16[1024,2048]{1,0:T(8,128)(2,1)} %param.21) | copy-start | bytes 12582916
  178.4 237.0 %all-reduce.22.cloned.1.call-start = ((), (), s32[]{:S(2)}) async-start(), calls=%async_computation.3 | async-start | bytes 4194304 | tf_op jit(solution)/shard_map/psum | solution.py:222
  264.6 21.7 %copy-start.8 = (f32[1024,8,64]{0,2,1:T(8,128)S(1)}, f32[1024,8,64]{0,2,1:T(8,128)}, u32[]{:S(2)}) copy-start(f32[1024,8,64]{0,2,1:T(8,128)} %get-tuple-element.585) | copy-start | bytes 6291460 | tf_op jit(solution)/shard_map/while/body/eval_jaxpr/while
  286.3 6.7 copy-start.15
  293.1 8.8 %copy-start.3 = (bf16[1024,8,64]{0,2,1:T(8,128)(2,1)S(1)}, bf16[1024,8,64]{0,2,1:T(8,128)(2,1)}, u32[]{:S(2)}) copy-start(bf16[1024,8,64]{0,2,1:T(8,128)(2,1)} %copy-done.2) | copy-start | bytes 3145732 | tf_op jit(solution)/shard_map/while/body/eval_jaxpr/while
  293.1 8.8 %copy-start.14 = (bf16[1024,8,64]{0,2,1:T(8,128)(2,1)S(1)}, bf16[1024,8,64]{0,2,1:T(8,128)(2,1)}, u32[]{:S(2)}) copy-start(bf16[1024,8,64]{0,2,1:T(8,128)(2,1)} %copy-done.13) | copy-start | bytes 3145732 | tf_op jit(solution)/shard_map/while/body/eval_jaxpr/while
  333.6 21.7 %copy-start.8 = (f32[1024,8,64]{0,2,1:T(8,128)S(1)}, f32[1024,8,64]{0,2,1:T(8,128)}, u32[]{:S(2)}) copy-start(f32[1024,8,64]{0,2,1:T(8,128)} %get-tuple-element.585) | copy-start | bytes 6291460 | tf_op jit(solution)/shard_map/while/body/eval_jaxpr/while
  355.3 6.7 copy-start.15
  362.1 9.4 %copy-start.3 = (bf16[1024,8,64]{0,2,1:T(8,128)(2,1)S(1)}, bf16[1024,8,64]{0,2,1:T(8,128)(2,1)}, u32[]{:S(2)}) copy-start(bf16[1024,8,64]{0,2,1:T(8,128)(2,1)} %copy-done.2) | copy-start | bytes 3145732 | tf_op jit(solution)/shard_map/while/body/eval_jaxpr/while
  362.1 9.4 %copy-start.14 = (bf16[1024,8,64]{0,2,1:T(8,128)(2,1)S(1)}, bf16[1024,8,64]{0,2,1:T(8,128)(2,1)}, u32[]{:S(2)}) copy-start(bf16[1024,8,64]{0,2,1:T(8,128)(2,1)} %copy-done.13) | copy-start | bytes 3145732 | tf_op jit(solution)/shard_map/while/body/eval_jaxpr/while
  385.0 7.9 copy-start.7
  385.0 7.9 copy-start.40
  385.0 7.9 copy-start.43
  385.0 7.9 copy-start.45
  385.0 7.9 copy-start.47
  385.0 7.9 copy-start.51
  385.0 7.9 copy-start.55
  385.0 7.9 copy-start.62
  385.0 7.9 copy-start.76
  392.8 10.4 %copy-start.35 = (bf16[64,8,2,512]{3,1,2,0:T(8,128)(2,1)S(1)}, bf16[64,8,2,512]{3,1,2,0:T(8,128)(2,1)}, u32[]{:S(2)}) copy-start(bf16[64,8,2,512]{3,1,2,0:T(8,128)(2,1)} %copy-done.34) | copy-start | bytes 3145732
  392.8 10.4 %copy-start.72 = (f32[1024]{0:T(1024)S(1)}, f32[1024]{0:T(1024)}, u32[]{:S(2)}) copy-start(f32[1024]{0:T(1024)} %copy-done.71) | copy-start | bytes 12292
  392.8 388.0 %all-reduce.24.cloned.1.call-start = ((), (), s32[]{:S(2)}) async-start(), calls=%async_computation.4 | async-start | bytes 25165824 | tf_op jit(solution)/shard_map/psum | solution.py:285
  393.0 10.3 %copy-start.25 = (f32[1024,1024]{1,0:T(8,128)S(1)}, f32[1024,1024]{1,0:T(8,128)}, u32[]{:S(2)}) copy-start(f32[1024,1024]{1,0:T(8,128)} %copy-done.24) | copy-start | bytes 12582916
  411.3 7.2 copy-start.64
  411.3 7.2 copy-start.69
  411.3 7.2 copy-start.58
  413.5 8.0 copy-start.63
  413.5 8.0 copy-start.67
  413.5 8.0 copy-start.68
  780.8 6.8 copy-start.23
  (49 other events, 161.1 us)
Sparse Core Ops, SparseCore 0:
  77.0 24.0 all-reduce.15
  124.7 22.4 all-reduce.17
  178.5 22.4 all-reduce.19
  392.9 22.4 all-reduce.21
  422.3 358.4 all-reduce.23
where the time goes:
time: 813 us; the launch traced here: 804 us
  waiting for transfers between devices  329 us (40%)
  matrix products  173 us (21%)
  other arithmetic  114 us (14%)
  local copies, waits for them, and re-layouts  90.3 us (11%)
  blocking collectives  81.8 us (10%)
  between operations  15.6 us (2%)
    psum x1, waiting for transfers between devices, body(): lax.psum(qkv_grad.astype(jnp.bfloat16), 'dp').astype(jnp.float32)  271 us
    psum x1, blocking collectives, body(): lax.psum(gain_grad.astype(jnp.bfloat16), 'dp').astype(jnp.float32)  81.8 us
    psum x2, waiting for transfers between devices, branch_sum(): return lax.psum(partial_sum.astype(jnp.bfloat16), 'mp').astype(jnp.float32)  46.7 us
    dynamic_update_slice x4, local copies, waits for them, and re-layouts, one_row(): lax.map(one_block, (query_row.reshape(block_count, block_len, head_count,...  43.4 us
    reduce_sum x8, other arithmetic, normalize(): return centred * lax.rsqrt(spread + EPSILON) * gain_vec + shift_vec  33.3 us
    dot_general x4, matrix products, block_scores(): jnp.einsum('qhd,khd->hqk', query_blk, key_row, preferred_element_type=jnp...  30.2 us
    dot_general x3, matrix products, contract_rows(): lax.dot_general(left_side, right_side, (((0,), (0,)), ((), ())), preferre...  26.3 us
    dot_general x3, matrix products, contract_cols(): lax.dot_general(left_side, right_side, (((1,), (1,)), ((), ())), preferre...  22.1 us
  transfers between devices with their start and end apart: 5, of which 5 were waited for; matrix products, arithmetic and copies ran while one was open for 6% of the time, Pallas kernels for 0%

commit v1 on v0

v1 whole, which is shorter than its diff:
```python
import functools
import math

import jax, jax.numpy as jnp
from jax import lax
from jax.experimental import pallas as pl
from jax.experimental.pallas import tpu as pltpu
from jax.sharding import PartitionSpec as P

HEAD_DIM = 64
DOC_MOST = 384
NEGATIVE = -1e30
BLOCK = 256
AUG = 16


def spans(seq_len):
    block = min(BLOCK, seq_len)
    return [(q, block, max(0, q - DOC_MOST)) for q in range(0, seq_len, block)]


def dot(a, b):
    return lax.dot_general(a, b, (((1,), (0,)), ((), ())), preferred_element_type=jnp.float32)


def spin(u, cosine, sine, sign):
    half = u.shape[0] // 2
    first, second = u[:half].astype(jnp.float32), u[half:].astype(jnp.float32)
    return first * cosine - sign * second * sine, second * cosine + sign * first * sine


def turned(ref, cosine, sine, scale):
    first, second = spin(ref[0], cosine, sine, 1.0)
    return jnp.concatenate([first * scale, second * scale], axis=0).astype(jnp.bfloat16)


def causal(block):
    key = lax.broadcasted_iota(jnp.int32, (block, block), 0)
    query = lax.broadcasted_iota(jnp.int32, (block, block), 1)
    return key <= query


def masked(scores, keep, block):
    last = jnp.where(keep, scores[-block:], NEGATIVE)
    if scores.shape[0] == block:
        return last
    return jnp.concatenate([scores[:-block], last], axis=0)


def setup(q_ref, k_ref, cos_ref, sin_ref, qaug_ref, kaug_ref, qt_scr, kn_scr):
    cosine, sine = cos_ref[...], sin_ref[...]
    seq_len = q_ref.shape[-1]
    pad = jnp.zeros((128 - HEAD_DIM - AUG, seq_len), jnp.bfloat16)
    q_low = turned(q_ref, cosine, sine, HEAD_DIM ** -0.5)
    k_low = turned(k_ref, cosine, sine, 1.0)
    qt_scr[...] = jnp.concatenate([q_low, qaug_ref[...], pad], axis=0)
    k_all = jnp.concatenate([k_low, kaug_ref[...], pad], axis=0)
    kn_scr[...] = k_all.T
    return q_low, k_low


def fwd_kernel(q_ref, k_ref, v_ref, cos_ref, sin_ref, qaug_ref, kaug_ref, o_ref, lse_ref, qt_scr, kn_scr):
    seq_len = q_ref.shape[-1]
    setup(q_ref, k_ref, cos_ref, sin_ref, qaug_ref, kaug_ref, qt_scr, kn_scr)
    for start, block, low in spans(seq_len):
        high = start + block
        scores = dot(kn_scr[low:high, :], qt_scr[:, start:high])
        scores = masked(scores, causal(block), block)
        top = jnp.max(scores, axis=0, keepdims=True)
        expo = jnp.exp(scores - top)
        total = jnp.sum(expo, axis=0, keepdims=True)
        out = dot(v_ref[0, :, low:high], expo.astype(jnp.bfloat16)) / total
        o_ref[:, start:high] = out.astype(jnp.bfloat16)
        lse_ref[0, :, start:high] = top + jnp.log(total)


def bwd_kernel(q_ref, k_ref, v_ref, cos_ref, sin_ref, qaug_ref, kaug_ref, o_ref, lse_ref, do_ref,
               dm_ref, qt_scr, kn_scr, qn_scr, kt_scr, vn_scr, don_scr, dk_scr, dv_scr):
    seq_len = q_ref.shape[-1]
    cosine, sine = cos_ref[...], sin_ref[...]
    q_low, k_low = setup(q_ref, k_ref, cos_ref, sin_ref, qaug_ref, kaug_ref, qt_scr, kn_scr)
    kt_scr[...] = k_low
    both = jnp.concatenate([q_low, do_ref[...]], axis=0).T
    qn_scr[...] = both[:, :HEAD_DIM]
    don_scr[...] = both[:, HEAD_DIM:]
    vn_scr[...] = v_ref[0].T
    dk_scr[...] = jnp.zeros_like(dk_scr)
    dv_scr[...] = jnp.zeros_like(dv_scr)
    inner = jnp.sum(o_ref[...].astype(jnp.float32) * do_ref[...].astype(jnp.float32), axis=0, keepdims=True)
    for start, block, low in spans(seq_len):
        high = start + block
        scores = dot(kn_scr[low:high, :], qt_scr[:, start:high])
        scores = masked(scores, causal(block), block)
        soft = jnp.exp(scores - lse_ref[0, :, start:high])
        d_soft = dot(vn_scr[low:high, :], do_ref[:, start:high])
        d_scores = (soft * (d_soft - inner[:, start:high])).astype(jnp.bfloat16)
        d_q = dot(kt_scr[:, low:high], d_scores) * HEAD_DIM ** -0.5
        first, second = spin(d_q, cosine[:, start:high], sine[:, start:high], -1.0)
        half = HEAD_DIM // 2
        dm_ref[0, :half, start:high] = first.astype(jnp.bfloat16)
        dm_ref[0, half:, start:high] = second.astype(jnp.bfloat16)
        dk_scr[low:high, :] += dot(d_scores, qn_scr[start:high, :])
        dv_scr[low:high, :] += dot(soft.astype(jnp.bfloat16), don_scr[start:high, :])
    first, second = spin(dk_scr[...].T, cosine, sine, -1.0)
    dm_ref[1] = jnp.concatenate([first, second], axis=0).astype(jnp.bfloat16)
    dm_ref[2] = dv_scr[...].T.astype(jnp.bfloat16)


def common_specs(seq_len):
    part = lambda c: pl.BlockSpec((1, HEAD_DIM, seq_len), lambda h: (c, h, 0))
    whole = lambda rows: pl.BlockSpec((rows, seq_len), lambda h: (0, 0))
    half = HEAD_DIM // 2
    return [part(0), part(1), part(2), whole(half), whole(half), whole(AUG), whole(AUG)]


def attention_forward(mixed, cosine, sine, qaug, kaug):
    _, inner, seq_len = mixed.shape
    heads = inner // HEAD_DIM
    head_spec = pl.BlockSpec((HEAD_DIM, seq_len), lambda h: (h, 0))
    return pl.pallas_call(
        fwd_kernel,
        grid=(heads,),
        in_specs=common_specs(seq_len),
        out_specs=[head_spec, pl.BlockSpec((1, 1, seq_len), lambda h: (h, 0, 0))],
        out_shape=[jax.ShapeDtypeStruct((inner, seq_len), jnp.bfloat16),
                   jax.ShapeDtypeStruct((heads, 1, seq_len), jnp.float32)],
        scratch_shapes=[pltpu.VMEM((128, seq_len), jnp.bfloat16), pltpu.VMEM((seq_len, 128), jnp.bfloat16)],
        name="attention_forward",
        cost_estimate=pl.CostEstimate(flops=heads * 2 * 2 * seq_len * 512 * 128, bytes_accessed=inner * seq_len * 8, transcendentals=heads * seq_len * 512),
    )(mixed, mixed, mixed, cosine, sine, qaug, kaug)


def attention_backward(mixed, cosine, sine, qaug, kaug, att, lse, d_att):
    _, inner, seq_len = mixed.shape
    heads = inner // HEAD_DIM
    head_spec = pl.BlockSpec((HEAD_DIM, seq_len), lambda h: (h, 0))
    return pl.pallas_call(
        bwd_kernel,
        grid=(heads,),
        in_specs=common_specs(seq_len) + [head_spec, pl.BlockSpec((1, 1, seq_len), lambda h: (h, 0, 0)), head_spec],
        out_specs=pl.BlockSpec((3, HEAD_DIM, seq_len), lambda h: (0, h, 0)),
        out_shape=jax.ShapeDtypeStruct(mixed.shape, jnp.bfloat16),
        scratch_shapes=[pltpu.VMEM((128, seq_len), jnp.bfloat16), pltpu.VMEM((seq_len, 128), jnp.bfloat16),
                        pltpu.VMEM((seq_len, HEAD_DIM), jnp.bfloat16), pltpu.VMEM((HEAD_DIM, seq_len), jnp.bfloat16),
                        pltpu.VMEM((seq_len, HEAD_DIM), jnp.bfloat16), pltpu.VMEM((seq_len, HEAD_DIM), jnp.bfloat16),
                        pltpu.VMEM((seq_len, HEAD_DIM), jnp.float32), pltpu.VMEM((seq_len, HEAD_DIM), jnp.float32)],
        name="attention_backward",
        cost_estimate=pl.CostEstimate(flops=heads * 5 * 2 * seq_len * 512 * 128, bytes_accessed=inner * seq_len * 16, transcendentals=heads * seq_len * 512),
    )(mixed, mixed, mixed, cosine, sine, qaug, kaug, att, lse, d_att)


EPSILON = 1e-05
GELU_SCALE = 0.7978845608028654
SEGMENTS = 9
GRIDS = {16: (4, 2, 2)}


def normalize(values_in, gain_vec, shift_vec):
    mean_vals = jnp.mean(values_in, axis=-1, keepdims=True)
    centred = values_in - mean_vals
    spread = jnp.mean(centred * centred, axis=-1, keepdims=True)
    return centred * lax.rsqrt(spread + EPSILON) * gain_vec + shift_vec


def gelu_tanh(hidden):
    return (
        0.5 * hidden * (1.0 + jnp.tanh(GELU_SCALE * (hidden + 0.044715 * hidden * hidden * hidden)))
    )


def row_layout(lengths, pad_count, seq_len, half_dim):
    position = jnp.arange(seq_len, dtype=jnp.int32)
    doc_ends = jnp.cumsum(lengths)
    passed = position[None, :] >= doc_ends[:, None]
    segment = jnp.sum(passed.astype(jnp.int32), axis=0)
    start_at = jnp.sum(jnp.where(passed, lengths[:, None], 0), axis=0)
    pad_start = seq_len - pad_count
    is_live = position < pad_start
    segment = jnp.where(is_live, segment, lengths.shape[0])
    start_at = jnp.where(is_live, start_at, pad_start)
    offset = (position - start_at).astype(jnp.float32)
    frequencies = jnp.exp(-math.log(10000.0) * jnp.arange(half_dim, dtype=jnp.float32) / half_dim)
    angles = frequencies[:, None] * offset[None, :]
    kind = jnp.arange(AUG, dtype=jnp.int32)[:, None]
    same = kind == segment[None, :]
    query_mark = same.astype(jnp.bfloat16)
    key_mark = jnp.where(same | (kind >= SEGMENTS), 0.0, NEGATIVE).astype(jnp.bfloat16)
    return (jnp.cos(angles), jnp.sin(angles), query_mark, key_mark)


def first_norm(rows_in, gain_all, shift_all):
    return normalize(rows_in, gain_all[0], shift_all[0])


def middle(att_rows, resid_rows, gain_all, shift_all):
    middle_rows = resid_rows + normalize(att_rows, gain_all[1], shift_all[1])
    return (middle_rows, normalize(middle_rows, gain_all[2], shift_all[2]))


def finish(mlp_rows, middle_rows, gain_all, shift_all):
    return middle_rows + normalize(mlp_rows, gain_all[3], shift_all[3])


def contract(left_side, right_side, left_dim, right_dim):
    return lax.dot_general(
        left_side, right_side, (((left_dim,), (right_dim,)), ((), ())), preferred_element_type=jnp.float32
    )


def low_add(one, other):
    return (one.astype(jnp.float32) + other.astype(jnp.float32)).astype(jnp.bfloat16)


class Grid:
    def __init__(self, sizes):
        self.sizes = sizes
        count = math.prod(sizes)
        x_size, y_size = sizes[2], sizes[1]
        plane = x_size * y_size
        self.x_pairs = [(i, i ^ 1) for i in range(count)]
        self.y_pairs = [(i, i ^ x_size) for i in range(count)]
        layer = lambda i: i // plane
        self.inward = [(i, i + plane) for i in range(count) if layer(i) == 0]
        self.inward += [(i, i - plane) for i in range(count) if layer(i) == 3]
        self.across = [(i, i + plane) for i in range(count) if layer(i) == 1]
        self.across += [(i, i - plane) for i in range(count) if layer(i) == 2]
        self.outward = [(b, a) for a, b in self.inward]
        index = lax.axis_index("dp")
        self.x_bit = index % x_size
        self.y_bit = (index // x_size) % y_size
        place = index // plane
        self.at_end = (place == 0) | (place == 3)

    def swap(self, values, pairs):
        return lax.ppermute(values, "dp", pairs)

    def line(self, values):
        values = low_add(values, self.swap(values, self.inward))
        values = low_add(values, self.swap(values, self.across))
        return jnp.where(self.at_end, self.swap(values, self.outward), values)

    def small(self, values):
        values = low_add(values, self.swap(values, self.x_pairs))
        values = low_add(values, self.swap(values, self.y_pairs))
        return self.line(values)

    def colour(self, values, x_first):
        order = [(self.x_pairs, self.x_bit), (self.y_pairs, self.y_bit)]
        if not x_first:
            order = order[::-1]
        for pairs, bit in order:
            half = values.shape[0] // 2
            send = lax.dynamic_slice_in_dim(values, (1 - bit) * half, half, 0)
            keep = lax.dynamic_slice_in_dim(values, bit * half, half, 0)
            values = low_add(keep, self.swap(send, pairs))
        values = self.line(values)
        pairs, bit = order[1]
        other = self.swap(values, pairs)
        quarter = values.shape[0]
        joined = jnp.concatenate([jnp.where(bit == 0, values, other), jnp.where(bit == 0, other, values)], axis=0)
        pairs, bit = order[0]
        return joined, self.swap(joined, pairs), bit

    def large(self, values, parts):
        half = values.shape[0] // 2
        pieces = []
        bits = []
        for colour in range(2):
            own, other, bit = self.colour(values[colour * half:(colour + 1) * half], colour == 0)
            pieces += [own, other]
            bits.append(bit)
        return assemble(jnp.stack(bits).astype(jnp.int32), pieces, parts)


def assemble_kernel(parts, bits_ref, own_a, other_a, own_b, other_b, out_ref):
    for colour, own, other in ((0, own_a, other_a), (1, own_b, other_b)):
        bit = bits_ref[colour]
        for slot, piece in ((2 * colour + bit, own), (2 * colour + 1 - bit, other)):
            if parts == 1:
                out_ref[slot] = piece[...].astype(jnp.float32)
            else:
                width = piece.shape[1] // parts
                for part in range(parts):
                    out_ref[slot, :, part, :] = piece[:, part * width:(part + 1) * width].astype(jnp.float32)


def assemble(bits, pieces, parts):
    rows, width = pieces[0].shape
    block = 32
    in_spec = pl.BlockSpec((block, width), lambda i, b: (i, 0))
    if parts == 1:
        shape, out_block, out_map = (4, rows, width), (4, block, width), lambda i, b: (0, i, 0)
    else:
        shape, out_block, out_map = (4, rows, parts, width // parts), (4, block, parts, width // parts), lambda i, b: (0, i, 0, 0)
    out = pl.pallas_call(
        functools.partial(assemble_kernel, parts),
        grid_spec=pltpu.PrefetchScalarGridSpec(
            num_scalar_prefetch=1,
            grid=(rows // block,),
            in_specs=[in_spec] * 4,
            out_specs=pl.BlockSpec(out_block, out_map),
        ),
        out_shape=jax.ShapeDtypeStruct(shape, jnp.float32),
        name="assemble",
        cost_estimate=pl.CostEstimate(flops=0, bytes_accessed=4 * rows * width * 6, transcendentals=0),
    )(bits, *pieces)
    return out.reshape((4 * rows,) + shape[2:])


def make_body(sizes):
    mp_size = sizes["mp"]
    grid_sizes = GRIDS.get(sizes["dp"])

    def pair_sum(partial_sum):
        low_part = partial_sum.astype(jnp.bfloat16)
        if mp_size == 2:
            other = lax.ppermute(low_part, "mp", [(0, 1), (1, 0)])
            return low_part.astype(jnp.float32) + other.astype(jnp.float32)
        return lax.psum(low_part, "mp").astype(jnp.float32)

    def plain_sum(values):
        return lax.psum(values.astype(jnp.bfloat16), "dp").astype(jnp.float32)

    def body(tokens, doc_lengths, pad_counts, norm_gain, norm_bias, qkv_weight, out_weight, up_weight, down_weight, cotangent):
        row_count, seq_len, width_all = tokens.shape
        token_count = row_count * seq_len
        inner_here = qkv_weight.shape[2]
        layouts = [row_layout(doc_lengths[r], pad_counts[r], seq_len, HEAD_DIM // 2) for r in range(row_count)]

        residual = tokens.reshape(token_count, width_all).astype(jnp.float32)
        normed_low = first_norm(residual, norm_gain, norm_bias).astype(jnp.bfloat16)
        mixed = contract(qkv_weight, normed_low, 0, 1).astype(jnp.bfloat16)
        spans_of = [slice(r * seq_len, (r + 1) * seq_len) for r in range(row_count)]
        forward = [attention_forward(mixed[:, :, s], *layout) for s, layout in zip(spans_of, layouts)]
        att_turned = jnp.concatenate([f[0] for f in forward], axis=1)
        att_sum = pair_sum(contract(att_turned, out_weight, 0, 0))
        middle_rows, mlp_norm = middle(att_sum, residual, norm_gain, norm_bias)
        mlp_low = mlp_norm.astype(jnp.bfloat16)
        hidden = contract(mlp_low, up_weight, 1, 0)
        act_low = gelu_tanh(hidden).astype(jnp.bfloat16)
        mlp_sum = pair_sum(contract(act_low, down_weight, 1, 0))
        output_rows = finish(mlp_sum, middle_rows, norm_gain, norm_bias)
        out_tokens = output_rows.astype(jnp.bfloat16).reshape(row_count, seq_len, width_all)
        grad_out = cotangent.reshape(token_count, width_all).astype(jnp.float32)
        _, finish_back = jax.vjp(finish, mlp_sum, middle_rows, norm_gain, norm_bias)
        grad_mlp_sum, grad_middle, gain_last, bias_last = finish_back(grad_out)
        grad_mlp_low = grad_mlp_sum.astype(jnp.bfloat16)
        down_grad = contract(act_low, grad_mlp_low, 0, 0).astype(jnp.bfloat16)
        down_sum = plain_sum(down_grad)
        grad_act = contract(grad_mlp_low, down_weight, 1, 1)
        _, gelu_back = jax.vjp(gelu_tanh, hidden)
        grad_hidden = gelu_back(grad_act)[0].astype(jnp.bfloat16)
        up_grad = contract(mlp_low, grad_hidden, 0, 0).astype(jnp.bfloat16)
        grad_mlp_norm = pair_sum(contract(grad_hidden, up_weight, 1, 1))
        _, middle_back = jax.vjp(middle, att_sum, residual, norm_gain, norm_bias)
        grad_att_sum, grad_resid_mid, gain_mid, bias_mid = middle_back((grad_middle, grad_mlp_norm))
        grad_att_low = grad_att_sum.astype(jnp.bfloat16)
        out_grad = contract(att_turned, grad_att_low, 1, 0).astype(jnp.bfloat16)
        grad_attended = contract(out_weight, grad_att_low, 1, 1).astype(jnp.bfloat16)
        grad_mixed = [
            attention_backward(mixed[:, :, s], *layout, f[0], f[1], grad_attended[:, s])
            for s, layout, f in zip(spans_of, layouts, forward)
        ]
        grad_mixed = jnp.concatenate(grad_mixed, axis=2)
        flat_mixed = grad_mixed.reshape(3 * inner_here, token_count)
        qkv_grad = contract(normed_low, flat_mixed, 0, 1).astype(jnp.bfloat16)
        grad_normed = pair_sum(
            lax.dot_general(
                grad_mixed, qkv_weight, (((0, 1), (1, 2)), ((), ())), preferred_element_type=jnp.float32
            )
        )
        _, first_back = jax.vjp(first_norm, residual, norm_gain, norm_bias)
        grad_resid_first, gain_first, bias_first = first_back(grad_normed)
        input_grad = (
            (grad_resid_mid + grad_resid_first)
            .astype(jnp.bfloat16)
            .reshape(row_count, seq_len, width_all)
        )
        small = jnp.concatenate([gain_last + gain_mid + gain_first, bias_last + bias_mid + bias_first], axis=0)
        if grid_sizes is None:
            qkv_sum = plain_sum(qkv_grad).reshape(width_all, 3, inner_here)
            out_sum, up_sum, small_sum = plain_sum(out_grad), plain_sum(up_grad), plain_sum(small)
        else:
            grid = Grid(grid_sizes)
            up_sum = grid.large(up_grad, 1)
            out_sum = grid.small(out_grad).astype(jnp.float32)
            qkv_sum = grid.large(qkv_grad, 3)
            small_sum = grid.small(small.astype(jnp.bfloat16)).astype(jnp.float32)
        norms = norm_gain.shape[0]
        return (out_tokens, input_grad, small_sum[:norms], small_sum[norms:], qkv_sum, out_sum, up_sum, down_sum)

    return body


def solution(mesh):
    in_specs = (
        P("dp", None, None),
        P("dp", None),
        P("dp"),
        P(),
        P(),
        P(None, None, "mp"),
        P("mp", None),
        P(None, "mp"),
        P("mp", None),
        P("dp", None, None),
    )
    out_specs = (
        P("dp", None, None),
        P("dp", None, None),
        P(),
        P(),
        P(None, None, "mp"),
        P("mp", None),
        P(None, "mp"),
        P("mp", None),
    )
    return jax.shard_map(make_body(dict(mesh.shape)), mesh=mesh, in_specs=in_specs, out_specs=out_specs, check_vma=False)
```

time: 813 us -> 511 us (0.63)
  the two profiles are of different devices: /device:TPU:0 before, /device:TPU:8 now
where the time goes in v1:
time: 511 us; the launch traced here: 502 us
  waiting for transfers between devices  179 us (35%)
  other arithmetic  86.3 us (17%)
  matrix products  71.2 us (14%)
  starting transfers between devices  63.6 us (12%)
  Pallas kernels  51.4 us (10%)
  local copies, waits for them, and re-layouts  33.8 us (7%)
  between operations  16.3 us (3%)
    ppermute x38, waiting for transfers between devices, swap(): return lax.ppermute(values, 'dp', pairs)  175 us
    dot_general x11, matrix products, contract(): lax.dot_general(left_side, right_side, (((left_dim,), (right_dim,)), ((),...  65.6 us
    ppermute x38, starting transfers between devices, swap(): return lax.ppermute(values, 'dp', pairs)  63.3 us
    reduce_sum x8, other arithmetic, normalize(): return centred * lax.rsqrt(spread + EPSILON) * gain_vec + shift_vec  32.1 us
    unnamed x83, local copies, waits for them, and re-layouts  29.4 us
    pallas_call x1, Pallas kernels, attention_backward(): pl.pallas_call(bwd_kernel, grid=(heads,), in_specs=common_specs(seq_len)...  21.1 us
    convert_element_type x24, other arithmetic, low_add(): (one.astype(jnp.float32) + other.astype(jnp.float32)).astype(jnp.bfloat16)  18.8 us
    pallas_call x2, Pallas kernels, assemble(): pl.pallas_call(functools.partial(assemble_kernel, parts), grid_spec=pltpu...  16.5 us
  transfers between devices with their start and end apart: 43, of which 15 were waited for; matrix products, arithmetic and copies ran while one was open for 22% of the time, Pallas kernels for 7%

profile of v1, /device:TPU:8, one launch (start us, length us, event | category | flops | bytes accessed | tf_op | source)
XLA Modules:
  0.0 502.0 jit_solution(17758107835944454565)
XLA Ops:
  12.7 3.9 copy.29
  22.2 5.5 %convert_bitcast_fusion.2.q_ref.k_ref.v_ref = bf16[3,512,1024]{2,1,0:T(8,128)(2,1)} fusion(bf16[1024,3,512]{2,0,1:T(8,128)(2,1)S(1)} %copy-done, bf16[1,1024,1024]{1,2,0:T(8,128)(2,1)S(1)} %copy-done.4, f32[1024]{0:T(1024)S(1)} %bitcast.151, f32[1024]{0:T(1024)S(1)} %bitcast.132, f32[1024]{0:T(1024)S(1)} %fusion.57, f32[1024]{0:T(1024)S(1)} %broadcast_multiply_fusion.3), kind=kOutput, calls=%fused_computation.71 | convolution fusion | flops 3229089792 | bytes 8404992 | tf_op jit(solution)/shard_map/dot_general | solution.py:205
  27.7 13.8 %attention_forward.1 = (bf16[512,1024]{1,0:T(8,128)(2,1)}, f32[8,1,1024]{2,1,0:T(1,128)}) custom-call(bf16[3,512,1024]{2,1,0:T(8,128)(2,1)} %convert_bitcast_fusion.2.q_ref.k_ref.v_ref, bf16[3,512,1024]{2,1,0:T(8,128)(2,1)} %convert_bitcast_fusion.2.q_ref.k_ref.v_ref, bf16[3,512,1024]{2,1,0:T(8,128)(2,1)} %convert_bitcast_fusion.2.q_ref.k_ref.v_ref, ...), custom_call_target="tpu_custom_call" | custom-call | flops 2147483648 | bytes 4194304 | tf_op jit(solution)/shard_map/attention_forward/pallas_call | solution.py:120
  41.6 2.8 convolution_convert_fusion.5
  44.5 4.1 collective-permute-done
  56.3 5.0 fusion.62
  61.3 6.0 %convolution_convert_fusion.4 = bf16[1024,1024]{0,1:T(8,128)(2,1)} fusion(bf16[2048,1024]{1,0:T(8,128)(2,1)S(1)} %copy-done.29, f32[1024,2048]{1,0:T(8,128)S(1)} %fusion.62), kind=kOutput, calls=%fused_computation.91 | convolution fusion | flops 4314890240 | bytes 14680064 | tf_op jit(solution)/shard_map/dot_general | solution.py:205
  67.4 3.9 copy.32
  73.9 3.1 fusion.34
  77.0 3.8 fusion.22
  80.9 6.0 %fusion.24 = (f32[1024]{0:T(1024)S(1)}, f32[1024]{0:T(1024)S(1)}, bf16[1,1024,1024]{1,2,0:T(8,128)(2,1)}) fusion(bf16[1,1024,1024]{1,2,0:T(8,128)(2,1)S(1)} %copy-done.8, bf16[1024,1024]{0,1:T(8,128)(2,1)} %collective-permute-done.1, bf16[1024,1024]{0,1:T(8,128)(2,1)} %convolution_convert_fusion.4, f32[1024]{0:T(1024)S(1)} %get-tuple-element.74, ...), kind=kLoop, calls=%fused_computation.38 | loop fusion | flops 18872320 | bytes 12611584 | tf_op jit(solution)/shard_map/transpose(jvp())/reduce_sum | solution.py:162
  86.9 15.2 %fusion.3 = bf16[1024,2048]{1,0:T(8,128)(2,1)S(1)} fusion(f32[1024,2048]{1,0:T(8,128)} %copy-done.36, bf16[2048,1024]{1,0:T(8,128)(2,1)S(1)} %copy-done.30, f32[1024]{0:T(1024)S(1)} %negate_multiply_fusion.3, bf16[1,1024,1024]{1,2,0:T(8,128)(2,1)S(1)} %copy-done.8, bf16[1024,1024]{0,1:T(8,128)(2,1)} %collective-permute-done.1, ...), kind=kOutput, calls=%fused_computation.7 | convolution fusion | flops 4357881856 | bytes 23089152 | tf_op jit(solution)/shard_map/dot_general | solution.py:205
  102.1 5.2 %convolution_convert_fusion.2 = bf16[1024,2048]{1,0:T(8,128)(2,1)S(1)} fusion(bf16[1024,2048]{1,0:T(8,128)(2,1)S(1)} %fusion.3, f32[1024,1024]{0,1:T(8,128)S(1)} %copy-done.2, f32[1024]{0:T(1024)S(1)} %bitcast.154, f32[1024]{0:T(1024)S(1)} %bitcast.128, f32[1024]{0:T(1024)S(1)} %fusion.59, f32[1024]{0:T(1024)S(1)} %broadcast_multiply_fusion.1), kind=kOutput, calls=%fused_computation.68 | convolution fusion | flops 4302307328 | bytes 12599296 | tf_op jit(solution)/shard_map/dot_general | solution.py:205
  111.3 6.4 %convolution_convert_fusion.3 = bf16[1024,1024]{0,1:T(8,128)(2,1)} fusion(bf16[1024,2048]{1,0:T(8,128)(2,1)S(1)} %fusion.3, bf16[1024,2048]{1,0:T(8,128)(2,1)S(1)} %copy-done.32), kind=kOutput, calls=%fused_computation.90 | convolution fusion | flops 4296015872 | bytes 10485760 | tf_op jit(solution)/shard_map/dot_general | solution.py:205
  117.6 15.8 %collective-permute-done.28 = bf16[256,2048]{1,0:T(8,128)(2,1)S(1)} collective-permute-done((bf16[256,2048]{1,0:T(8,128)(2,1)S(1)}, bf16[256,2048]{1,0:T(8,128)(2,1)S(1)}, u32[]{:S(2)}, u32[]{:S(2)}) %collective-permute-start.28) | collective-permute-done | bytes 1048608 | tf_op jit(solution)/shard_map/ppermute | solution.py:235
  139.2 8.1 %collective-permute-done.29 = bf16[128,2048]{1,0:T(8,128)(2,1)S(1)} collective-permute-done((bf16[128,2048]{1,0:T(8,128)(2,1)S(1)}, bf16[128,2048]{1,0:T(8,128)(2,1)S(1)}, u32[]{:S(2)}, u32[]{:S(2)}) %collective-permute-start.29) | collective-permute-done | bytes 524320 | tf_op jit(solution)/shard_map/ppermute | solution.py:235
  149.6 10.9 %convolution_convert_fusion.1 = bf16[2048,1024]{1,0:T(8,128)(2,1)} fusion(f32[1024]{0:T(1024)S(1)} %negate_multiply_fusion.3, f32[1024,2048]{1,0:T(8,128)S(1)} %bitcast.160, bf16[1,1024,1024]{1,2,0:T(8,128)(2,1)S(1)} %copy-done.8, bf16[1024,1024]{0,1:T(8,128)(2,1)} %collective-permute-done.1, bf16[1024,1024]{0,1:T(8,128)(2,1)} %convolution_convert_fusion.4, ...), kind=kOutput, calls=%fused_computation.67 | convolution fusion | flops 4328521728 | bytes 18894848 | tf_op jit(solution)/shard_map/dot_general | solution.py:205
  160.5 3.9 copy.37
  169.3 3.7 collective-permute-start.31
  173.1 5.0 %multiply_reduce_fusion.3 = f32[1024]{0:T(1024)S(1)} fusion(bf16[1024,1024]{0,1:T(8,128)(2,1)} %collective-permute-done.2, bf16[1024,1024]{0,1:T(8,128)(2,1)} %convolution_convert_fusion.3, f32[1024,1024]{0,1:T(8,128)} %copy-done.1, f32[1024]{0:T(1024)S(1)} %bitcast.129, f32[1024]{0:T(1024)S(1)} %broadcast_multiply_fusion.1), kind=kLoop, calls=%fused_computation.52 | loop fusion | flops 7339008 | bytes 8400896 | tf_op jit(solution)/shard_map/transpose(jvp())/reduce_sum | solution.py:162
  178.1 4.6 multiply_reduce_fusion.1
  182.7 6.1 %multiply_reduce_fusion = (f32[1024]{0:T(1024)S(1)}, f32[1024]{0:T(1024)S(1)}, f32[1024]{0:T(1024)S(1)}, f32[1024,1024]{0,1:T(8,128)S(1)}) fusion(bf16[1024,1024]{0,1:T(8,128)(2,1)S(1)} %copy-done.13, bf16[1024,1024]{0,1:T(8,128)(2,1)S(1)} %copy-done.11, f32[1024]{0:T(1024)S(1)} %fusion.58, f32[1024]{0:T(1024)S(1)} %broadcast_multiply_fusion.2, ...), kind=kLoop, calls=%fused_computation.46 | loop fusion | flops 24114176 | bytes 18919424 | tf_op jit(solution)/shard_map/transpose(jvp())/reduce_sum | solution.py:162
  196.4 2.9 collective-permute-start.38
  200.8 21.1 %attention_backward.1 = bf16[3,512,1024]{2,1,0:T(8,128)(2,1)} custom-call(bf16[3,512,1024]{2,1,0:T(8,128)(2,1)} %convert_bitcast_fusion.2.q_ref.k_ref.v_ref, bf16[3,512,1024]{2,1,0:T(8,128)(2,1)} %convert_bitcast_fusion.2.q_ref.k_ref.v_ref, bf16[3,512,1024]{2,1,0:T(8,128)(2,1)} %convert_bitcast_fusion.2.q_ref.k_ref.v_ref, ...), custom_call_target="tpu_custom_call" | custom-call | flops 5368709120 | bytes 8388608 | tf_op jit(solution)/shard_map/attention_backward/pallas_call | solution.py:137
  221.9 5.7 %bitcast_convert_fusion = bf16[1024,1024]{0,1:T(8,128)(2,1)S(1)} fusion(bf16[1024,3,512]{2,0,1:T(8,128)(2,1)S(1)} %copy-done, bf16[3,512,1024]{2,1,0:T(8,128)(2,1)} %attention_backward.1), kind=kOutput, calls=%fused_computation.45 | convolution fusion | flops 3222274048 | bytes 8388608 | tf_op jit(solution)/shard_map/dot_general | solution.py:368
  227.7 4.0 convolution_convert_fusion
  238.9 17.9 %collective-permute-done.9 = bf16[256,1536]{1,0:T(8,128)(2,1)S(1)} collective-permute-done((bf16[256,1536]{1,0:T(8,128)(2,1)S(1)}, bf16[256,1536]{1,0:T(8,128)(2,1)S(1)}, u32[]{:S(2)}, u32[]{:S(2)}) %collective-permute-start.9) | collective-permute-done | bytes 786464 | tf_op jit(solution)/shard_map/ppermute | solution.py:235
  262.0 3.0 add_convert_fusion.10
  265.4 9.4 %collective-permute-done.39 = bf16[128,2048]{1,0:T(8,128)(2,1)S(1)} collective-permute-done((bf16[128,2048]{1,0:T(8,128)(2,1)S(1)}, bf16[128,2048]{1,0:T(8,128)(2,1)S(1)}, u32[]{:S(2)}, u32[]{:S(2)}) %collective-permute-start.39) | collective-permute-done | bytes 524320 | tf_op jit(solution)/shard_map/ppermute | solution.py:235
  278.4 36.0 %collective-permute-done.33 = bf16[128,2048]{1,0:T(8,128)(2,1)S(1)} collective-permute-done((bf16[128,2048]{1,0:T(8,128)(2,1)S(1)}, bf16[128,2048]{1,0:T(8,128)(2,1)S(1)}, u32[]{:S(2)}, u32[]{:S(2)}) %collective-permute-start.33) | collective-permute-done | bytes 524320 | tf_op jit(solution)/shard_map/ppermute | solution.py:235
  320.2 7.9 %collective-permute-done.18 = bf16[128,1536]{1,0:T(8,128)(2,1)S(1)} collective-permute-done((bf16[128,1536]{1,0:T(8,128)(2,1)S(1)}, bf16[128,1536]{1,0:T(8,128)(2,1)S(1)}, u32[]{:S(2)}, u32[]{:S(2)}) %collective-permute-start.18) | collective-permute-done | bytes 393248 | tf_op jit(solution)/shard_map/ppermute | solution.py:235
  328.1 3.7 collective-permute-start.12
  335.2 3.5 fusion.21
  338.8 25.0 %collective-permute-done.12 = bf16[128,1536]{1,0:T(8,128)(2,1)S(1)} collective-permute-done((bf16[128,1536]{1,0:T(8,128)(2,1)S(1)}, bf16[128,1536]{1,0:T(8,128)(2,1)S(1)}, u32[]{:S(2)}, u32[]{:S(2)}) %collective-permute-start.12) | collective-permute-done | bytes 393248 | tf_op jit(solution)/shard_map/ppermute | solution.py:235
  363.9 3.6 collective-permute-done.4
  370.4 12.2 %collective-permute-done.19 = bf16[128,1536]{1,0:T(8,128)(2,1)S(1)} collective-permute-done((bf16[128,1536]{1,0:T(8,128)(2,1)S(1)}, bf16[128,1536]{1,0:T(8,128)(2,1)S(1)}, u32[]{:S(2)}, u32[]{:S(2)}) %collective-permute-start.19) | collective-permute-done | bytes 393248 | tf_op jit(solution)/shard_map/ppermute | solution.py:235
  384.9 6.7 %convert_element_type.454 = f32[2048,1024]{1,0:T(8,128)} convert(bf16[2048,1024]{1,0:T(8,128)(2,1)} %all-reduce.10.cloned.1.call-done) | non-fusion elementwise | flops 2097152 | bytes 12582912 | tf_op jit(solution)/shard_map/convert_element_type | solution.py:322
  401.7 3.3 collective-permute-done.7
  406.4 4.6 collective-permute-start.8
  412.7 16.5 %collective-permute-done.25 = bf16[512,1024]{1,0:T(8,128)(2,1)S(1)} collective-permute-done((bf16[512,1024]{1,0:T(8,128)(2,1)S(1)}, bf16[512,1024]{1,0:T(8,128)(2,1)S(1)}, u32[]{:S(2)}, u32[]{:S(2)}) %collective-permute-start.25) | collective-permute-done | bytes 1048608 | tf_op jit(solution)/shard_map/ppermute | solution.py:235
  430.1 3.7 collective-permute-start.26
  434.9 4.1 collective-permute-done.21
  440.5 12.9 %collective-permute-done.26 = bf16[512,1024]{1,0:T(8,128)(2,1)S(1)} collective-permute-done((bf16[512,1024]{1,0:T(8,128)(2,1)S(1)}, bf16[512,1024]{1,0:T(8,128)(2,1)S(1)}, u32[]{:S(2)}, u32[]{:S(2)}) %collective-permute-start.26) | collective-permute-done | bytes 1048608 | tf_op jit(solution)/shard_map/ppermute | solution.py:235
  459.4 3.5 fusion.38
  462.9 4.0 copy.38
  467.5 8.1 %assemble.3 = f32[4,256,2048]{2,1,0:T(8,128)} custom-call(s32[2]{0:T(128)} %pad_add_fusion.bits_ref, bf16[256,2048]{1,0:T(8,128)(2,1)} %pad_maximum_fusion.own_a, bf16[256,2048]{1,0:T(8,128)(2,1)} %collective-permute-done.34.other_a, bf16[256,2048]{1,0:T(8,128)(2,1)} %pad_maximum_fusion.1.own_b, bf16[256,2048]{1,0:T(8,128)(2,1)} %collective-permute-done.41.other_b), custom_call_target="tpu_custom_call" | custom-call | bytes 12582912 | tf_op jit(solution)/shard_map/assemble/pallas_call | solution.py:295
  475.5 8.4 %assemble.2 = f32[4,256,3,512]{3,2,1,0:T(4,128)} custom-call(s32[2]{0:T(128)} %pad_add_fusion.bits_ref, bf16[256,1536]{1,0:T(8,128)(2,1)} %pad_maximum_fusion.2.own_a, bf16[256,1536]{1,0:T(8,128)(2,1)} %collective-permute-done.15.other_a, bf16[256,1536]{1,0:T(8,128)(2,1)} %pad_maximum_fusion.3.own_b, bf16[256,1536]{1,0:T(8,128)(2,1)} %collective-permute-done.22.other_b), custom_call_target="tpu_custom_call" | custom-call | bytes 9437184 | tf_op jit(solution)/shard_map/assemble/pallas_call | solution.py:295
  484.0 8.1 %copy.39 = f32[1024,3,512]{2,0,1:T(8,128)} copy(f32[1024,3,512]{2,1,0:T(4,128)} %bitcast.122) | data formatting | bytes 12582912
  (235 shorter events, 103.1 us)
Async XLA Ops:
  7.2 377.8 %all-reduce.10.cloned.1.call-start = ((), (), s32[]{:S(2)}) async-start(), calls=%async_computation | async-start | bytes 8388608 | tf_op jit(solution)/shard_map/psum | solution.py:322
  44.4 4.2 collective-permute-start
  67.3 6.6 %collective-permute-start.1 = (bf16[1024,1024]{0,1:T(8,128)(2,1)}, bf16[1024,1024]{0,1:T(8,128)(2,1)}, u32[]{:S(2)}, u32[]{:S(2)}) collective-permute-start(bf16[1024,1024]{0,1:T(8,128)(2,1)} %convolution_convert_fusion.4), channel_id=1, source_target_pairs={{0,1},{1,0},{2,3},{3,2},{4,5},{5,4},{6,7},{7,6},{8,9},{9,8},{10,11... | collective-permute-start | bytes 6291464 | tf_op jit(solution)/shard_map/ppermute | solution.py:317
  107.9 41.7 %slice-start = ((s8[8388608]{0:T(1024)(128)(4,1)}), s8[4194304]{0:T(1024)(128)(4,1)S(1)}, s32[]{:S(2)}) async-start(s8[8388608]{0:T(1024)(128)(4,1)} %bitcast.159), calls=%async_computation.1 | async-start | bytes 8388608
  108.0 25.5 %collective-permute-start.28 = (bf16[256,2048]{1,0:T(8,128)(2,1)S(1)}, bf16[256,2048]{1,0:T(8,128)(2,1)S(1)}, u32[]{:S(2)}, u32[]{:S(2)}) collective-permute-start(bf16[256,2048]{1,0:T(8,128)(2,1)S(1)} %constant_dynamic-slice_fusion.3), channel_id=1, source_target_pairs={{0,2},{2,0},{4,6},{6,4},{8,10},{10,8},{12,14},{14,12},{16,18},{18,... | collective-permute-start | bytes 3145736 | tf_op jit(solution)/shard_map/ppermute | solution.py:235
  109.7 39.9 %slice-start.1 = ((s8[8388608]{0:T(1024)(128)(4,1)}), s8[4194304]{0:T(1024)(128)(4,1)S(1)}, s32[]{:S(2)}) async-start(s8[8388608]{0:T(1024)(128)(4,1)} %bitcast.159), calls=%async_computation.2 | async-start | bytes 8388608
  109.7 25.8 %collective-permute-start.35 = (bf16[256,2048]{1,0:T(8,128)(2,1)S(1)}, bf16[256,2048]{1,0:T(8,128)(2,1)S(1)}, u32[]{:S(2)}, u32[]{:S(2)}) collective-permute-start(bf16[256,2048]{1,0:T(8,128)(2,1)S(1)} %constant_dynamic-slice_fusion.1), channel_id=1, source_target_pairs={{0,4},{2,6},{4,0},{6,2},{8,12},{10,14},{12,8},{14,10},{16,20},{18,... | collective-permute-start | bytes 3145736 | tf_op jit(solution)/shard_map/ppermute | solution.py:235
  117.6 55.4 %collective-permute-start.2 = (bf16[1024,1024]{0,1:T(8,128)(2,1)}, bf16[1024,1024]{0,1:T(8,128)(2,1)}, u32[]{:S(2)}, u32[]{:S(2)}) collective-permute-start(bf16[1024,1024]{0,1:T(8,128)(2,1)} %convolution_convert_fusion.3), channel_id=1, source_target_pairs={{0,1},{1,0},{2,3},{3,2},{4,5},{5,4},{6,7},{7,6},{8,9},{9,8},{10,11... | collective-permute-start | bytes 6291464 | tf_op jit(solution)/shard_map/ppermute | solution.py:317
  133.9 13.4 %collective-permute-start.29 = (bf16[128,2048]{1,0:T(8,128)(2,1)S(1)}, bf16[128,2048]{1,0:T(8,128)(2,1)S(1)}, u32[]{:S(2)}, u32[]{:S(2)}) collective-permute-start(bf16[128,2048]{1,0:T(8,128)(2,1)S(1)} %constant_dynamic-slice_fusion.2), channel_id=1, source_target_pairs={{0,4},{2,6},{4,0},{6,2},{8,12},{10,14},{12,8},{14,10},{16,20},{18,... | collective-permute-start | bytes 1572872 | tf_op jit(solution)/shard_map/ppermute | solution.py:235
  137.7 26.7 %collective-permute-start.36 = (bf16[128,2048]{1,0:T(8,128)(2,1)}, bf16[128,2048]{1,0:T(8,128)(2,1)}, u32[]{:S(2)}, u32[]{:S(2)}) collective-permute-start(bf16[128,2048]{1,0:T(8,128)(2,1)} %constant_dynamic-slice_fusion), channel_id=1, source_target_pairs={{0,2},{2,0},{4,6},{6,4},{8,10},{10,8},{12,14},{14,12},{16,18},{18,... | collective-permute-start | bytes 1572872 | tf_op jit(solution)/shard_map/ppermute | solution.py:235
  148.3 18.9 %collective-permute-start.30 = (bf16[128,2048]{1,0:T(8,128)(2,1)}, bf16[128,2048]{1,0:T(8,128)(2,1)}, u32[]{:S(2)}, u32[]{:S(2)}) collective-permute-start(bf16[128,2048]{1,0:T(8,128)(2,1)} %add_convert_fusion.18), channel_id=1, source_target_pairs={{0,8},{2,10},{4,12},{6,14},{24,16},{26,18},{28,20},{30,22},{1,9},{... | collective-permute-start | bytes 1572872 | tf_op jit(solution)/shard_map/ppermute | solution.py:235
  165.8 29.6 %collective-permute-start.37 = (bf16[128,2048]{1,0:T(8,128)(2,1)S(1)}, bf16[128,2048]{1,0:T(8,128)(2,1)S(1)}, u32[]{:S(2)}, u32[]{:S(2)}) collective-permute-start(bf16[128,2048]{1,0:T(8,128)(2,1)S(1)} %add_convert_fusion.15), channel_id=1, source_target_pairs={{0,8},{2,10},{4,12},{6,14},{24,16},{26,18},{28,20},{30,22},{1,9},{... | collective-permute-start | bytes 1572872 | tf_op jit(solution)/shard_map/ppermute | solution.py:235
  169.3 63.5 %collective-permute-start.31 = (bf16[128,2048]{1,0:T(8,128)(2,1)}, bf16[128,2048]{1,0:T(8,128)(2,1)}, u32[]{:S(2)}, u32[]{:S(2)}) collective-permute-start(bf16[128,2048]{1,0:T(8,128)(2,1)} %add_convert_fusion.17), channel_id=1, source_target_pairs={{8,16},{10,18},{12,20},{14,22},{16,8},{18,10},{20,12},{22,14},{9,1... | collective-permute-start | bytes 1572872 | tf_op jit(solution)/shard_map/ppermute | solution.py:235
  196.4 39.3 %collective-permute-start.38 = (bf16[128,2048]{1,0:T(8,128)(2,1)}, bf16[128,2048]{1,0:T(8,128)(2,1)}, u32[]{:S(2)}, u32[]{:S(2)}) collective-permute-start(bf16[128,2048]{1,0:T(8,128)(2,1)} %add_convert_fusion.14), channel_id=1, source_target_pairs={{8,16},{10,18},{12,20},{14,22},{16,8},{18,10},{20,12},{22,14},{9,1... | collective-permute-start | bytes 1572872 | tf_op jit(solution)/shard_map/ppermute | solution.py:235
  199.3 62.0 %collective-permute-start.23 = (bf16[512,1024]{1,0:T(8,128)(2,1)}, bf16[512,1024]{1,0:T(8,128)(2,1)}, u32[]{:S(2)}, u32[]{:S(2)}) collective-permute-start(bf16[512,1024]{1,0:T(8,128)(2,1)} %convolution_convert_fusion.7), channel_id=1, source_target_pairs={{0,2},{2,0},{4,6},{6,4},{8,10},{10,8},{12,14},{14,12},{16,18},{18,... | collective-permute-start | bytes 3145736 | tf_op jit(solution)/shard_map/ppermute | solution.py:235
  227.6 107.6 %copy-start.16 = (bf16[1024,1024]{0,1:T(8,128)(2,1)}, bf16[1024,1024]{0,1:T(8,128)(2,1)S(1)}, u32[]{:S(2)}) copy-start(bf16[1024,1024]{0,1:T(8,128)(2,1)S(1)} %bitcast_convert_fusion) | copy-start | bytes 6291460
  227.6 104.3 %collective-permute-start.3 = (bf16[1024,1024]{0,1:T(8,128)(2,1)S(1)}, bf16[1024,1024]{0,1:T(8,128)(2,1)S(1)}, u32[]{:S(2)}, u32[]{:S(2)}) collective-permute-start(bf16[1024,1024]{0,1:T(8,128)(2,1)S(1)} %bitcast_convert_fusion), channel_id=1, source_target_pairs={{0,1},{1,0},{2,3},{3,2},{4,5},{5,4},{6,7},{7,6},{8,9},{9,8},{10,11... | collective-permute-start | bytes 6291464 | tf_op jit(solution)/shard_map/ppermute | solution.py:317
  232.1 24.7 %collective-permute-start.9 = (bf16[256,1536]{1,0:T(8,128)(2,1)S(1)}, bf16[256,1536]{1,0:T(8,128)(2,1)S(1)}, u32[]{:S(2)}, u32[]{:S(2)}) collective-permute-start(bf16[256,1536]{1,0:T(8,128)(2,1)S(1)} %constant_dynamic-slice_fusion.7), channel_id=1, source_target_pairs={{0,2},{2,0},{4,6},{6,4},{8,10},{10,8},{12,14},{14,12},{16,18},{18,... | collective-permute-start | bytes 2359304 | tf_op jit(solution)/shard_map/ppermute | solution.py:235
  232.8 26.8 %collective-permute-start.16 = (bf16[256,1536]{1,0:T(8,128)(2,1)S(1)}, bf16[256,1536]{1,0:T(8,128)(2,1)S(1)}, u32[]{:S(2)}, u32[]{:S(2)}) collective-permute-start(bf16[256,1536]{1,0:T(8,128)(2,1)S(1)} %constant_dynamic-slice_fusion.5), channel_id=1, source_target_pairs={{0,4},{2,6},{4,0},{6,2},{8,12},{10,14},{12,8},{14,10},{16,20},{18,... | collective-permute-start | bytes 2359304 | tf_op jit(solution)/shard_map/ppermute | solution.py:235
  235.7 29.3 %collective-permute-start.32 = (bf16[128,2048]{1,0:T(8,128)(2,1)S(1)}, bf16[128,2048]{1,0:T(8,128)(2,1)S(1)}, u32[]{:S(2)}, u32[]{:S(2)}) collective-permute-start(bf16[128,2048]{1,0:T(8,128)(2,1)S(1)} %add_convert_fusion.16), channel_id=1, source_target_pairs={{8,0},{10,2},{12,4},{14,6},{16,24},{18,26},{20,28},{22,30},{9,1},{... | collective-permute-start | bytes 1572872 | tf_op jit(solution)/shard_map/ppermute | solution.py:235
  256.8 18.0 %collective-permute-start.39 = (bf16[128,2048]{1,0:T(8,128)(2,1)S(1)}, bf16[128,2048]{1,0:T(8,128)(2,1)S(1)}, u32[]{:S(2)}, u32[]{:S(2)}) collective-permute-start(bf16[128,2048]{1,0:T(8,128)(2,1)S(1)} %add_convert_fusion.13), channel_id=1, source_target_pairs={{8,0},{10,2},{12,4},{14,6},{16,24},{18,26},{20,28},{22,30},{9,1},{... | collective-permute-start | bytes 1572872 | tf_op jit(solution)/shard_map/ppermute | solution.py:235
  259.5 16.7 %collective-permute-start.10 = (bf16[128,1536]{1,0:T(8,128)(2,1)S(1)}, bf16[128,1536]{1,0:T(8,128)(2,1)S(1)}, u32[]{:S(2)}, u32[]{:S(2)}) collective-permute-start(bf16[128,1536]{1,0:T(8,128)(2,1)S(1)} %constant_dynamic-slice_fusion.6), channel_id=1, source_target_pairs={{0,4},{2,6},{4,0},{6,2},{8,12},{10,14},{12,8},{14,10},{16,20},{18,... | collective-permute-start | bytes 1179656 | tf_op jit(solution)/shard_map/ppermute | solution.py:235
  261.3 15.7 %collective-permute-start.17 = (bf16[128,1536]{1,0:T(8,128)(2,1)S(1)}, bf16[128,1536]{1,0:T(8,128)(2,1)S(1)}, u32[]{:S(2)}, u32[]{:S(2)}) collective-permute-start(bf16[128,1536]{1,0:T(8,128)(2,1)S(1)} %constant_dynamic-slice_fusion.4), channel_id=1, source_target_pairs={{0,2},{2,0},{4,6},{6,4},{8,10},{10,8},{12,14},{14,12},{16,18},{18,... | collective-permute-start | bytes 1179656 | tf_op jit(solution)/shard_map/ppermute | solution.py:235
  265.0 128.8 %collective-permute-start.24 = (bf16[512,1024]{1,0:T(8,128)(2,1)}, bf16[512,1024]{1,0:T(8,128)(2,1)}, u32[]{:S(2)}, u32[]{:S(2)}) collective-permute-start(bf16[512,1024]{1,0:T(8,128)(2,1)} %add_convert_fusion.10), channel_id=1, source_target_pairs={{0,4},{2,6},{4,0},{6,2},{8,12},{10,14},{12,8},{14,10},{16,20},{18,... | collective-permute-start | bytes 3145736 | tf_op jit(solution)/shard_map/ppermute | solution.py:235
  274.7 39.7 %collective-permute-start.33 = (bf16[128,2048]{1,0:T(8,128)(2,1)S(1)}, bf16[128,2048]{1,0:T(8,128)(2,1)S(1)}, u32[]{:S(2)}, u32[]{:S(2)}) collective-permute-start(bf16[128,2048]{1,0:T(8,128)(2,1)S(1)} %broadcast_select_fusion.3), channel_id=1, source_target_pairs={{0,4},{2,6},{4,0},{6,2},{8,12},{10,14},{12,8},{14,10},{16,20},{18,... | collective-permute-start | bytes 1572872 | tf_op jit(solution)/shard_map/ppermute | solution.py:235
  276.3 40.6 %collective-permute-start.40 = (bf16[128,2048]{1,0:T(8,128)(2,1)S(1)}, bf16[128,2048]{1,0:T(8,128)(2,1)S(1)}, u32[]{:S(2)}, u32[]{:S(2)}) collective-permute-start(bf16[128,2048]{1,0:T(8,128)(2,1)S(1)} %broadcast_select_fusion.2), channel_id=1, source_target_pairs={{0,2},{2,0},{4,6},{6,4},{8,10},{10,8},{12,14},{14,12},{16,18},{18,... | collective-permute-start | bytes 1572872 | tf_op jit(solution)/shard_map/ppermute | solution.py:235
  277.0 41.3 %collective-permute-start.11 = (bf16[128,1536]{1,0:T(8,128)(2,1)S(1)}, bf16[128,1536]{1,0:T(8,128)(2,1)S(1)}, u32[]{:S(2)}, u32[]{:S(2)}) collective-permute-start(bf16[128,1536]{1,0:T(8,128)(2,1)S(1)} %add_convert_fusion.30), channel_id=1, source_target_pairs={{0,8},{2,10},{4,12},{6,14},{24,16},{26,18},{28,20},{30,22},{1,9},{... | collective-permute-start | bytes 1179656 | tf_op jit(solution)/shard_map/ppermute | solution.py:235
  314.4 13.6 %collective-permute-start.18 = (bf16[128,1536]{1,0:T(8,128)(2,1)S(1)}, bf16[128,1536]{1,0:T(8,128)(2,1)S(1)}, u32[]{:S(2)}, u32[]{:S(2)}) collective-permute-start(bf16[128,1536]{1,0:T(8,128)(2,1)S(1)} %add_convert_fusion.27), channel_id=1, source_target_pairs={{0,8},{2,10},{4,12},{6,14},{24,16},{26,18},{28,20},{30,22},{1,9},{... | collective-permute-start | bytes 1179656 | tf_op jit(solution)/shard_map/ppermute | solution.py:235
  316.9 150.6 %collective-permute-start.34 = (bf16[256,2048]{1,0:T(8,128)(2,1)}, bf16[256,2048]{1,0:T(8,128)(2,1)}, u32[]{:S(2)}, u32[]{:S(2)}) collective-permute-start(bf16[256,2048]{1,0:T(8,128)(2,1)} %pad_maximum_fusion.own_a), channel_id=1, source_target_pairs={{0,2},{2,0},{4,6},{6,4},{8,10},{10,8},{12,14},{14,12},{16,18},{18,... | collective-permute-start | bytes 3145736 | tf_op jit(solution)/shard_map/ppermute | solution.py:235
  318.3 149.2 %collective-permute-start.41 = (bf16[256,2048]{1,0:T(8,128)(2,1)}, bf16[256,2048]{1,0:T(8,128)(2,1)}, u32[]{:S(2)}, u32[]{:S(2)}) collective-permute-start(bf16[256,2048]{1,0:T(8,128)(2,1)} %pad_maximum_fusion.1.own_b), channel_id=1, source_target_pairs={{0,4},{2,6},{4,0},{6,2},{8,12},{10,14},{12,8},{14,10},{16,20},{18,... | collective-permute-start | bytes 3145736 | tf_op jit(solution)/shard_map/ppermute | solution.py:235
  328.1 35.7 %collective-permute-start.12 = (bf16[128,1536]{1,0:T(8,128)(2,1)S(1)}, bf16[128,1536]{1,0:T(8,128)(2,1)S(1)}, u32[]{:S(2)}, u32[]{:S(2)}) collective-permute-start(bf16[128,1536]{1,0:T(8,128)(2,1)S(1)} %add_convert_fusion.29), channel_id=1, source_target_pairs={{8,16},{10,18},{12,20},{14,22},{16,8},{18,10},{20,12},{22,14},{9,1... | collective-permute-start | bytes 1179656 | tf_op jit(solution)/shard_map/ppermute | solution.py:235
  331.9 50.7 %collective-permute-start.19 = (bf16[128,1536]{1,0:T(8,128)(2,1)S(1)}, bf16[128,1536]{1,0:T(8,128)(2,1)S(1)}, u32[]{:S(2)}, u32[]{:S(2)}) collective-permute-start(bf16[128,1536]{1,0:T(8,128)(2,1)S(1)} %add_convert_fusion.26), channel_id=1, source_target_pairs={{8,16},{10,18},{12,20},{14,22},{16,8},{18,10},{20,12},{22,14},{9,1... | collective-permute-start | bytes 1179656 | tf_op jit(solution)/shard_map/ppermute | solution.py:235
  363.8 3.7 collective-permute-start.4
  367.5 38.8 %collective-permute-start.13 = (bf16[128,1536]{1,0:T(8,128)(2,1)S(1)}, bf16[128,1536]{1,0:T(8,128)(2,1)}, u32[]{:S(2)}, u32[]{:S(2)}) collective-permute-start(bf16[128,1536]{1,0:T(8,128)(2,1)S(1)} %add_convert_fusion.28), channel_id=1, source_target_pairs={{8,0},{10,2},{12,4},{14,6},{16,24},{18,26},{20,28},{22,30},{9,1},{... | collective-permute-start | bytes 1179656 | tf_op jit(solution)/shard_map/ppermute | solution.py:235
  382.6 9.0 %collective-permute-start.5 = (bf16[8,1024]{1,0:T(8,128)(2,1)}, bf16[8,1024]{1,0:T(8,128)(2,1)}, u32[]{:S(2)}, u32[]{:S(2)}) collective-permute-start(bf16[8,1024]{1,0:T(8,128)(2,1)} %add_convert_fusion.34), channel_id=1, source_target_pairs={{0,4},{2,6},{4,0},{6,2},{8,12},{10,14},{12,8},{14,10},{16,20},{18,... | collective-permute-start | bytes 49160 | tf_op jit(solution)/shard_map/ppermute | solution.py:235
  391.6 19.4 %collective-permute-start.20 = (bf16[128,1536]{1,0:T(8,128)(2,1)S(1)}, bf16[128,1536]{1,0:T(8,128)(2,1)S(1)}, u32[]{:S(2)}, u32[]{:S(2)}) collective-permute-start(bf16[128,1536]{1,0:T(8,128)(2,1)S(1)} %copy-done.21), channel_id=1, source_target_pairs={{8,0},{10,2},{12,4},{14,6},{16,24},{18,26},{20,28},{22,30},{9,1},{... | collective-permute-start | bytes 1179656 | tf_op jit(solution)/shard_map/ppermute | solution.py:235
  393.8 5.6 %collective-permute-start.6 = (bf16[8,1024]{1,0:T(8,128)(2,1)S(1)}, bf16[8,1024]{1,0:T(8,128)(2,1)S(1)}, u32[]{:S(2)}, u32[]{:S(2)}) collective-permute-start(bf16[8,1024]{1,0:T(8,128)(2,1)S(1)} %add_convert_fusion.33), channel_id=1, source_target_pairs={{0,8},{2,10},{4,12},{6,14},{24,16},{26,18},{28,20},{30,22},{1,9},{... | collective-permute-start | bytes 49160 | tf_op jit(solution)/shard_map/ppermute | solution.py:235
  399.4 5.6 %collective-permute-start.7 = (bf16[8,1024]{1,0:T(8,128)(2,1)S(1)}, bf16[8,1024]{1,0:T(8,128)(2,1)S(1)}, u32[]{:S(2)}, u32[]{:S(2)}) collective-permute-start(bf16[8,1024]{1,0:T(8,128)(2,1)S(1)} %add_convert_fusion.32), channel_id=1, source_target_pairs={{8,16},{10,18},{12,20},{14,22},{16,8},{18,10},{20,12},{22,14},{9,1... | collective-permute-start | bytes 49160 | tf_op jit(solution)/shard_map/ppermute | solution.py:235
  405.0 24.1 %collective-permute-start.25 = (bf16[512,1024]{1,0:T(8,128)(2,1)S(1)}, bf16[512,1024]{1,0:T(8,128)(2,1)S(1)}, u32[]{:S(2)}, u32[]{:S(2)}) collective-permute-start(bf16[512,1024]{1,0:T(8,128)(2,1)S(1)} %add_convert_fusion.9), channel_id=1, source_target_pairs={{0,8},{2,10},{4,12},{6,14},{24,16},{26,18},{28,20},{30,22},{1,9},{... | collective-permute-start | bytes 3145736 | tf_op jit(solution)/shard_map/ppermute | solution.py:235
  406.4 28.6 %copy-start.22 = (bf16[8,1024]{1,0:T(8,128)(2,1)}, bf16[8,1024]{1,0:T(8,128)(2,1)S(1)}, u32[]{:S(2)}) copy-start(bf16[8,1024]{1,0:T(8,128)(2,1)S(1)} %add_convert_fusion.31) | copy-start | bytes 49156
  406.4 50.1 %collective-permute-start.8 = (bf16[8,1024]{1,0:T(8,128)(2,1)S(1)}, bf16[8,1024]{1,0:T(8,128)(2,1)S(1)}, u32[]{:S(2)}, u32[]{:S(2)}) collective-permute-start(bf16[8,1024]{1,0:T(8,128)(2,1)S(1)} %add_convert_fusion.31), channel_id=1, source_target_pairs={{8,0},{10,2},{12,4},{14,6},{16,24},{18,26},{20,28},{22,30},{9,1},{... | collective-permute-start | bytes 49160 | tf_op jit(solution)/shard_map/ppermute | solution.py:235
  411.1 19.1 %collective-permute-start.14 = (bf16[128,1536]{1,0:T(8,128)(2,1)S(1)}, bf16[128,1536]{1,0:T(8,128)(2,1)S(1)}, u32[]{:S(2)}, u32[]{:S(2)}) collective-permute-start(bf16[128,1536]{1,0:T(8,128)(2,1)S(1)} %broadcast_select_fusion.9), channel_id=1, source_target_pairs={{0,4},{2,6},{4,0},{6,2},{8,12},{10,14},{12,8},{14,10},{16,20},{18,... | collective-permute-start | bytes 1179656 | tf_op jit(solution)/shard_map/ppermute | solution.py:235
  429.2 9.8 %collective-permute-start.21 = (bf16[128,1536]{1,0:T(8,128)(2,1)S(1)}, bf16[128,1536]{1,0:T(8,128)(2,1)S(1)}, u32[]{:S(2)}, u32[]{:S(2)}) collective-permute-start(bf16[128,1536]{1,0:T(8,128)(2,1)S(1)} %broadcast_select_fusion.8), channel_id=1, source_target_pairs={{0,2},{2,0},{4,6},{6,4},{8,10},{10,8},{12,14},{14,12},{16,18},{18,... | collective-permute-start | bytes 1179656 | tf_op jit(solution)/shard_map/ppermute | solution.py:235
  429.7 29.7 %copy-start.19 = (bf16[1024,1024]{0,1:T(8,128)(2,1)S(1)}, bf16[1024,1024]{0,1:T(8,128)(2,1)}, u32[]{:S(2)}) copy-start(bf16[1024,1024]{0,1:T(8,128)(2,1)} %copy-done.18) | copy-start | bytes 6291460
  430.1 23.3 %collective-permute-start.26 = (bf16[512,1024]{1,0:T(8,128)(2,1)S(1)}, bf16[512,1024]{1,0:T(8,128)(2,1)S(1)}, u32[]{:S(2)}, u32[]{:S(2)}) collective-permute-start(bf16[512,1024]{1,0:T(8,128)(2,1)S(1)} %add_convert_fusion.8), channel_id=1, source_target_pairs={{8,16},{10,18},{12,20},{14,22},{16,8},{18,10},{20,12},{22,14},{9,1... | collective-permute-start | bytes 3145736 | tf_op jit(solution)/shard_map/ppermute | solution.py:235
  439.0 36.6 %collective-permute-start.15 = (bf16[256,1536]{1,0:T(8,128)(2,1)}, bf16[256,1536]{1,0:T(8,128)(2,1)}, u32[]{:S(2)}, u32[]{:S(2)}) collective-permute-start(bf16[256,1536]{1,0:T(8,128)(2,1)} %pad_maximum_fusion.2.own_a), channel_id=1, source_target_pairs={{0,2},{2,0},{4,6},{6,4},{8,10},{10,8},{12,14},{14,12},{16,18},{18,... | collective-permute-start | bytes 2359304 | tf_op jit(solution)/shard_map/ppermute | solution.py:235
  453.5 22.1 %collective-permute-start.22 = (bf16[256,1536]{1,0:T(8,128)(2,1)}, bf16[256,1536]{1,0:T(8,128)(2,1)}, u32[]{:S(2)}, u32[]{:S(2)}) collective-permute-start(bf16[256,1536]{1,0:T(8,128)(2,1)} %pad_maximum_fusion.3.own_b), channel_id=1, source_target_pairs={{0,4},{2,6},{4,0},{6,2},{8,12},{10,14},{12,8},{14,10},{16,20},{18,... | collective-permute-start | bytes 2359304 | tf_op jit(solution)/shard_map/ppermute | solution.py:235
  457.1 35.0 %collective-permute-start.27 = (bf16[512,1024]{1,0:T(8,128)(2,1)}, bf16[512,1024]{1,0:T(8,128)(2,1)}, u32[]{:S(2)}, u32[]{:S(2)}) collective-permute-start(bf16[512,1024]{1,0:T(8,128)(2,1)} %add_convert_fusion.7), channel_id=1, source_target_pairs={{8,0},{10,2},{12,4},{14,6},{16,24},{18,26},{20,28},{22,30},{9,1},{... | collective-permute-start | bytes 3145736 | tf_op jit(solution)/shard_map/ppermute | solution.py:235
  (34 other events, 251.5 us)
Sparse Core Ops, SparseCore 0:
  164.6 215.3 all-reduce.9

commit v2 on v1

v2 whole, which is shorter than its diff:
```python
import functools
import math

import jax, jax.numpy as jnp
from jax import lax
from jax.experimental import pallas as pl
from jax.experimental.pallas import tpu as pltpu
from jax.sharding import PartitionSpec as P

HEAD_DIM = 64
DOC_MOST = 384
NEGATIVE = -1e30
BLOCK = 256
AUG = 16


def spans(seq_len):
    block = min(BLOCK, seq_len)
    return [(q, block, max(0, q - DOC_MOST)) for q in range(0, seq_len, block)]


def dot(a, b):
    return lax.dot_general(a, b, (((1,), (0,)), ((), ())), preferred_element_type=jnp.float32)


def spin(u, cosine, sine, sign):
    half = u.shape[0] // 2
    first, second = u[:half].astype(jnp.float32), u[half:].astype(jnp.float32)
    return first * cosine - sign * second * sine, second * cosine + sign * first * sine


def turned(ref, cosine, sine, scale):
    first, second = spin(ref[0], cosine, sine, 1.0)
    return jnp.concatenate([first * scale, second * scale], axis=0).astype(jnp.bfloat16)


def causal(block):
    key = lax.broadcasted_iota(jnp.int32, (block, block), 0)
    query = lax.broadcasted_iota(jnp.int32, (block, block), 1)
    return key <= query


def masked(scores, keep, block):
    last = jnp.where(keep, scores[-block:], NEGATIVE)
    if scores.shape[0] == block:
        return last
    return jnp.concatenate([scores[:-block], last], axis=0)


def setup(q_ref, k_ref, cos_ref, sin_ref, qaug_ref, kaug_ref, qt_scr, kn_scr):
    cosine, sine = cos_ref[...], sin_ref[...]
    seq_len = q_ref.shape[-1]
    pad = jnp.zeros((128 - HEAD_DIM - AUG, seq_len), jnp.bfloat16)
    q_low = turned(q_ref, cosine, sine, HEAD_DIM ** -0.5)
    k_low = turned(k_ref, cosine, sine, 1.0)
    qt_scr[...] = jnp.concatenate([q_low, qaug_ref[...], pad], axis=0)
    k_all = jnp.concatenate([k_low, kaug_ref[...], pad], axis=0)
    kn_scr[...] = k_all.T
    return q_low, k_low


def fwd_kernel(q_ref, k_ref, v_ref, cos_ref, sin_ref, qaug_ref, kaug_ref, o_ref, lse_ref, qt_scr, kn_scr):
    seq_len = q_ref.shape[-1]
    setup(q_ref, k_ref, cos_ref, sin_ref, qaug_ref, kaug_ref, qt_scr, kn_scr)
    for start, block, low in spans(seq_len):
        high = start + block
        scores = dot(kn_scr[low:high, :], qt_scr[:, start:high])
        scores = masked(scores, causal(block), block)
        top = jnp.max(scores, axis=0, keepdims=True)
        expo = jnp.exp(scores - top)
        total = jnp.sum(expo, axis=0, keepdims=True)
        out = dot(v_ref[0, :, low:high], expo.astype(jnp.bfloat16)) / total
        o_ref[:, start:high] = out.astype(jnp.bfloat16)
        lse_ref[0, :, start:high] = top + jnp.log(total)


def bwd_kernel(q_ref, k_ref, v_ref, cos_ref, sin_ref, qaug_ref, kaug_ref, o_ref, lse_ref, do_ref,
               dm_ref, qt_scr, kn_scr, qn_scr, kt_scr, vn_scr, don_scr, dk_scr, dv_scr):
    seq_len = q_ref.shape[-1]
    cosine, sine = cos_ref[...], sin_ref[...]
    q_low, k_low = setup(q_ref, k_ref, cos_ref, sin_ref, qaug_ref, kaug_ref, qt_scr, kn_scr)
    kt_scr[...] = k_low
    both = jnp.concatenate([q_low, do_ref[...]], axis=0).T
    qn_scr[...] = both[:, :HEAD_DIM]
    don_scr[...] = both[:, HEAD_DIM:]
    vn_scr[...] = v_ref[0].T
    dk_scr[...] = jnp.zeros_like(dk_scr)
    dv_scr[...] = jnp.zeros_like(dv_scr)
    inner = jnp.sum(o_ref[...].astype(jnp.float32) * do_ref[...].astype(jnp.float32), axis=0, keepdims=True)
    for start, block, low in spans(seq_len):
        high = start + block
        scores = dot(kn_scr[low:high, :], qt_scr[:, start:high])
        scores = masked(scores, causal(block), block)
        soft = jnp.exp(scores - lse_ref[0, :, start:high])
        d_soft = dot(vn_scr[low:high, :], do_ref[:, start:high])
        d_scores = (soft * (d_soft - inner[:, start:high])).astype(jnp.bfloat16)
        d_q = dot(kt_scr[:, low:high], d_scores) * HEAD_DIM ** -0.5
        first, second = spin(d_q, cosine[:, start:high], sine[:, start:high], -1.0)
        half = HEAD_DIM // 2
        dm_ref[0, :half, start:high] = first.astype(jnp.bfloat16)
        dm_ref[0, half:, start:high] = second.astype(jnp.bfloat16)
        dk_scr[low:high, :] += dot(d_scores, qn_scr[start:high, :])
        dv_scr[low:high, :] += dot(soft.astype(jnp.bfloat16), don_scr[start:high, :])
    first, second = spin(dk_scr[...].T, cosine, sine, -1.0)
    dm_ref[1] = jnp.concatenate([first, second], axis=0).astype(jnp.bfloat16)
    dm_ref[2] = dv_scr[...].T.astype(jnp.bfloat16)


def common_specs(seq_len):
    part = lambda c: pl.BlockSpec((1, HEAD_DIM, seq_len), lambda h: (c, h, 0))
    whole = lambda rows: pl.BlockSpec((rows, seq_len), lambda h: (0, 0))
    half = HEAD_DIM // 2
    return [part(0), part(1), part(2), whole(half), whole(half), whole(AUG), whole(AUG)]


def attention_forward(mixed, cosine, sine, qaug, kaug):
    _, inner, seq_len = mixed.shape
    heads = inner // HEAD_DIM
    head_spec = pl.BlockSpec((HEAD_DIM, seq_len), lambda h: (h, 0))
    return pl.pallas_call(
        fwd_kernel,
        grid=(heads,),
        in_specs=common_specs(seq_len),
        out_specs=[head_spec, pl.BlockSpec((1, 1, seq_len), lambda h: (h, 0, 0))],
        out_shape=[jax.ShapeDtypeStruct((inner, seq_len), jnp.bfloat16),
                   jax.ShapeDtypeStruct((heads, 1, seq_len), jnp.float32)],
        scratch_shapes=[pltpu.VMEM((128, seq_len), jnp.bfloat16), pltpu.VMEM((seq_len, 128), jnp.bfloat16)],
        name="attention_forward",
        cost_estimate=pl.CostEstimate(flops=heads * 2 * 2 * seq_len * 512 * 128, bytes_accessed=inner * seq_len * 8, transcendentals=heads * seq_len * 512),
    )(mixed, mixed, mixed, cosine, sine, qaug, kaug)


def attention_backward(mixed, cosine, sine, qaug, kaug, att, lse, d_att):
    _, inner, seq_len = mixed.shape
    heads = inner // HEAD_DIM
    head_spec = pl.BlockSpec((HEAD_DIM, seq_len), lambda h: (h, 0))
    return pl.pallas_call(
        bwd_kernel,
        grid=(heads,),
        in_specs=common_specs(seq_len) + [head_spec, pl.BlockSpec((1, 1, seq_len), lambda h: (h, 0, 0)), head_spec],
        out_specs=pl.BlockSpec((3, HEAD_DIM, seq_len), lambda h: (0, h, 0)),
        out_shape=jax.ShapeDtypeStruct(mixed.shape, jnp.bfloat16),
        scratch_shapes=[pltpu.VMEM((128, seq_len), jnp.bfloat16), pltpu.VMEM((seq_len, 128), jnp.bfloat16),
                        pltpu.VMEM((seq_len, HEAD_DIM), jnp.bfloat16), pltpu.VMEM((HEAD_DIM, seq_len), jnp.bfloat16),
                        pltpu.VMEM((seq_len, HEAD_DIM), jnp.bfloat16), pltpu.VMEM((seq_len, HEAD_DIM), jnp.bfloat16),
                        pltpu.VMEM((seq_len, HEAD_DIM), jnp.float32), pltpu.VMEM((seq_len, HEAD_DIM), jnp.float32)],
        name="attention_backward",
        cost_estimate=pl.CostEstimate(flops=heads * 5 * 2 * seq_len * 512 * 128, bytes_accessed=inner * seq_len * 16, transcendentals=heads * seq_len * 512),
    )(mixed, mixed, mixed, cosine, sine, qaug, kaug, att, lse, d_att)


EPSILON = 1e-05
GELU_SCALE = 0.7978845608028654
GELU_CUBE = 0.044715
SEGMENTS = 9
GRIDS = {16: (4, 2, 2)}


def row_layout(lengths, pad_count, seq_len, half_dim):
    position = jnp.arange(seq_len, dtype=jnp.int32)
    doc_ends = jnp.cumsum(lengths)
    passed = position[None, :] >= doc_ends[:, None]
    segment = jnp.sum(passed.astype(jnp.int32), axis=0)
    start_at = jnp.sum(jnp.where(passed, lengths[:, None], 0), axis=0)
    pad_start = seq_len - pad_count
    is_live = position < pad_start
    segment = jnp.where(is_live, segment, lengths.shape[0])
    start_at = jnp.where(is_live, start_at, pad_start)
    offset = (position - start_at).astype(jnp.float32)
    frequencies = jnp.exp(-math.log(10000.0) * jnp.arange(half_dim, dtype=jnp.float32) / half_dim)
    angles = frequencies[:, None] * offset[None, :]
    kind = jnp.arange(AUG, dtype=jnp.int32)[:, None]
    same = kind == segment[None, :]
    query_mark = same.astype(jnp.bfloat16)
    key_mark = jnp.where(same | (kind >= SEGMENTS), 0.0, NEGATIVE).astype(jnp.bfloat16)
    return (jnp.cos(angles), jnp.sin(angles), query_mark, key_mark)


def contract(left_side, right_side, left_dim, right_dim):
    return lax.dot_general(
        left_side, right_side, (((left_dim,), (right_dim,)), ((), ())), preferred_element_type=jnp.float32
    )


def low_add(one, other):
    return (one.astype(jnp.float32) + other.astype(jnp.float32)).astype(jnp.bfloat16)


def total_of(refs):
    value = refs[0][...].astype(jnp.float32)
    for ref in refs[1:]:
        value = value + ref[...].astype(jnp.float32)
    return value


def whiten(values):
    centred = values - jnp.mean(values, axis=-1, keepdims=True)
    scale = lax.rsqrt(jnp.mean(centred * centred, axis=-1, keepdims=True) + EPSILON)
    return centred * scale, scale


def whiten_back(white, scale, gain, grad):
    weighted = grad * gain
    return (
        weighted
        - jnp.mean(weighted, axis=-1, keepdims=True)
        - white * jnp.mean(weighted * white, axis=-1, keepdims=True)
    ) * scale


def collect(ref, row, white, grad):
    gain_part = jnp.sum(grad * white, axis=0, keepdims=True)
    bias_part = jnp.sum(grad, axis=0, keepdims=True)

    @pl.when(pl.program_id(0) == 0)
    def _():
        ref[row:row + 1, :] = gain_part
        ref[row + 1:row + 2, :] = bias_part

    @pl.when(pl.program_id(0) != 0)
    def _():
        ref[row:row + 1, :] += gain_part
        ref[row + 1:row + 2, :] += bias_part


def first_kernel(gain, bias, x, normed):
    white, _ = whiten(x[...].astype(jnp.float32))
    normed[...] = (white * gain[0:1] + bias[0:1]).astype(jnp.bfloat16)


def middle_kernel(gain, bias, x, *refs):
    *parts, middle, mlp = refs
    white, _ = whiten(total_of(parts))
    rows = x[...].astype(jnp.float32) + white * gain[1:2] + bias[1:2]
    middle[...] = rows
    white, _ = whiten(rows)
    mlp[...] = (white * gain[2:3] + bias[2:3]).astype(jnp.bfloat16)


def finish_kernel(gain, bias, middle, cot, *refs):
    *parts, out, d_mlp, sums = refs
    white, scale = whiten(total_of(parts))
    out[...] = (middle[...] + white * gain[3:4] + bias[3:4]).astype(jnp.bfloat16)
    grad = cot[...].astype(jnp.float32)
    d_mlp[...] = whiten_back(white, scale, gain[3:4], grad).astype(jnp.bfloat16)
    collect(sums, 0, white, grad)


def middle_back_kernel(count, gain, bias, middle, cot, *refs):
    att_parts, parts = refs[:count], refs[count:2 * count]
    d_middle, d_att, sums = refs[2 * count:]
    grad = total_of(parts)
    white, scale = whiten(middle[...])
    collect(sums, 2, white, grad)
    grad = cot[...].astype(jnp.float32) + whiten_back(white, scale, gain[2:3], grad)
    d_middle[...] = grad
    white, scale = whiten(total_of(att_parts))
    collect(sums, 0, white, grad)
    d_att[...] = whiten_back(white, scale, gain[1:2], grad).astype(jnp.bfloat16)


def first_back_kernel(gain, bias, x, d_middle, *refs):
    *parts, out, sums = refs
    grad = total_of(parts)
    white, scale = whiten(x[...].astype(jnp.float32))
    collect(sums, 0, white, grad)
    out[...] = (d_middle[...] + whiten_back(white, scale, gain[0:1], grad)).astype(jnp.bfloat16)


def rowwise(kernel, name, gain, bias, inputs, out_types, sum_rows=0):
    rows, width = inputs[0].shape
    block = 128
    spec = pl.BlockSpec((block, width), lambda i: (i, 0))
    fixed = pl.BlockSpec(gain.shape, lambda i: (0, 0))
    out_specs = [spec] * len(out_types)
    out_shape = [jax.ShapeDtypeStruct((rows, width), t) for t in out_types]
    if sum_rows:
        out_specs.append(pl.BlockSpec((sum_rows, width), lambda i: (0, 0)))
        out_shape.append(jax.ShapeDtypeStruct((sum_rows, width), jnp.float32))
    moved = sum(a.size * a.dtype.itemsize for a in inputs) + sum(rows * width * jnp.dtype(t).itemsize for t in out_types)
    return pl.pallas_call(
        kernel,
        grid=(rows // block,),
        in_specs=[fixed, fixed] + [spec] * len(inputs),
        out_specs=out_specs,
        out_shape=out_shape,
        name=name,
        cost_estimate=pl.CostEstimate(flops=rows * width * 20, bytes_accessed=moved, transcendentals=0),
    )(gain, bias, *inputs)


class Grid:
    def __init__(self, sizes):
        count = math.prod(sizes)
        x_size, y_size = sizes[2], sizes[1]
        plane = x_size * y_size
        index = lax.axis_index("dp")
        self.x = ([(i, i ^ 1) for i in range(count)], index % x_size)
        self.y = ([(i, i ^ x_size) for i in range(count)], (index // x_size) % y_size)
        layer = lambda i: i // plane
        place = index // plane
        self.near = ([(i, i ^ plane) for i in range(count)], place % 2)
        self.far = ([(i, i ^ (2 * plane)) for i in range(count)], place // 2)

    def small(self, values):
        for pairs, _ in (self.x, self.y, self.near, self.far):
            received = yield [(values, pairs)]
            values = low_add(values, received[0])
        return values

    def colour(self, values, order):
        for pairs, bit in order:
            half = values.shape[0] // 2
            send = lax.dynamic_slice_in_dim(values, (1 - bit) * half, half, 0)
            keep = lax.dynamic_slice_in_dim(values, bit * half, half, 0)
            received = yield [(send, pairs)]
            values = low_add(keep, received[0])
        for pairs, bit in order[:0:-1]:
            received = yield [(values, pairs)]
            other = received[0]
            values = jnp.concatenate([jnp.where(bit == 0, values, other), jnp.where(bit == 0, other, values)], axis=0)
        pairs, bit = order[0]
        received = yield [(values, pairs)]
        return values, received[0], bit

    def large(self, values):
        half = values.shape[0] // 2
        first = self.colour(values[:half], (self.x, self.y, self.near, self.far))
        second = self.colour(values[half:], (self.y, self.x, self.near, self.far))
        return both(first, second)


def both(first, second):
    one, two = next(first), next(second)
    while True:
        received = yield one + two
        ends = []
        try:
            one_next = first.send(received[:len(one)])
        except StopIteration as stop:
            ends.append(stop.value)
        try:
            two_next = second.send(received[len(one):])
        except StopIteration as stop:
            ends.append(stop.value)
        if ends:
            return ends
        one, two = one_next, two_next


class Flows:
    def __init__(self):
        self.active = []
        self.results = {}

    def launch(self, name, flow, chain):
        return self.post([(name, flow, next(flow))], chain)

    def post(self, entries, chain):
        sends = [[value for value, _ in wanted] for _, _, wanted in entries]
        chain, sends = lax.optimization_barrier((chain, sends))
        for (name, flow, wanted), values in zip(entries, sends):
            flight = [lax.ppermute(value, "dp", pairs) for value, (_, pairs) in zip(values, wanted)]
            self.active.append((name, flow, flight))
        return chain

    def step(self, chain, names=None):
        chosen = [entry for entry in self.active if names is None or entry[0] in names]
        self.active = [entry for entry in self.active if names is not None and entry[0] not in names]
        chain, flights = lax.optimization_barrier((chain, [flight for _, _, flight in chosen]))
        entries = []
        for (name, flow, _), flight in zip(chosen, flights):
            try:
                entries.append((name, flow, flow.send(flight)))
            except StopIteration as stop:
                self.results[name] = stop.value
        return self.post(entries, chain) if entries else chain


def place_kernel(slot_ref, piece, *refs):
    refs[-1][0] = piece[...].astype(jnp.float32)


def place(slot, piece, base):
    rows, width = piece.shape
    blocks = 2
    operands, in_specs, aliases = [piece], [pl.BlockSpec((rows // blocks, width), lambda i, s: (i, 0))], {}
    if base is not None:
        operands.append(base)
        in_specs.append(pl.BlockSpec(memory_space=pl.ANY))
        aliases = {2: 0}
    return pl.pallas_call(
        place_kernel,
        grid_spec=pltpu.PrefetchScalarGridSpec(
            num_scalar_prefetch=1,
            grid=(blocks,),
            in_specs=in_specs,
            out_specs=pl.BlockSpec((1, rows // blocks, width), lambda i, s: (s[0], i, 0)),
        ),
        out_shape=jax.ShapeDtypeStruct((4, rows, width), jnp.float32),
        input_output_aliases=aliases,
        name="place",
        cost_estimate=pl.CostEstimate(flops=0, bytes_accessed=rows * width * 6, transcendentals=0),
    )(slot.reshape(1).astype(jnp.int32), *operands)


def assembled(ends):
    out = None
    for which in (0, 1):
        for colour, (own, other, bit) in enumerate(ends):
            slot = 2 * colour + (bit if which == 0 else 1 - bit)
            out = place(slot, own if which == 0 else other, out)
    return out.reshape((-1,) + out.shape[2:])


def make_body(sizes):
    mp_size = sizes["mp"]
    grid_sizes = GRIDS.get(sizes["dp"])

    def pair_parts(partial_sum):
        low_part = partial_sum.astype(jnp.bfloat16)
        if mp_size == 2:
            return [low_part, lax.ppermute(low_part, "mp", [(0, 1), (1, 0)])]
        return [lax.psum(low_part, "mp")]

    def plain_sum(values):
        return lax.psum(values.astype(jnp.bfloat16), "dp").astype(jnp.float32)

    def body(tokens, doc_lengths, pad_counts, gain, bias, qkv_weight, out_weight, up_weight, down_weight, cotangent):
        row_count, seq_len, width = tokens.shape
        count = row_count * seq_len
        inner = qkv_weight.shape[2]
        layouts = [row_layout(doc_lengths[r], pad_counts[r], seq_len, HEAD_DIM // 2) for r in range(row_count)]
        rows_of = [slice(r * seq_len, (r + 1) * seq_len) for r in range(row_count)]
        low, wide = jnp.bfloat16, jnp.float32
        x = tokens.reshape(count, width)
        cot = cotangent.reshape(count, width)
        qkv = jnp.transpose(qkv_weight, (1, 0, 2))

        normed = rowwise(first_kernel, "first_norm", gain, bias, [x], [low])[0]
        mixed = jnp.stack([contract(qkv[c], normed, 0, 1).astype(low) for c in range(3)])
        forward = [attention_forward(mixed[:, :, s], *layout) for s, layout in zip(rows_of, layouts)]
        att = jnp.concatenate([f[0] for f in forward], axis=1)
        att_parts = pair_parts(contract(att, out_weight, 0, 0))
        middle, mlp = rowwise(middle_kernel, "middle_norms", gain, bias, [x] + att_parts, [wide, low])
        hidden = contract(mlp, up_weight, 1, 0)
        squared = hidden * hidden
        curve = jnp.tanh(GELU_SCALE * hidden * (1.0 + GELU_CUBE * squared))
        act = (0.5 * hidden * (1.0 + curve)).astype(low)
        slope = 0.5 * (1.0 + curve) + 0.5 * GELU_SCALE * hidden * (1.0 - curve * curve) * (
            1.0 + 3.0 * GELU_CUBE * squared
        )
        slope = slope.astype(low)
        mlp_parts = pair_parts(contract(act, down_weight, 1, 0))
        out_tokens, d_mlp, last_sums = rowwise(
            finish_kernel, "finish_norm", gain, bias, [middle, cot] + mlp_parts, [low, low], 2
        )
        down_grad = contract(act, d_mlp, 0, 0).astype(low)
        down_sum = plain_sum(down_grad)
        d_mlp, _ = lax.optimization_barrier((d_mlp, down_grad))
        d_hidden = (contract(d_mlp, down_weight, 1, 1) * slope.astype(wide)).astype(low)
        up_grad = contract(mlp, d_hidden, 0, 0).astype(low)
        grid = Grid(grid_sizes) if grid_sizes else None
        flows = Flows()

        def launch(name, values, chain, kind):
            return flows.launch(name, getattr(grid, kind)(values), chain) if grid else chain

        def step(chain, names=None):
            return flows.step(chain, names) if flows.active else chain

        d_hidden = launch("up", up_grad, d_hidden, "large")
        d_mlp_parts = pair_parts(contract(d_hidden, up_weight, 1, 1))
        d_middle, d_att, middle_sums = rowwise(
            functools.partial(middle_back_kernel, len(att_parts)),
            "middle_back",
            gain,
            bias,
            [middle, cot] + att_parts + d_mlp_parts,
            [wide, low],
            4,
        )
        out_grad = contract(att, d_att, 1, 0).astype(low)
        d_attended = contract(out_weight, d_att, 1, 1).astype(low)
        d_attended = step(d_attended)
        d_attended = launch("out", out_grad, d_attended, "small")
        d_mixed = [
            attention_backward(mixed[:, :, s], *layout, f[0], f[1], d_attended[:, s])
            for s, layout, f in zip(rows_of, layouts, forward)
        ]
        d_mixed = jnp.concatenate(d_mixed, axis=2)
        d_mixed = step(d_mixed)
        qkv_grad = jnp.concatenate([contract(normed, d_mixed[c], 0, 1).astype(low) for c in range(3)], axis=0)
        d_mixed = launch("qkv", qkv_grad, d_mixed, "large")
        d_normed = sum(contract(d_mixed[c], qkv[c], 0, 1) for c in range(3))
        d_normed_parts = pair_parts(d_normed)
        d_middle = step(d_middle, ("up", "out"))
        input_grad, first_sums = rowwise(
            first_back_kernel, "first_back", gain, bias, [x, d_middle] + d_normed_parts, [low], 2
        )
        sums = jnp.concatenate([first_sums, middle_sums, last_sums], axis=0)
        if grid is None:
            qkv_sum, out_sum, up_sum, sums = plain_sum(qkv_grad), plain_sum(out_grad), plain_sum(up_grad), plain_sum(sums)
        else:
            sums = launch("sums", sums.astype(low), sums, "small")
            while flows.active:
                sums = flows.step(sums)
            qkv_sum, up_sum = assembled(flows.results["qkv"]), assembled(flows.results["up"])
            out_sum, sums = flows.results["out"].astype(wide), flows.results["sums"].astype(wide)
        qkv_sum = jnp.transpose(qkv_sum.reshape(3, width, inner), (1, 0, 2))
        return (
            out_tokens.reshape(tokens.shape),
            input_grad.reshape(tokens.shape),
            sums[0::2],
            sums[1::2],
            qkv_sum,
            out_sum,
            up_sum,
            down_sum,
        )

    return body


def solution(mesh):
    in_specs = (
        P("dp", None, None),
        P("dp", None),
        P("dp"),
        P(),
        P(),
        P(None, None, "mp"),
        P("mp", None),
        P(None, "mp"),
        P("mp", None),
        P("dp", None, None),
    )
    out_specs = (
        P("dp", None, None),
        P("dp", None, None),
        P(),
        P(),
        P(None, None, "mp"),
        P("mp", None),
        P(None, "mp"),
        P("mp", None),
    )
    return jax.shard_map(make_body(dict(mesh.shape)), mesh=mesh, in_specs=in_specs, out_specs=out_specs, check_vma=False)
```

time: 511 us -> 595 us (1.16)
  the two profiles are of different devices: /device:TPU:8 before, /device:TPU:0 now
where the time goes in v2:
time: 595 us; the launch traced here: 585 us
  waiting for transfers between devices  283 us (48%)
  Pallas kernels  99.3 us (17%)
  matrix products  70.7 us (12%)
  starting transfers between devices  54.2 us (9%)
  other arithmetic  44.2 us (7%)
  local copies, waits for them, and re-layouts  17.6 us (3%)
  between operations  16.1 us (3%)
    ppermute x40, waiting for transfers between devices, post(): lax.ppermute(value, 'dp', pairs)  165 us
    psum x1, waiting for transfers between devices, plain_sum(): return lax.psum(values.astype(jnp.bfloat16), 'dp').astype(jnp.float32)  110 us
    dot_general x18, matrix products, contract(): lax.dot_general(left_side, right_side, (((left_dim,), (right_dim,)), ((),...  70.7 us
    ppermute x40, starting transfers between devices, post(): lax.ppermute(value, 'dp', pairs)  52.7 us
    pallas_call x5, Pallas kernels, rowwise(): pl.pallas_call(kernel, grid=(rows // block,), in_specs=[fixed, fixed] + [...  45.8 us
    pallas_call x1, Pallas kernels, attention_backward(): pl.pallas_call(bwd_kernel, grid=(heads,), in_specs=common_specs(seq_len)...  21 us
    pallas_call x8, Pallas kernels, place(): pl.pallas_call(place_kernel, grid_spec=pltpu.PrefetchScalarGridSpec(num_s...  18.6 us
    convert_element_type x21, other arithmetic, low_add(): (one.astype(jnp.float32) + other.astype(jnp.float32)).astype(jnp.bfloat16)  17.9 us
  transfers between devices with their start and end apart: 45, of which 24 were waited for; matrix products, arithmetic and copies ran while one was open for 4% of the time, Pallas kernels for 10%

profile of v2, /device:TPU:0, one launch (start us, length us, event | category | flops | bytes accessed | tf_op | source)
XLA Modules:
  0.0 585.4 jit_solution(7523602213360834411)
XLA Ops:
  7.2 6.6 %first_norm.1 = bf16[1024,1024]{1,0:T(8,128)(2,1)} custom-call(f32[4,1024]{1,0:T(4,128)} %gain.9, f32[4,1024]{1,0:T(4,128)} %bias.9, bf16[1024,1024]{1,0:T(8,128)(2,1)} %bitcast.85), custom_call_target="tpu_custom_call" | custom-call | flops 20971520 | bytes 4194304 | tf_op jit(solution)/shard_map/first_norm/pallas_call | solution.py:281
  13.9 3.3 fusion.1
  24.4 3.2 pad_maximum_fusion.q_ref.k_ref.v_ref
  27.6 13.8 %attention_forward.1 = (bf16[512,1024]{1,0:T(8,128)(2,1)}, f32[8,1,1024]{2,1,0:T(1,128)}) custom-call(bf16[3,512,1024]{2,1,0:T(8,128)(2,1)} %pad_maximum_fusion.q_ref.k_ref.v_ref, bf16[3,512,1024]{2,1,0:T(8,128)(2,1)} %pad_maximum_fusion.q_ref.k_ref.v_ref, bf16[3,512,1024]{2,1,0:T(8,128)(2,1)} %pad_maximum_fusion.q_ref.k_ref.v_ref, ...), custom_call_target="tpu_custom_call" | custom-call | flops 2147483648 | bytes 4194304 | tf_op jit(solution)/shard_map/attention_forward/pallas_call | solution.py:120
  41.5 2.5 convolution_convert_fusion.4.refs_0_
  44.6 3.9 collective-permute-done.refs_1_
  48.5 8.1 %middle_norms.1 = (f32[1024,1024]{1,0:T(8,128)}, bf16[1024,1024]{1,0:T(8,128)(2,1)}) custom-call(f32[4,1024]{1,0:T(4,128)} %gain.9, f32[4,1024]{1,0:T(4,128)} %bias.9, bf16[1024,1024]{1,0:T(8,128)(2,1)} %bitcast.86, bf16[1024,1024]{1,0:T(8,128)(2,1)} %copy-done.2, bf16[1024,1024]{1,0:T(8,128)(2,1)} %collective-permute-done.refs_1_), custom_call_target="tpu_custom_call" | custom-call | flops 20971520 | bytes 12582912 | tf_op jit(solution)/shard_map/middle_norms/pallas_call | solution.py:281
  56.6 7.1 %fusion.30 = f32[1024,2048]{1,0:T(8,128)S(1)} fusion(bf16[1024,1024]{1,0:T(8,128)(2,1)} %get-tuple-element.113, bf16[1024,2048]{1,0:T(8,128)(2,1)} %param.17), kind=kOutput, calls=%fused_computation.146 | convolution fusion | flops 4294967296 | bytes 14680064 | tf_op jit(solution)/shard_map/dot_general | solution.py:180
  63.7 5.4 convolution_convert_fusion.3.refs_0_
  69.6 3.9 collective-permute-done.1.refs_1_
  73.5 9.9 %finish_norm.1 = (bf16[1024,1024]{1,0:T(8,128)(2,1)}, bf16[1024,1024]{1,0:T(8,128)(2,1)}, f32[2,1024]{1,0:T(2,128)}) custom-call(f32[4,1024]{1,0:T(4,128)} %gain.9, f32[4,1024]{1,0:T(4,128)} %bias.9, f32[1024,1024]{1,0:T(8,128)} %get-tuple-element.112.middle, bf16[1024,1024]{1,0:T(8,128)(2,1)} %bitcast.88, bf16[1024,1024]{1,0:T(8,128)(2,1)} %copy-done.19, ...), custom_call_target="tpu_custom_call" | custom-call | flops 20971520 | bytes 14680064 | tf_op jit(solution)/shard_map/finish_norm/pallas_call | solution.py:281
  83.4 12.1 %convolution_convert_fusion.1 = bf16[2048,1024]{1,0:T(8,128)(2,1)} fusion(bf16[1024,1024]{1,0:T(8,128)(2,1)} %get-tuple-element.116, f32[1024,2048]{1,0:T(8,128)} %copy-done.46), kind=kOutput, calls=%fused_computation.7 | convolution fusion | flops 4315938816 | bytes 14680064 | tf_op jit(solution)/shard_map/dot_general | solution.py:180
  95.4 11.5 %multiply_convert_fusion = bf16[1024,2048]{1,0:T(8,128)(2,1)S(1)} fusion(f32[1024,2048]{1,0:T(8,128)} %copy-done.46, bf16[1024,1024]{1,0:T(8,128)(2,1)S(1)} %copy-done.44, bf16[2048,1024]{1,0:T(8,128)(2,1)} %param.18), kind=kOutput, calls=%fused_computation | convolution fusion | flops 4334813184 | bytes 18874368 | tf_op jit(solution)/shard_map/dot_general | solution.py:180
  107.0 4.9 convolution_convert_fusion
  115.9 5.9 %convolution_convert_fusion.2.refs_2_ = bf16[1024,1024]{1,0:T(8,128)(2,1)} fusion(bf16[1024,2048]{1,0:T(8,128)(2,1)S(1)} %multiply_convert_fusion, bf16[1024,2048]{1,0:T(8,128)(2,1)S(1)} %copy-done.42), kind=kOutput, calls=%fused_computation.15 | convolution fusion | flops 4296015872 | bytes 10485760 | tf_op jit(solution)/shard_map/dot_general | solution.py:180
  122.2 2.6 collective-permute-start.3
  126.3 11.9 %middle_back.1 = (f32[1024,1024]{1,0:T(8,128)}, bf16[1024,1024]{1,0:T(8,128)(2,1)}, f32[4,1024]{1,0:T(4,128)}) custom-call(f32[4,1024]{1,0:T(4,128)} %gain.9, f32[4,1024]{1,0:T(4,128)} %bias.9, f32[1024,1024]{1,0:T(8,128)} %get-tuple-element.112.middle, bf16[1024,1024]{1,0:T(8,128)(2,1)} %bitcast.89, bf16[1024,1024]{1,0:T(8,128)(2,1)} %copy-done.2, ...), custom_call_target="tpu_custom_call" | custom-call | flops 20971520 | bytes 20971520 | tf_op jit(solution)/shard_map/middle_back/pallas_call | solution.py:281
  138.3 4.3 convolution_convert_fusion.8
  144.9 3.9 collective-permute-done.3
  159.8 21.0 %attention_backward.1 = bf16[3,512,1024]{2,1,0:T(8,128)(2,1)} custom-call(bf16[3,512,1024]{2,1,0:T(8,128)(2,1)} %pad_maximum_fusion.q_ref.k_ref.v_ref, bf16[3,512,1024]{2,1,0:T(8,128)(2,1)} %pad_maximum_fusion.q_ref.k_ref.v_ref, bf16[3,512,1024]{2,1,0:T(8,128)(2,1)} %pad_maximum_fusion.q_ref.k_ref.v_ref, f32[32,1024]{1,0:T(8,128)} %get-tuple-element.247.cos_ref, ...), custom_call_target="tpu_custom_call" | custom-call | flops 5368709120 | bytes 8388608 | tf_op jit(solution)/shard_map/attention_backward/pallas_call | solution.py:137
  180.8 11.1 %collective-permute-done.6 = bf16[128,2048]{1,0:T(8,128)(2,1)S(1)} collective-permute-done((bf16[128,2048]{1,0:T(8,128)(2,1)}, bf16[128,2048]{1,0:T(8,128)(2,1)S(1)}, u32[]{:S(2)}, u32[]{:S(2)}) %collective-permute-start.6) | collective-permute-done | bytes 524320 | tf_op jit(solution)/shard_map/ppermute | solution.py:363
  197.9 3.4 fusion.23
  209.0 4.4 collective-permute-done.8
  213.4 2.8 collective-permute-done.9
  216.2 8.5 %collective-permute-done.10 = bf16[512,1024]{1,0:T(8,128)(2,1)S(1)} collective-permute-done((bf16[512,1024]{1,0:T(8,128)(2,1)S(1)}, bf16[512,1024]{1,0:T(8,128)(2,1)S(1)}, u32[]{:S(2)}, u32[]{:S(2)}) %collective-permute-start.10) | collective-permute-done | bytes 1048608 | tf_op jit(solution)/shard_map/ppermute | solution.py:363
  229.9 2.8 collective-permute-start.14
  234.4 9.2 %first_back.1 = (bf16[1024,1024]{1,0:T(8,128)(2,1)}, f32[2,1024]{1,0:T(2,128)}) custom-call(f32[4,1024]{1,0:T(4,128)} %gain.9, f32[4,1024]{1,0:T(4,128)} %bias.9, bf16[1024,1024]{1,0:T(8,128)(2,1)} %bitcast.87, f32[1024,1024]{1,0:T(8,128)} %get-tuple-element.142.d_middle, bf16[1024,1024]{1,0:T(8,128)(2,1)} %copy-done.5, bf16[1024,1024]{1,0:T(8,128)(2,1)} %copy-done.20), custom_call_target="tpu_custom_call" | custom-call | flops 20971520 | bytes 12582912 | tf_op jit(solution)/shard_map/first_back/pallas_call | solution.py:281
  246.0 6.2 %collective-permute-done.14 = bf16[32,2048]{1,0:T(8,128)(2,1)} collective-permute-done((bf16[32,2048]{1,0:T(8,128)(2,1)}, bf16[32,2048]{1,0:T(8,128)(2,1)}, u32[]{:S(2)}, u32[]{:S(2)}) %collective-permute-start.14) | collective-permute-done | bytes 131104 | tf_op jit(solution)/shard_map/ppermute | solution.py:363
  258.8 3.6 add_convert_fusion.8
  264.2 2.5 collective-permute-start.22
  270.3 4.5 collective-permute-done.23
  275.3 43.8 %collective-permute-done.20 = bf16[32,2048]{1,0:T(8,128)(2,1)S(1)} collective-permute-done((bf16[32,2048]{1,0:T(8,128)(2,1)S(1)}, bf16[32,2048]{1,0:T(8,128)(2,1)S(1)}, u32[]{:S(2)}, u32[]{:S(2)}) %collective-permute-start.20) | collective-permute-done | bytes 131104 | tf_op jit(solution)/shard_map/ppermute | solution.py:363
  330.5 16.8 %collective-permute-done.28 = bf16[8,1024]{1,0:T(8,128)(2,1)S(1)} collective-permute-done((bf16[8,1024]{1,0:T(8,128)(2,1)S(1)}, bf16[8,1024]{1,0:T(8,128)(2,1)S(1)}, u32[]{:S(2)}, u32[]{:S(2)}) %collective-permute-start.28) | collective-permute-done | bytes 16416 | tf_op jit(solution)/shard_map/ppermute | solution.py:363
  356.8 3.4 collective-permute-start.29
  360.2 2.9 collective-permute-start.33
  363.1 6.3 %collective-permute-done.33 = bf16[8,1024]{1,0:T(8,128)(2,1)S(1)} collective-permute-done((bf16[8,1024]{1,0:T(8,128)(2,1)S(1)}, bf16[8,1024]{1,0:T(8,128)(2,1)S(1)}, u32[]{:S(2)}, u32[]{:S(2)}) %collective-permute-start.33) | collective-permute-done | bytes 16416 | tf_op jit(solution)/shard_map/ppermute | solution.py:363
  374.8 4.9 collective-permute-start.34
  379.8 14.1 %collective-permute-done.34 = bf16[96,512]{1,0:T(8,128)(2,1)S(1)} collective-permute-done((bf16[96,512]{1,0:T(8,128)(2,1)S(1)}, bf16[96,512]{1,0:T(8,128)(2,1)S(1)}, u32[]{:S(2)}, u32[]{:S(2)}) %collective-permute-start.34) | collective-permute-done | bytes 98336 | tf_op jit(solution)/shard_map/ppermute | solution.py:363
  393.9 5.4 collective-permute-done.35
  399.4 4.0 collective-permute-done.36.piece
  406.5 10.1 %collective-permute-done.38 = bf16[192,512]{1,0:T(8,128)(2,1)S(1)} collective-permute-done((bf16[192,512]{1,0:T(8,128)(2,1)S(1)}, bf16[192,512]{1,0:T(8,128)(2,1)S(1)}, u32[]{:S(2)}, u32[]{:S(2)}) %collective-permute-start.38) | collective-permute-done | bytes 196640 | tf_op jit(solution)/shard_map/ppermute | solution.py:363
  416.7 4.0 collective-permute-done.39
  423.5 13.6 %collective-permute-done.40 = bf16[384,512]{1,0:T(8,128)(2,1)S(1)} collective-permute-done((bf16[384,512]{1,0:T(8,128)(2,1)S(1)}, bf16[384,512]{1,0:T(8,128)(2,1)S(1)}, u32[]{:S(2)}, u32[]{:S(2)}) %collective-permute-start.40) | collective-permute-done | bytes 393248 | tf_op jit(solution)/shard_map/ppermute | solution.py:363
  439.7 110.1 %all-reduce.2.cloned.1.call-done = bf16[2048,1024]{1,0:T(8,128)(2,1)} async-done(((bf16[2048,1024]{1,0:T(8,128)(2,1)}), bf16[2048,1024]{1,0:T(8,128)(2,1)}) %all-reduce.2.cloned.1.call-update) | async-done | bytes 4194320 | tf_op jit(solution)/shard_map/psum | solution.py:427
  549.8 6.7 %convert_element_type.411 = f32[2048,1024]{1,0:T(8,128)} convert(bf16[2048,1024]{1,0:T(8,128)(2,1)} %all-reduce.2.cloned.1.call-done) | non-fusion elementwise | flops 2097152 | bytes 12582912 | tf_op jit(solution)/shard_map/convert_element_type | solution.py:427
  559.5 2.4 place.12.refs_0_
  561.9 2.4 place.13.refs_0_
  566.8 2.4 place.15
  (246 shorter events, 110.6 us)
Async XLA Ops:
  7.2 542.6 %all-reduce.2.cloned.1.call-start = ((), (), s32[]{:S(2)}) async-start(), calls=%async_computation | async-start | bytes 8388608 | tf_op jit(solution)/shard_map/psum | solution.py:427
  44.0 4.5 collective-permute-start
  69.1 4.4 collective-permute-start.1
  121.8 4.5 collective-permute-start.2
  122.2 26.6 %collective-permute-start.3 = (bf16[256,2048]{1,0:T(8,128)(2,1)}, bf16[256,2048]{1,0:T(8,128)(2,1)}, u32[]{:S(2)}, u32[]{:S(2)}) collective-permute-start(bf16[256,2048]{1,0:T(8,128)(2,1)} %constant_dynamic-slice_fusion.13), channel_id=1, source_target_pairs={{0,2},{2,0},{4,6},{6,4},{8,10},{10,8},{12,14},{14,12},{16,18},{18,... | collective-permute-start | bytes 3145736 | tf_op jit(solution)/shard_map/ppermute | solution.py:363
  124.8 25.5 %collective-permute-start.4 = (bf16[256,2048]{1,0:T(8,128)(2,1)}, bf16[256,2048]{1,0:T(8,128)(2,1)}, u32[]{:S(2)}, u32[]{:S(2)}) collective-permute-start(bf16[256,2048]{1,0:T(8,128)(2,1)} %constant_dynamic-slice_fusion.12), channel_id=1, source_target_pairs={{0,4},{2,6},{4,0},{6,2},{8,12},{10,14},{12,8},{14,10},{16,20},{18,... | collective-permute-start | bytes 3145736 | tf_op jit(solution)/shard_map/ppermute | solution.py:363
  156.2 35.7 %collective-permute-start.7 = (bf16[512,1024]{1,0:T(8,128)(2,1)}, bf16[512,1024]{1,0:T(8,128)(2,1)S(1)}, u32[]{:S(2)}, u32[]{:S(2)}) collective-permute-start(bf16[512,1024]{1,0:T(8,128)(2,1)} %convolution_convert_fusion.8), channel_id=1, source_target_pairs={{0,2},{2,0},{4,6},{6,4},{8,10},{10,8},{12,14},{14,12},{16,18},{18,... | collective-permute-start | bytes 3145736 | tf_op jit(solution)/shard_map/ppermute | solution.py:363
  156.5 24.3 %collective-permute-start.5 = (bf16[128,2048]{1,0:T(8,128)(2,1)}, bf16[128,2048]{1,0:T(8,128)(2,1)S(1)}, u32[]{:S(2)}, u32[]{:S(2)}) collective-permute-start(bf16[128,2048]{1,0:T(8,128)(2,1)} %constant_dynamic-slice_fusion.11), channel_id=1, source_target_pairs={{0,4},{2,6},{4,0},{6,2},{8,12},{10,14},{12,8},{14,10},{16,20},{18,... | collective-permute-start | bytes 1572872 | tf_op jit(solution)/shard_map/ppermute | solution.py:363
  158.3 33.7 %collective-permute-start.6 = (bf16[128,2048]{1,0:T(8,128)(2,1)}, bf16[128,2048]{1,0:T(8,128)(2,1)S(1)}, u32[]{:S(2)}, u32[]{:S(2)}) collective-permute-start(bf16[128,2048]{1,0:T(8,128)(2,1)} %constant_dynamic-slice_fusion.10), channel_id=1, source_target_pairs={{0,2},{2,0},{4,6},{6,4},{8,10},{10,8},{12,14},{14,12},{16,18},{18,... | collective-permute-start | bytes 1572872 | tf_op jit(solution)/shard_map/ppermute | solution.py:363
  201.3 23.4 %collective-permute-start.10 = (bf16[512,1024]{1,0:T(8,128)(2,1)S(1)}, bf16[512,1024]{1,0:T(8,128)(2,1)S(1)}, u32[]{:S(2)}, u32[]{:S(2)}) collective-permute-start(bf16[512,1024]{1,0:T(8,128)(2,1)S(1)} %add_convert_fusion.5), channel_id=1, source_target_pairs={{0,4},{2,6},{4,0},{6,2},{8,12},{10,14},{12,8},{14,10},{16,20},{18,... | collective-permute-start | bytes 3145736 | tf_op jit(solution)/shard_map/ppermute | solution.py:363
  204.2 9.2 %collective-permute-start.8 = (bf16[64,2048]{1,0:T(8,128)(2,1)S(1)}, bf16[64,2048]{1,0:T(8,128)(2,1)S(1)}, u32[]{:S(2)}, u32[]{:S(2)}) collective-permute-start(bf16[64,2048]{1,0:T(8,128)(2,1)S(1)} %constant_dynamic-slice_fusion.9), channel_id=1, source_target_pairs={{0,8},{2,10},{4,12},{6,14},{8,0},{10,2},{12,4},{14,6},{16,24},{18,... | collective-permute-start | bytes 786440 | tf_op jit(solution)/shard_map/ppermute | solution.py:363
  205.8 10.4 %collective-permute-start.9 = (bf16[64,2048]{1,0:T(8,128)(2,1)S(1)}, bf16[64,2048]{1,0:T(8,128)(2,1)S(1)}, u32[]{:S(2)}, u32[]{:S(2)}) collective-permute-start(bf16[64,2048]{1,0:T(8,128)(2,1)S(1)} %constant_dynamic-slice_fusion.8), channel_id=1, source_target_pairs={{0,8},{2,10},{4,12},{6,14},{8,0},{10,2},{12,4},{14,6},{16,24},{18,... | collective-permute-start | bytes 786440 | tf_op jit(solution)/shard_map/ppermute | solution.py:363
  209.0 23.8 %collective-permute-start.11 = (bf16[1024,1024]{1,0:T(8,128)(2,1)S(1)}, bf16[1024,1024]{1,0:T(8,128)(2,1)S(1)}, u32[]{:S(2)}, u32[]{:S(2)}) collective-permute-start(bf16[1024,1024]{1,0:T(8,128)(2,1)S(1)} %add_convert_fusion.1.refs_0_), channel_id=1, source_target_pairs={{0,1},{1,0},{2,3},{3,2},{4,5},{5,4},{6,7},{7,6},{8,9},{9,8},{10,11... | collective-permute-start | bytes 6291464 | tf_op jit(solution)/shard_map/ppermute | solution.py:423
  226.1 28.4 %collective-permute-start.16 = (bf16[512,1024]{1,0:T(8,128)(2,1)S(1)}, bf16[512,1024]{1,0:T(8,128)(2,1)}, u32[]{:S(2)}, u32[]{:S(2)}) collective-permute-start(bf16[512,1024]{1,0:T(8,128)(2,1)S(1)} %add_convert_fusion.4), channel_id=1, source_target_pairs={{0,8},{2,10},{4,12},{6,14},{8,0},{10,2},{12,4},{14,6},{16,24},{18,... | collective-permute-start | bytes 3145736 | tf_op jit(solution)/shard_map/ppermute | solution.py:363
  227.8 17.2 %collective-permute-start.12 = (bf16[768,512]{1,0:T(8,128)(2,1)}, bf16[768,512]{1,0:T(8,128)(2,1)}, u32[]{:S(2)}, u32[]{:S(2)}) collective-permute-start(bf16[768,512]{1,0:T(8,128)(2,1)} %get-tuple-element.150), channel_id=1, source_target_pairs={{0,2},{2,0},{4,6},{6,4},{8,10},{10,8},{12,14},{14,12},{16,18},{18,... | collective-permute-start | bytes 2359304 | tf_op jit(solution)/shard_map/ppermute | solution.py:363
  228.4 17.6 %collective-permute-start.13 = (bf16[768,512]{1,0:T(8,128)(2,1)}, bf16[768,512]{1,0:T(8,128)(2,1)}, u32[]{:S(2)}, u32[]{:S(2)}) collective-permute-start(bf16[768,512]{1,0:T(8,128)(2,1)} %get-tuple-element.151), channel_id=1, source_target_pairs={{0,4},{2,6},{4,0},{6,2},{8,12},{10,14},{12,8},{14,10},{16,20},{18,... | collective-permute-start | bytes 2359304 | tf_op jit(solution)/shard_map/ppermute | solution.py:363
  229.9 22.3 %collective-permute-start.14 = (bf16[32,2048]{1,0:T(8,128)(2,1)}, bf16[32,2048]{1,0:T(8,128)(2,1)}, u32[]{:S(2)}, u32[]{:S(2)}) collective-permute-start(bf16[32,2048]{1,0:T(8,128)(2,1)} %constant_dynamic-slice_fusion.7), channel_id=1, source_target_pairs={{0,16},{2,18},{4,20},{6,22},{8,24},{10,26},{12,28},{14,30},{16,0},... | collective-permute-start | bytes 393224 | tf_op jit(solution)/shard_map/ppermute | solution.py:363
  234.1 19.4 %collective-permute-start.15 = (bf16[32,2048]{1,0:T(8,128)(2,1)S(1)}, bf16[32,2048]{1,0:T(8,128)(2,1)}, u32[]{:S(2)}, u32[]{:S(2)}) collective-permute-start(bf16[32,2048]{1,0:T(8,128)(2,1)S(1)} %constant_dynamic-slice_fusion.6), channel_id=1, source_target_pairs={{0,16},{2,18},{4,20},{6,22},{8,24},{10,26},{12,28},{14,30},{16,0},... | collective-permute-start | bytes 393224 | tf_op jit(solution)/shard_map/ppermute | solution.py:363
  244.9 9.6 %collective-permute-start.17 = (bf16[8,1024]{1,0:T(8,128)(2,1)S(1)}, bf16[8,1024]{1,0:T(8,128)(2,1)S(1)}, u32[]{:S(2)}, u32[]{:S(2)}) collective-permute-start(bf16[8,1024]{1,0:T(8,128)(2,1)S(1)} %fusion.28), channel_id=1, source_target_pairs={{0,2},{2,0},{4,6},{6,4},{8,10},{10,8},{12,14},{14,12},{16,18},{18,... | collective-permute-start | bytes 49160 | tf_op jit(solution)/shard_map/ppermute | solution.py:363
  264.2 56.3 %collective-permute-start.22 = (bf16[512,1024]{1,0:T(8,128)(2,1)S(1)}, bf16[512,1024]{1,0:T(8,128)(2,1)S(1)}, u32[]{:S(2)}, u32[]{:S(2)}) collective-permute-start(bf16[512,1024]{1,0:T(8,128)(2,1)S(1)} %add_convert_fusion.3), channel_id=1, source_target_pairs={{0,16},{2,18},{4,20},{6,22},{8,24},{10,26},{12,28},{14,30},{16,0},... | collective-permute-start | bytes 3145736 | tf_op jit(solution)/shard_map/ppermute | solution.py:363
  266.7 53.9 %collective-permute-start.18 = (bf16[384,512]{1,0:T(8,128)(2,1)}, bf16[384,512]{1,0:T(8,128)(2,1)}, u32[]{:S(2)}, u32[]{:S(2)}) collective-permute-start(bf16[384,512]{1,0:T(8,128)(2,1)} %constant_dynamic-slice_fusion.5), channel_id=1, source_target_pairs={{0,4},{2,6},{4,0},{6,2},{8,12},{10,14},{12,8},{14,10},{16,20},{18,... | collective-permute-start | bytes 1179656 | tf_op jit(solution)/shard_map/ppermute | solution.py:363
  268.2 52.3 %collective-permute-start.19 = (bf16[384,512]{1,0:T(8,128)(2,1)}, bf16[384,512]{1,0:T(8,128)(2,1)}, u32[]{:S(2)}, u32[]{:S(2)}) collective-permute-start(bf16[384,512]{1,0:T(8,128)(2,1)} %constant_dynamic-slice_fusion.4), channel_id=1, source_target_pairs={{0,2},{2,0},{4,6},{6,4},{8,10},{10,8},{12,14},{14,12},{16,18},{18,... | collective-permute-start | bytes 1179656 | tf_op jit(solution)/shard_map/ppermute | solution.py:363
  268.8 6.0 %collective-permute-start.23 = (bf16[8,1024]{1,0:T(8,128)(2,1)S(1)}, bf16[8,1024]{1,0:T(8,128)(2,1)S(1)}, u32[]{:S(2)}, u32[]{:S(2)}) collective-permute-start(bf16[8,1024]{1,0:T(8,128)(2,1)S(1)} %add_convert_fusion.25), channel_id=1, source_target_pairs={{0,4},{2,6},{4,0},{6,2},{8,12},{10,14},{12,8},{14,10},{16,20},{18,... | collective-permute-start | bytes 49160 | tf_op jit(solution)/shard_map/ppermute | solution.py:363
  269.3 49.8 %collective-permute-start.20 = (bf16[32,2048]{1,0:T(8,128)(2,1)S(1)}, bf16[32,2048]{1,0:T(8,128)(2,1)S(1)}, u32[]{:S(2)}, u32[]{:S(2)}) collective-permute-start(bf16[32,2048]{1,0:T(8,128)(2,1)S(1)} %add_convert_fusion.19), channel_id=1, source_target_pairs={{0,16},{2,18},{4,20},{6,22},{8,24},{10,26},{12,28},{14,30},{16,0},... | collective-permute-start | bytes 393224 | tf_op jit(solution)/shard_map/ppermute | solution.py:363
  274.8 45.7 %collective-permute-start.21 = (bf16[32,2048]{1,0:T(8,128)(2,1)S(1)}, bf16[32,2048]{1,0:T(8,128)(2,1)S(1)}, u32[]{:S(2)}, u32[]{:S(2)}) collective-permute-start(bf16[32,2048]{1,0:T(8,128)(2,1)S(1)} %add_convert_fusion.18), channel_id=1, source_target_pairs={{0,16},{2,18},{4,20},{6,22},{8,24},{10,26},{12,28},{14,30},{16,0},... | collective-permute-start | bytes 393224 | tf_op jit(solution)/shard_map/ppermute | solution.py:363
  326.1 21.2 %collective-permute-start.26 = (bf16[64,2048]{1,0:T(8,128)(2,1)S(1)}, bf16[64,2048]{1,0:T(8,128)(2,1)S(1)}, u32[]{:S(2)}, u32[]{:S(2)}) collective-permute-start(bf16[64,2048]{1,0:T(8,128)(2,1)S(1)} %pad_maximum_fusion.9), channel_id=1, source_target_pairs={{0,8},{2,10},{4,12},{6,14},{8,0},{10,2},{12,4},{14,6},{16,24},{18,... | collective-permute-start | bytes 786440 | tf_op jit(solution)/shard_map/ppermute | solution.py:363
  326.4 20.9 %collective-permute-start.27 = (bf16[64,2048]{1,0:T(8,128)(2,1)S(1)}, bf16[64,2048]{1,0:T(8,128)(2,1)S(1)}, u32[]{:S(2)}, u32[]{:S(2)}) collective-permute-start(bf16[64,2048]{1,0:T(8,128)(2,1)S(1)} %pad_maximum_fusion.10), channel_id=1, source_target_pairs={{0,8},{2,10},{4,12},{6,14},{8,0},{10,2},{12,4},{14,6},{16,24},{18,... | collective-permute-start | bytes 786440 | tf_op jit(solution)/shard_map/ppermute | solution.py:363
  328.2 19.1 %collective-permute-start.24 = (bf16[192,512]{1,0:T(8,128)(2,1)}, bf16[192,512]{1,0:T(8,128)(2,1)}, u32[]{:S(2)}, u32[]{:S(2)}) collective-permute-start(bf16[192,512]{1,0:T(8,128)(2,1)} %constant_dynamic-slice_fusion.3), channel_id=1, source_target_pairs={{0,8},{2,10},{4,12},{6,14},{8,0},{10,2},{12,4},{14,6},{16,24},{18,... | collective-permute-start | bytes 589832 | tf_op jit(solution)/shard_map/ppermute | solution.py:363
  328.4 18.9 %collective-permute-start.25 = (bf16[192,512]{1,0:T(8,128)(2,1)}, bf16[192,512]{1,0:T(8,128)(2,1)}, u32[]{:S(2)}, u32[]{:S(2)}) collective-permute-start(bf16[192,512]{1,0:T(8,128)(2,1)} %constant_dynamic-slice_fusion.2), channel_id=1, source_target_pairs={{0,8},{2,10},{4,12},{6,14},{8,0},{10,2},{12,4},{14,6},{16,24},{18,... | collective-permute-start | bytes 589832 | tf_op jit(solution)/shard_map/ppermute | solution.py:363
  330.2 17.1 %collective-permute-start.28 = (bf16[8,1024]{1,0:T(8,128)(2,1)S(1)}, bf16[8,1024]{1,0:T(8,128)(2,1)S(1)}, u32[]{:S(2)}, u32[]{:S(2)}) collective-permute-start(bf16[8,1024]{1,0:T(8,128)(2,1)S(1)} %add_convert_fusion.24), channel_id=1, source_target_pairs={{0,8},{2,10},{4,12},{6,14},{8,0},{10,2},{12,4},{14,6},{16,24},{18,... | collective-permute-start | bytes 49160 | tf_op jit(solution)/shard_map/ppermute | solution.py:363
  354.6 14.8 %collective-permute-start.31 = (bf16[128,2048]{1,0:T(8,128)(2,1)}, bf16[128,2048]{1,0:T(8,128)(2,1)}, u32[]{:S(2)}, u32[]{:S(2)}) collective-permute-start(bf16[128,2048]{1,0:T(8,128)(2,1)} %pad_maximum_fusion.5), channel_id=1, source_target_pairs={{0,4},{2,6},{4,0},{6,2},{8,12},{10,14},{12,8},{14,10},{16,20},{18,... | collective-permute-start | bytes 1572872 | tf_op jit(solution)/shard_map/ppermute | solution.py:363
  356.8 12.6 %collective-permute-start.32 = (bf16[128,2048]{1,0:T(8,128)(2,1)}, bf16[128,2048]{1,0:T(8,128)(2,1)}, u32[]{:S(2)}, u32[]{:S(2)}) collective-permute-start(bf16[128,2048]{1,0:T(8,128)(2,1)} %pad_maximum_fusion.6), channel_id=1, source_target_pairs={{0,2},{2,0},{4,6},{6,4},{8,10},{10,8},{12,14},{14,12},{16,18},{18,... | collective-permute-start | bytes 1572872 | tf_op jit(solution)/shard_map/ppermute | solution.py:363
  356.8 12.6 %collective-permute-start.29 = (bf16[96,512]{1,0:T(8,128)(2,1)S(1)}, bf16[96,512]{1,0:T(8,128)(2,1)S(1)}, u32[]{:S(2)}, u32[]{:S(2)}) collective-permute-start(bf16[96,512]{1,0:T(8,128)(2,1)S(1)} %constant_dynamic-slice_fusion.1), channel_id=1, source_target_pairs={{0,16},{2,18},{4,20},{6,22},{8,24},{10,26},{12,28},{14,30},{16,0},... | collective-permute-start | bytes 294920 | tf_op jit(solution)/shard_map/ppermute | solution.py:363
  360.2 9.3 %collective-permute-start.30 = (bf16[96,512]{1,0:T(8,128)(2,1)S(1)}, bf16[96,512]{1,0:T(8,128)(2,1)S(1)}, u32[]{:S(2)}, u32[]{:S(2)}) collective-permute-start(bf16[96,512]{1,0:T(8,128)(2,1)S(1)} %constant_dynamic-slice_fusion), channel_id=1, source_target_pairs={{0,16},{2,18},{4,20},{6,22},{8,24},{10,26},{12,28},{14,30},{16,0},... | collective-permute-start | bytes 294920 | tf_op jit(solution)/shard_map/ppermute | solution.py:363
  360.2 9.2 %collective-permute-start.33 = (bf16[8,1024]{1,0:T(8,128)(2,1)S(1)}, bf16[8,1024]{1,0:T(8,128)(2,1)S(1)}, u32[]{:S(2)}, u32[]{:S(2)}) collective-permute-start(bf16[8,1024]{1,0:T(8,128)(2,1)S(1)} %add_convert_fusion.23), channel_id=1, source_target_pairs={{0,16},{2,18},{4,20},{6,22},{8,24},{10,26},{12,28},{14,30},{16,0},... | collective-permute-start | bytes 49160 | tf_op jit(solution)/shard_map/ppermute | solution.py:363
  372.6 64.7 %copy-start.7 = (bf16[256,2048]{1,0:T(8,128)(2,1)}, bf16[256,2048]{1,0:T(8,128)(2,1)S(1)}, u32[]{:S(2)}) copy-start(bf16[256,2048]{1,0:T(8,128)(2,1)S(1)} %pad_maximum_fusion.2.piece) | copy-start | bytes 3145732
  372.7 30.7 %collective-permute-start.36 = (bf16[256,2048]{1,0:T(8,128)(2,1)S(1)}, bf16[256,2048]{1,0:T(8,128)(2,1)S(1)}, u32[]{:S(2)}, u32[]{:S(2)}) collective-permute-start(bf16[256,2048]{1,0:T(8,128)(2,1)S(1)} %pad_maximum_fusion.1.piece), channel_id=1, source_target_pairs={{0,2},{2,0},{4,6},{6,4},{8,10},{10,8},{12,14},{14,12},{16,18},{18,... | collective-permute-start | bytes 3145736 | tf_op jit(solution)/shard_map/ppermute | solution.py:363
  374.5 29.8 %collective-permute-start.37 = (bf16[256,2048]{1,0:T(8,128)(2,1)S(1)}, bf16[256,2048]{1,0:T(8,128)(2,1)}, u32[]{:S(2)}, u32[]{:S(2)}) collective-permute-start(bf16[256,2048]{1,0:T(8,128)(2,1)S(1)} %pad_maximum_fusion.2.piece), channel_id=1, source_target_pairs={{0,4},{2,6},{4,0},{6,2},{8,12},{10,14},{12,8},{14,10},{16,20},{18,... | collective-permute-start | bytes 3145736 | tf_op jit(solution)/shard_map/ppermute | solution.py:363
  374.8 19.1 %collective-permute-start.34 = (bf16[96,512]{1,0:T(8,128)(2,1)S(1)}, bf16[96,512]{1,0:T(8,128)(2,1)S(1)}, u32[]{:S(2)}, u32[]{:S(2)}) collective-permute-start(bf16[96,512]{1,0:T(8,128)(2,1)S(1)} %add_convert_fusion.21), channel_id=1, source_target_pairs={{0,16},{2,18},{4,20},{6,22},{8,24},{10,26},{12,28},{14,30},{16,0},... | collective-permute-start | bytes 294920 | tf_op jit(solution)/shard_map/ppermute | solution.py:363
  379.7 19.6 %collective-permute-start.35 = (bf16[96,512]{1,0:T(8,128)(2,1)S(1)}, bf16[96,512]{1,0:T(8,128)(2,1)S(1)}, u32[]{:S(2)}, u32[]{:S(2)}) collective-permute-start(bf16[96,512]{1,0:T(8,128)(2,1)S(1)} %add_convert_fusion.20), channel_id=1, source_target_pairs={{0,16},{2,18},{4,20},{6,22},{8,24},{10,26},{12,28},{14,30},{16,0},... | collective-permute-start | bytes 294920 | tf_op jit(solution)/shard_map/ppermute | solution.py:363
  404.4 12.2 %collective-permute-start.38 = (bf16[192,512]{1,0:T(8,128)(2,1)S(1)}, bf16[192,512]{1,0:T(8,128)(2,1)S(1)}, u32[]{:S(2)}, u32[]{:S(2)}) collective-permute-start(bf16[192,512]{1,0:T(8,128)(2,1)S(1)} %pad_maximum_fusion.11), channel_id=1, source_target_pairs={{0,8},{2,10},{4,12},{6,14},{8,0},{10,2},{12,4},{14,6},{16,24},{18,... | collective-permute-start | bytes 589832 | tf_op jit(solution)/shard_map/ppermute | solution.py:363
  406.4 14.3 %collective-permute-start.39 = (bf16[192,512]{1,0:T(8,128)(2,1)S(1)}, bf16[192,512]{1,0:T(8,128)(2,1)S(1)}, u32[]{:S(2)}, u32[]{:S(2)}) collective-permute-start(bf16[192,512]{1,0:T(8,128)(2,1)S(1)} %pad_maximum_fusion.12), channel_id=1, source_target_pairs={{0,8},{2,10},{4,12},{6,14},{8,0},{10,2},{12,4},{14,6},{16,24},{18,... | collective-permute-start | bytes 589832 | tf_op jit(solution)/shard_map/ppermute | solution.py:363
  420.9 16.2 %collective-permute-start.40 = (bf16[384,512]{1,0:T(8,128)(2,1)S(1)}, bf16[384,512]{1,0:T(8,128)(2,1)S(1)}, u32[]{:S(2)}, u32[]{:S(2)}) collective-permute-start(bf16[384,512]{1,0:T(8,128)(2,1)S(1)} %pad_maximum_fusion.7), channel_id=1, source_target_pairs={{0,4},{2,6},{4,0},{6,2},{8,12},{10,14},{12,8},{14,10},{16,20},{18,... | collective-permute-start | bytes 1179656 | tf_op jit(solution)/shard_map/ppermute | solution.py:363
  421.7 15.4 %collective-permute-start.41 = (bf16[384,512]{1,0:T(8,128)(2,1)S(1)}, bf16[384,512]{1,0:T(8,128)(2,1)S(1)}, u32[]{:S(2)}, u32[]{:S(2)}) collective-permute-start(bf16[384,512]{1,0:T(8,128)(2,1)S(1)} %pad_maximum_fusion.8), channel_id=1, source_target_pairs={{0,2},{2,0},{4,6},{6,4},{8,10},{10,8},{12,14},{14,12},{16,18},{18,... | collective-permute-start | bytes 1179656 | tf_op jit(solution)/shard_map/ppermute | solution.py:363
  437.3 119.2 %copy-start.16 = (bf16[768,512]{1,0:T(8,128)(2,1)}, bf16[768,512]{1,0:T(8,128)(2,1)S(1)}, u32[]{:S(2)}) copy-start(bf16[768,512]{1,0:T(8,128)(2,1)S(1)} %pad_maximum_fusion.3.piece) | copy-start | bytes 2359300
  437.6 119.0 %copy-start.18 = (bf16[768,512]{1,0:T(8,128)(2,1)}, bf16[768,512]{1,0:T(8,128)(2,1)S(1)}, u32[]{:S(2)}) copy-start(bf16[768,512]{1,0:T(8,128)(2,1)S(1)} %pad_maximum_fusion.4.piece) | copy-start | bytes 2359300
  437.6 136.0 %collective-permute-start.42 = (bf16[768,512]{1,0:T(8,128)(2,1)S(1)}, bf16[768,512]{1,0:T(8,128)(2,1)}, u32[]{:S(2)}, u32[]{:S(2)}) collective-permute-start(bf16[768,512]{1,0:T(8,128)(2,1)S(1)} %pad_maximum_fusion.3.piece), channel_id=1, source_target_pairs={{0,2},{2,0},{4,6},{6,4},{8,10},{10,8},{12,14},{14,12},{16,18},{18,... | collective-permute-start | bytes 2359304 | tf_op jit(solution)/shard_map/ppermute | solution.py:363
  439.1 134.5 %collective-permute-start.43 = (bf16[768,512]{1,0:T(8,128)(2,1)S(1)}, bf16[768,512]{1,0:T(8,128)(2,1)}, u32[]{:S(2)}, u32[]{:S(2)}) collective-permute-start(bf16[768,512]{1,0:T(8,128)(2,1)S(1)} %pad_maximum_fusion.4.piece), channel_id=1, source_target_pairs={{0,4},{2,6},{4,0},{6,2},{8,12},{10,14},{12,8},{14,10},{16,20},{18,... | collective-permute-start | bytes 2359304 | tf_op jit(solution)/shard_map/ppermute | solution.py:363
  (44 other events, 368.8 us)
Sparse Core Ops, SparseCore 0:
  363.2 186.5 all-reduce.1

commit v3 on v2

--- a/solution.py
+++ b/solution.py
@@ -106,8 +106,8 @@
     dm_ref[2] = dv_scr[...].T.astype(jnp.bfloat16)
 
 
-def common_specs(seq_len):
-    part = lambda c: pl.BlockSpec((1, HEAD_DIM, seq_len), lambda h: (c, h, 0))
+def common_specs(seq_len, first=0):
+    part = lambda c: pl.BlockSpec((1, HEAD_DIM, seq_len), lambda h: (c, h + first, 0))
     whole = lambda rows: pl.BlockSpec((rows, seq_len), lambda h: (0, 0))
     half = HEAD_DIM // 2
     return [part(0), part(1), part(2), whole(half), whole(half), whole(AUG), whole(AUG)]
@@ -130,23 +130,35 @@
     )(mixed, mixed, mixed, cosine, sine, qaug, kaug)
 
 
-def attention_backward(mixed, cosine, sine, qaug, kaug, att, lse, d_att):
+def attention_backward(mixed, cosine, sine, qaug, kaug, att, lse, d_att, first, heads, base):
     _, inner, seq_len = mixed.shape
-    heads = inner // HEAD_DIM
-    head_spec = pl.BlockSpec((HEAD_DIM, seq_len), lambda h: (h, 0))
+    head_spec = pl.BlockSpec((HEAD_DIM, seq_len), lambda h: (h + first, 0))
+    operands = [mixed, mixed, mixed, cosine, sine, qaug, kaug, att, lse, d_att]
+    in_specs = common_specs(seq_len, first)
+    in_specs += [head_spec, pl.BlockSpec((1, 1, seq_len), lambda h: (h + first, 0, 0)), head_spec]
+    aliases = {}
+    if base is not None:
+        operands.append(base)
+        in_specs.append(pl.BlockSpec(memory_space=pl.ANY))
+        aliases = {10: 0}
     return pl.pallas_call(
-        bwd_kernel,
+        bwd_kernel if base is None else bwd_kernel_onto,
         grid=(heads,),
-        in_specs=common_specs(seq_len) + [head_spec, pl.BlockSpec((1, 1, seq_len), lambda h: (h, 0, 0)), head_spec],
-        out_specs=pl.BlockSpec((3, HEAD_DIM, seq_len), lambda h: (0, h, 0)),
+        in_specs=in_specs,
+        out_specs=pl.BlockSpec((3, HEAD_DIM, seq_len), lambda h: (0, h + first, 0)),
         out_shape=jax.ShapeDtypeStruct(mixed.shape, jnp.bfloat16),
+        input_output_aliases=aliases,
         scratch_shapes=[pltpu.VMEM((128, seq_len), jnp.bfloat16), pltpu.VMEM((seq_len, 128), jnp.bfloat16),
                         pltpu.VMEM((seq_len, HEAD_DIM), jnp.bfloat16), pltpu.VMEM((HEAD_DIM, seq_len), jnp.bfloat16),
                         pltpu.VMEM((seq_len, HEAD_DIM), jnp.bfloat16), pltpu.VMEM((seq_len, HEAD_DIM), jnp.bfloat16),
                         pltpu.VMEM((seq_len, HEAD_DIM), jnp.float32), pltpu.VMEM((seq_len, HEAD_DIM), jnp.float32)],
         name="attention_backward",
-        cost_estimate=pl.CostEstimate(flops=heads * 5 * 2 * seq_len * 512 * 128, bytes_accessed=inner * seq_len * 16, transcendentals=heads * seq_len * 512),
-    )(mixed, mixed, mixed, cosine, sine, qaug, kaug, att, lse, d_att)
+        cost_estimate=pl.CostEstimate(flops=heads * 5 * 2 * seq_len * 512 * 128, bytes_accessed=heads * HEAD_DIM * seq_len * 16, transcendentals=heads * seq_len * 512),
+    )(*operands)
+
+
+def bwd_kernel_onto(*refs):
+    bwd_kernel(*refs[:10], *refs[11:])
 
 
 EPSILON = 1e-05
@@ -269,7 +281,7 @@
 
 def rowwise(kernel, name, gain, bias, inputs, out_types, sum_rows=0):
     rows, width = inputs[0].shape
-    block = 128
+    block = min(256, rows)
     spec = pl.BlockSpec((block, width), lambda i: (i, 0))
     fixed = pl.BlockSpec(gain.shape, lambda i: (0, 0))
     out_specs = [spec] * len(out_types)
@@ -381,7 +393,7 @@
     refs[-1][0] = piece[...].astype(jnp.float32)
 
 
-def place(slot, piece, base):
+def place(slot, piece, slots, base):
     rows, width = piece.shape
     blocks = 2
     operands, in_specs, aliases = [piece], [pl.BlockSpec((rows // blocks, width), lambda i, s: (i, 0))], {}
@@ -397,7 +409,7 @@
             in_specs=in_specs,
             out_specs=pl.BlockSpec((1, rows // blocks, width), lambda i, s: (s[0], i, 0)),
         ),
-        out_shape=jax.ShapeDtypeStruct((4, rows, width), jnp.float32),
+        out_shape=jax.ShapeDtypeStruct((slots, rows, width), jnp.float32),
         input_output_aliases=aliases,
         name="place",
         cost_estimate=pl.CostEstimate(flops=0, bytes_accessed=rows * width * 6, transcendentals=0),
@@ -409,8 +421,16 @@
     for which in (0, 1):
         for colour, (own, other, bit) in enumerate(ends):
             slot = 2 * colour + (bit if which == 0 else 1 - bit)
-            out = place(slot, own if which == 0 else other, out)
+            out = place(slot, own if which == 0 else other, 4, out)
     return out.reshape((-1,) + out.shape[2:])
+
+
+def assembled_last(ends):
+    (own, other, bit), (own_last, other_last, bit_last) = ends
+    out = place(1 - bit, other, 3, place(bit, own, 3, None))
+    third = jnp.where(bit_last == 0, own_last, other_last)
+    rest = jnp.where(bit_last == 0, other_last, own_last)
+    return place(jnp.int32(2), third, 3, out), rest.astype(jnp.float32)
 
 
 def make_body(sizes):
@@ -455,22 +475,22 @@
         out_tokens, d_mlp, last_sums = rowwise(
             finish_kernel, "finish_norm", gain, bias, [middle, cot] + mlp_parts, [low, low], 2
         )
+        grid = Grid(grid_sizes) if grid_sizes else None
+        flows = Flows()
+
+        def launch(name, values, chain, kind):
+            return flows.launch(name, getattr(grid, kind)(values), chain) if grid else chain
+
+        def step(chain, names=None):
+            return flows.step(chain, names) if flows.active else chain
+
         down_grad = contract(act, d_mlp, 0, 0).astype(low)
-        down_sum = plain_sum(down_grad)
-        d_mlp, _ = lax.optimization_barrier((d_mlp, down_grad))
+        d_mlp = launch("down", down_grad, d_mlp, "large")
         d_hidden = (contract(d_mlp, down_weight, 1, 1) * slope.astype(wide)).astype(low)
         up_grad = contract(mlp, d_hidden, 0, 0).astype(low)
-        grid = Grid(grid_sizes) if grid_sizes else None
-        flows = Flows()
-
-        def launch(name, values, chain, kind):
-            return flows.launch(name, getattr(grid, kind)(values), chain) if grid else chain
-
-        def step(chain, names=None):
-            return flows.step(chain, names) if flows.active else chain
-
         d_hidden = launch("up", up_grad, d_hidden, "large")
-        d_mlp_parts = pair_parts(contract(d_hidden, up_weight, 1, 1))
+        d_mlp_norm = step(contract(d_hidden, up_weight, 1, 1).astype(low), ("down",))
+        d_mlp_parts = pair_parts(d_mlp_norm)
         d_middle, d_att, middle_sums = rowwise(
             functools.partial(middle_back_kernel, len(att_parts)),
             "middle_back",
@@ -480,33 +500,48 @@
             [wide, low],
             4,
         )
+        d_attended = step(contract(out_weight, d_att, 1, 1).astype(low))
+        heads = inner // HEAD_DIM
+        early = heads // 2
+        both_kinds = [(0, early), (early, heads - early)] if early else [(0, heads)]
+        d_mixed = [None] * row_count
+        for first, size in both_kinds:
+            for r, (s, layout, f) in enumerate(zip(rows_of, layouts, forward)):
+                d_mixed[r] = attention_backward(
+                    mixed[:, :, s], *layout, f[0], f[1], d_attended[:, s], first, size, d_mixed[r]
+                )
+            d_mixed, d_attended = step((d_mixed, d_attended))
+        d_mixed = jnp.concatenate(d_mixed, axis=2)
+        half = width // 2
+        qkv_grad = [contract(normed, d_mixed[c], 0, 1).astype(low) for c in range(3)]
         out_grad = contract(att, d_att, 1, 0).astype(low)
-        d_attended = contract(out_weight, d_att, 1, 1).astype(low)
-        d_attended = step(d_attended)
-        d_attended = launch("out", out_grad, d_attended, "small")
-        d_mixed = [
-            attention_backward(mixed[:, :, s], *layout, f[0], f[1], d_attended[:, s])
-            for s, layout, f in zip(rows_of, layouts, forward)
-        ]
-        d_mixed = jnp.concatenate(d_mixed, axis=2)
-        d_mixed = step(d_mixed)
-        qkv_grad = jnp.concatenate([contract(normed, d_mixed[c], 0, 1).astype(low) for c in range(3)], axis=0)
-        d_mixed = launch("qkv", qkv_grad, d_mixed, "large")
-        d_normed = sum(contract(d_mixed[c], qkv[c], 0, 1) for c in range(3))
+        if grid:
+            last_grad = jnp.concatenate(qkv_grad + [out_grad[:, :half], out_grad[:, half:]], axis=0)
+            d_mixed = launch("last", last_grad, d_mixed, "large")
+        d_normed = sum(contract(d_mixed[c], qkv[c], 0, 1) for c in range(3)).astype(low)
+        d_normed = step(d_normed, ("down", "up"))
         d_normed_parts = pair_parts(d_normed)
-        d_middle = step(d_middle, ("up", "out"))
         input_grad, first_sums = rowwise(
             first_back_kernel, "first_back", gain, bias, [x, d_middle] + d_normed_parts, [low], 2
         )
         sums = jnp.concatenate([first_sums, middle_sums, last_sums], axis=0)
         if grid is None:
-            qkv_sum, out_sum, up_sum, sums = plain_sum(qkv_grad), plain_sum(out_grad), plain_sum(up_grad), plain_sum(sums)
+            qkv_sum, out_sum = plain_sum(jnp.concatenate(qkv_grad, axis=0)), plain_sum(out_grad)
+            down_sum, up_sum, sums = plain_sum(down_grad), plain_sum(up_grad), plain_sum(sums)
         else:
-            sums = launch("sums", sums.astype(low), sums, "small")
+            kept = [input_grad]
+            kept = launch("sums", sums.astype(low), kept, "small")
+            done = {}
             while flows.active:
-                sums = flows.step(sums)
-            qkv_sum, up_sum = assembled(flows.results["qkv"]), assembled(flows.results["up"])
-            out_sum, sums = flows.results["out"].astype(wide), flows.results["sums"].astype(wide)
+                kept = flows.step(kept)
+                for name, result in flows.results.items():
+                    if name in ("down", "up") and name not in done:
+                        done[name] = len(kept)
+                        kept = kept + [assembled(result)]
+            input_grad, down_sum, up_sum = kept[0], kept[done["down"]], kept[done["up"]]
+            qkv_sum, halves = assembled_last(flows.results["last"])
+            out_sum = jnp.concatenate([halves[:inner], halves[inner:]], axis=1)
+            sums = flows.results["sums"].astype(wide)
         qkv_sum = jnp.transpose(qkv_sum.reshape(3, width, inner), (1, 0, 2))
         return (
             out_tokens.reshape(tokens.shape),

time: 595 us -> 489 us (0.82)
  waiting for transfers between devices: 283 us -> 159 us
  other arithmetic: 44.2 us -> 60.7 us
  between operations: 16.1 us -> 3.14 us
  local copies, waits for them, and re-layouts: 17.6 us -> 25.8 us
  starting transfers between devices: 54.2 us -> 62.4 us
    psum x1 -> x0, waiting for transfers between devices: 110 us -> none  [plain_sum(): return lax.psum(values.astype(jnp.bfloat16), 'dp').astype(jnp.float32)]
    ppermute x40 -> x52, waiting for transfers between devices: 165 us -> 150 us  [post(): lax.ppermute(value, 'dp', pairs)]
    convert_element_type x21 -> x27, other arithmetic: 17.9 us -> 29.3 us  [low_add(): (one.astype(jnp.float32) + other.astype(jnp.float32)).astype(jnp.bfloat16)]
    ppermute x40 -> x52, starting transfers between devices: 52.7 us -> 61.4 us  [post(): lax.ppermute(value, 'dp', pairs)]
    pallas_call x8 -> x11, Pallas kernels: 18.6 us -> 26.8 us  [place(): pl.pallas_call(place_kernel, grid_spec=pltpu.PrefetchScalarGridSpec(num_s...]
    pallas_call x5, Pallas kernels: 45.8 us -> 38.2 us  [rowwise(): pl.pallas_call(kernel, grid=(rows // block,), in_specs=[fixed, fixed] + [...]
    dynamic_slice x14 -> x23, local copies, waits for them, and re-layouts: 7.65 us -> 13.3 us  [colour(): send = lax.dynamic_slice_in_dim(values, (1 - bit) * half, half, 0)]
    pallas_call x1 -> x2, Pallas kernels: 21 us -> 23.2 us  [attention_backward(): pl.pallas_call(bwd_kernel if base is None else bwd_kernel_onto, grid=(hea...]
  transfers between devices with their start and end apart: 45 -> 56, of which waited for: 24 -> 32; matrix products, arithmetic and copies ran while one was open for 4% -> 4% of each run, Pallas kernels for 10% -> 13%
where the time goes in v3:
time: 489 us; the launch traced here: 480 us
  waiting for transfers between devices  159 us (33%)
  Pallas kernels  102 us (21%)
  matrix products  67.3 us (14%)
  starting transfers between devices  62.4 us (13%)
  other arithmetic  60.7 us (12%)
  local copies, waits for them, and re-layouts  25.8 us (5%)
    ppermute x52, waiting for transfers between devices, post(): lax.ppermute(value, 'dp', pairs)  150 us
    dot_general x18, matrix products, contract(): lax.dot_general(left_side, right_side, (((left_dim,), (right_dim,)), ((),...  67.3 us
    ppermute x52, starting transfers between devices, post(): lax.ppermute(value, 'dp', pairs)  61.4 us
    pallas_call x5, Pallas kernels, rowwise(): pl.pallas_call(kernel, grid=(rows // block,), in_specs=[fixed, fixed] + [...  38.2 us
    convert_element_type x27, other arithmetic, low_add(): (one.astype(jnp.float32) + other.astype(jnp.float32)).astype(jnp.bfloat16)  29.3 us
    pallas_call x11, Pallas kernels, place(): pl.pallas_call(place_kernel, grid_spec=pltpu.PrefetchScalarGridSpec(num_s...  26.8 us
    pallas_call x2, Pallas kernels, attention_backward(): pl.pallas_call(bwd_kernel if base is None else bwd_kernel_onto, grid=(hea...  23.2 us
    pallas_call x1, Pallas kernels, attention_forward(): pl.pallas_call(fwd_kernel, grid=(heads,), in_specs=common_specs(seq_len),...  13.8 us
  transfers between devices with their start and end apart: 56, of which 32 were waited for; matrix products, arithmetic and copies ran while one was open for 4% of the time, Pallas kernels for 13%

profile of v3, /device:TPU:0, one launch (start us, length us, event | category | flops | bytes accessed | tf_op | source)
XLA Modules:
  0.0 479.9 jit_solution(10741142483893846840)
XLA Ops:
  0.6 4.6 first_norm.1
  5.2 3.3 fusion.1
  15.8 3.2 pad_maximum_fusion.q_ref.k_ref.v_ref.refs_0_.refs_1_.refs_2_
  19.1 13.8 %attention_forward.1 = (bf16[512,1024]{1,0:T(8,128)(2,1)}, f32[8,1,1024]{2,1,0:T(1,128)}) custom-call(bf16[3,512,1024]{2,1,0:T(8,128)(2,1)} %pad_maximum_fusion.q_ref.k_ref.v_ref.refs_0_.refs_1_.refs_2_, bf16[3,512,1024]{2,1,0:T(8,128)(2,1)} %pad_maximum_fusion.q_ref.k_ref.v_ref.refs_0_.refs_1_.refs_2_, ...), custom_call_target="tpu_custom_call" | custom-call | flops 2147483648 | bytes 4194304 | tf_op jit(solution)/shard_map/attention_forward/pallas_call | solution.py:120
  32.9 2.5 convolution_convert_fusion.4.refs_0_
  36.0 3.9 collective-permute-done.refs_1_
  39.9 6.8 %middle_norms.1 = (f32[1024,1024]{1,0:T(8,128)}, bf16[1024,1024]{1,0:T(8,128)(2,1)}) custom-call(f32[4,1024]{1,0:T(4,128)} %gain.9, f32[4,1024]{1,0:T(4,128)} %bias.9, bf16[1024,1024]{1,0:T(8,128)(2,1)} %bitcast.86, bf16[1024,1024]{1,0:T(8,128)(2,1)} %copy-done.3, bf16[1024,1024]{1,0:T(8,128)(2,1)} %collective-permute-done.refs_1_), custom_call_target="tpu_custom_call" | custom-call | flops 20971520 | bytes 12582912 | tf_op jit(solution)/shard_map/middle_norms/pallas_call | solution.py:293
  46.7 7.1 %fusion.29 = f32[1024,2048]{1,0:T(8,128)S(1)} fusion(bf16[1024,1024]{1,0:T(8,128)(2,1)} %get-tuple-element.173, bf16[1024,2048]{1,0:T(8,128)(2,1)} %param.17), kind=kOutput, calls=%fused_computation.176 | convolution fusion | flops 4294967296 | bytes 14680064 | tf_op jit(solution)/shard_map/dot_general | solution.py:192
  53.8 5.6 %convolution_convert_fusion.3.refs_0_ = bf16[1024,1024]{1,0:T(8,128)(2,1)S(1)} fusion(bf16[2048,1024]{1,0:T(8,128)(2,1)S(1)} %copy-done.76, f32[1024,2048]{1,0:T(8,128)S(1)} %fusion.29), kind=kOutput, calls=%fused_computation.22 | convolution fusion | flops 4314890240 | bytes 14680064 | tf_op jit(solution)/shard_map/dot_general | solution.py:192
  59.8 3.9 collective-permute-done.1.refs_1_
  63.7 8.3 %finish_norm.1 = (bf16[1024,1024]{1,0:T(8,128)(2,1)}, bf16[1024,1024]{1,0:T(8,128)(2,1)}, f32[2,1024]{1,0:T(2,128)}) custom-call(f32[4,1024]{1,0:T(4,128)} %gain.9, f32[4,1024]{1,0:T(4,128)} %bias.9, f32[1024,1024]{1,0:T(8,128)} %get-tuple-element.172.middle, bf16[1024,1024]{1,0:T(8,128)(2,1)} %bitcast.88, bf16[1024,1024]{1,0:T(8,128)(2,1)} %copy-done.35, ...), custom_call_target="tpu_custom_call" | custom-call | flops 20971520 | bytes 14680064 | tf_op jit(solution)/shard_map/finish_norm/pallas_call | solution.py:293
  72.1 10.0 %convolution_convert_fusion.1 = bf16[2048,1024]{1,0:T(8,128)(2,1)S(1)} fusion(bf16[1024,1024]{1,0:T(8,128)(2,1)} %get-tuple-element.176, f32[1024,2048]{1,0:T(8,128)} %copy-done.82), kind=kOutput, calls=%fused_computation.7 | convolution fusion | flops 4315938816 | bytes 14680064 | tf_op jit(solution)/shard_map/dot_general | solution.py:192
  85.1 8.6 %multiply_convert_fusion = bf16[1024,2048]{1,0:T(8,128)(2,1)S(1)} fusion(f32[1024,2048]{1,0:T(8,128)S(1)} %copy-done.83, bf16[1024,1024]{1,0:T(8,128)(2,1)S(1)} %copy-done.81, bf16[2048,1024]{1,0:T(8,128)(2,1)S(1)} %copy-done.77), kind=kOutput, calls=%fused_computation | convolution fusion | flops 4334813184 | bytes 18874368 | tf_op jit(solution)/shard_map/dot_general | solution.py:192
  93.7 5.4 %convolution_convert_fusion = bf16[1024,2048]{1,0:T(8,128)(2,1)S(1)} fusion(bf16[1024,1024]{1,0:T(8,128)(2,1)S(1)} %copy-done.79, bf16[1024,2048]{1,0:T(8,128)(2,1)S(1)} %multiply_convert_fusion), kind=kOutput, calls=%fused_computation.6 | convolution fusion | flops 4297064448 | bytes 10485760 | tf_op jit(solution)/shard_map/dot_general | solution.py:192
  103.0 2.8 collective-permute-start.2
  107.4 5.8 %convolution_convert_fusion.2.refs_2_ = bf16[1024,1024]{1,0:T(8,128)(2,1)} fusion(bf16[1024,2048]{1,0:T(8,128)(2,1)S(1)} %multiply_convert_fusion, bf16[1024,2048]{1,0:T(8,128)(2,1)S(1)} %copy-done.78), kind=kOutput, calls=%fused_computation.21 | convolution fusion | flops 4296015872 | bytes 10485760 | tf_op jit(solution)/shard_map/dot_general | solution.py:192
  113.1 16.2 %collective-permute-done.2 = bf16[512,1024]{1,0:T(8,128)(2,1)S(1)} collective-permute-done((bf16[512,1024]{1,0:T(8,128)(2,1)S(1)}, bf16[512,1024]{1,0:T(8,128)(2,1)S(1)}, u32[]{:S(2)}, u32[]{:S(2)}) %collective-permute-start.2) | collective-permute-done | bytes 1048608 | tf_op jit(solution)/shard_map/ppermute | solution.py:375
  138.2 10.6 %middle_back.1 = (f32[1024,1024]{1,0:T(8,128)}, bf16[1024,1024]{1,0:T(8,128)(2,1)}, f32[4,1024]{1,0:T(4,128)}) custom-call(f32[4,1024]{1,0:T(4,128)} %gain.9, f32[4,1024]{1,0:T(4,128)} %bias.9, f32[1024,1024]{1,0:T(8,128)} %get-tuple-element.172.middle, bf16[1024,1024]{1,0:T(8,128)(2,1)} %bitcast.89, bf16[1024,1024]{1,0:T(8,128)(2,1)} %copy-done.3, ...), custom_call_target="tpu_custom_call" | custom-call | flops 20971520 | bytes 20971520 | tf_op jit(solution)/shard_map/middle_back/pallas_call | solution.py:293
  148.8 4.0 fusion.4.do_ref.refs_9_
  152.8 7.2 %collective-permute-done.5 = bf16[256,2048]{1,0:T(8,128)(2,1)} collective-permute-done((bf16[256,2048]{1,0:T(8,128)(2,1)}, bf16[256,2048]{1,0:T(8,128)(2,1)}, u32[]{:S(2)}, u32[]{:S(2)}) %collective-permute-start.5) | collective-permute-done | bytes 1048608 | tf_op jit(solution)/shard_map/ppermute | solution.py:375
  160.4 10.5 %collective-permute-done.7 = bf16[256,1024]{1,0:T(8,128)(2,1)} collective-permute-done((bf16[256,1024]{1,0:T(8,128)(2,1)}, bf16[256,1024]{1,0:T(8,128)(2,1)}, u32[]{:S(2)}, u32[]{:S(2)}) %collective-permute-start.7) | collective-permute-done | bytes 524320 | tf_op jit(solution)/shard_map/ppermute | solution.py:375
  188.1 11.7 %attention_backward.2.refs_10_ = bf16[3,512,1024]{2,1,0:T(8,128)(2,1)} custom-call(bf16[3,512,1024]{2,1,0:T(8,128)(2,1)} %pad_maximum_fusion.q_ref.k_ref.v_ref.refs_0_.refs_1_.refs_2_, bf16[3,512,1024]{2,1,0:T(8,128)(2,1)} %pad_maximum_fusion.q_ref.k_ref.v_ref.refs_0_.refs_1_.refs_2_, ...), custom_call_target="tpu_custom_call" | custom-call | flops 2684354560 | bytes 4194304 | tf_op jit(solution)/shard_map/attention_backward/pallas_call | solution.py:144
  210.2 2.6 collective-permute-start.15
  213.1 11.5 %attention_backward.3 = bf16[3,512,1024]{2,1,0:T(8,128)(2,1)} custom-call(bf16[3,512,1024]{2,1,0:T(8,128)(2,1)} %pad_maximum_fusion.q_ref.k_ref.v_ref.refs_0_.refs_1_.refs_2_, bf16[3,512,1024]{2,1,0:T(8,128)(2,1)} %pad_maximum_fusion.q_ref.k_ref.v_ref.refs_0_.refs_1_.refs_2_, ...), custom_call_target="tpu_custom_call", output_to_operand_aliasing={{}: (10, {})} | custom-call | flops 2684354560 | bytes 4194304 | tf_op jit(solution)/shard_map/attention_backward/pallas_call | solution.py:144
  229.2 2.7 convolution_convert_fusion.6
  235.9 2.8 fusion.6
  241.3 2.5 collective-permute-start.17
  248.5 9.9 %collective-permute-done.17 = bf16[32,2048]{1,0:T(8,128)(2,1)S(1)} collective-permute-done((bf16[32,2048]{1,0:T(8,128)(2,1)S(1)}, bf16[32,2048]{1,0:T(8,128)(2,1)S(1)}, u32[]{:S(2)}, u32[]{:S(2)}) %collective-permute-start.17) | collective-permute-done | bytes 131104 | tf_op jit(solution)/shard_map/ppermute | solution.py:375
  258.4 2.8 collective-permute-done.18
  261.2 2.7 collective-permute-done.19
  268.8 3.3 collective-permute-start.26
  272.1 5.8 %collective-permute-done.24 = bf16[32,2048]{1,0:T(8,128)(2,1)S(1)} collective-permute-done((bf16[32,2048]{1,0:T(8,128)(2,1)S(1)}, bf16[32,2048]{1,0:T(8,128)(2,1)S(1)}, u32[]{:S(2)}, u32[]{:S(2)}) %collective-permute-start.24) | collective-permute-done | bytes 131104 | tf_op jit(solution)/shard_map/ppermute | solution.py:375
  281.1 8.0 %first_back.1 = (bf16[1024,1024]{1,0:T(8,128)(2,1)}, f32[2,1024]{1,0:T(2,128)}) custom-call(f32[4,1024]{1,0:T(4,128)} %gain.9, f32[4,1024]{1,0:T(4,128)} %bias.9, bf16[1024,1024]{1,0:T(8,128)(2,1)} %bitcast.87, f32[1024,1024]{1,0:T(8,128)} %get-tuple-element.184.d_middle, bf16[1024,1024]{1,0:T(8,128)(2,1)} %copy-done.6, bf16[1024,1024]{1,0:T(8,128)(2,1)} %copy-done.36), custom_call_target="tpu_custom_call" | custom-call | flops 20971520 | bytes 12582912 | tf_op jit(solution)/shard_map/first_back/pallas_call | solution.py:293
  302.0 3.0 add_convert_fusion.3
  313.9 3.8 collective-permute-done.31
  318.7 6.6 %collective-permute-done.32 = bf16[64,2048]{1,0:T(8,128)(2,1)} collective-permute-done((bf16[64,2048]{1,0:T(8,128)(2,1)}, bf16[64,2048]{1,0:T(8,128)(2,1)}, u32[]{:S(2)}, u32[]{:S(2)}) %collective-permute-start.32) | collective-permute-done | bytes 262176 | tf_op jit(solution)/shard_map/ppermute | solution.py:375
  325.5 8.3 %collective-permute-done.33 = bf16[256,1024]{1,0:T(8,128)(2,1)S(1)} collective-permute-done((bf16[256,1024]{1,0:T(8,128)(2,1)}, bf16[256,1024]{1,0:T(8,128)(2,1)S(1)}, u32[]{:S(2)}, u32[]{:S(2)}) %collective-permute-start.33) | collective-permute-done | bytes 524320 | tf_op jit(solution)/shard_map/ppermute | solution.py:375
  351.4 2.8 collective-permute-done.36
  355.7 5.8 %collective-permute-done.37 = bf16[256,512]{1,0:T(8,128)(2,1)S(1)} collective-permute-done((bf16[256,512]{1,0:T(8,128)(2,1)}, bf16[256,512]{1,0:T(8,128)(2,1)S(1)}, u32[]{:S(2)}, u32[]{:S(2)}) %collective-permute-start.37) | collective-permute-done | bytes 262176 | tf_op jit(solution)/shard_map/ppermute | solution.py:375
  361.5 17.8 %collective-permute-done.38 = bf16[128,2048]{1,0:T(8,128)(2,1)S(1)} collective-permute-done((bf16[128,2048]{1,0:T(8,128)(2,1)}, bf16[128,2048]{1,0:T(8,128)(2,1)S(1)}, u32[]{:S(2)}, u32[]{:S(2)}) %collective-permute-start.38) | collective-permute-done | bytes 524320 | tf_op jit(solution)/shard_map/ppermute | solution.py:375
  402.7 5.2 %collective-permute-done.45.piece = bf16[256,2048]{1,0:T(8,128)(2,1)S(1)} collective-permute-done((bf16[256,2048]{1,0:T(8,128)(2,1)S(1)}, bf16[256,2048]{1,0:T(8,128)(2,1)S(1)}, u32[]{:S(2)}, u32[]{:S(2)}) %collective-permute-start.45) | collective-permute-done | bytes 1048608 | tf_op jit(solution)/shard_map/ppermute | solution.py:375
  426.4 6.1 %collective-permute-done.50 = bf16[256,512]{1,0:T(8,128)(2,1)S(1)} collective-permute-done((bf16[256,512]{1,0:T(8,128)(2,1)S(1)}, bf16[256,512]{1,0:T(8,128)(2,1)S(1)}, u32[]{:S(2)}, u32[]{:S(2)}) %collective-permute-start.50) | collective-permute-done | bytes 262176 | tf_op jit(solution)/shard_map/ppermute | solution.py:375
  432.5 2.8 collective-permute-done.51
  438.5 7.8 %collective-permute-done.52 = bf16[512,512]{1,0:T(8,128)(2,1)S(1)} collective-permute-done((bf16[512,512]{1,0:T(8,128)(2,1)S(1)}, bf16[512,512]{1,0:T(8,128)(2,1)S(1)}, u32[]{:S(2)}, u32[]{:S(2)}) %collective-permute-start.52) | collective-permute-done | bytes 524320 | tf_op jit(solution)/shard_map/ppermute | solution.py:375
  446.3 2.9 collective-permute-done.53
  455.1 15.3 %collective-permute-done.54.piece = bf16[1024,512]{1,0:T(8,128)(2,1)} collective-permute-done((bf16[1024,512]{1,0:T(8,128)(2,1)S(1)}, bf16[1024,512]{1,0:T(8,128)(2,1)}, u32[]{:S(2)}, u32[]{:S(2)}) %collective-permute-start.54) | collective-permute-done | bytes 1048608 | tf_op jit(solution)/shard_map/ppermute | solution.py:375
  470.3 2.6 select_convert_fusion
  477.0 2.5 place.21
  (379 shorter events, 173.1 us)
Async XLA Ops:
  103.0 26.3 %collective-permute-start.2 = (bf16[512,1024]{1,0:T(8,128)(2,1)S(1)}, bf16[512,1024]{1,0:T(8,128)(2,1)S(1)}, u32[]{:S(2)}, u32[]{:S(2)}) collective-permute-start(bf16[512,1024]{1,0:T(8,128)(2,1)S(1)} %constant_dynamic-slice_fusion.22), channel_id=1, source_target_pairs={{0,2},{2,0},{4,6},{6,4},{8,10},{10,8},{12,14},{14,12},{16,18},{18,... | collective-permute-start | bytes 3145736 | tf_op jit(solution)/shard_map/ppermute | solution.py:375
  105.8 24.9 %collective-permute-start.3 = (bf16[512,1024]{1,0:T(8,128)(2,1)S(1)}, bf16[512,1024]{1,0:T(8,128)(2,1)S(1)}, u32[]{:S(2)}, u32[]{:S(2)}) collective-permute-start(bf16[512,1024]{1,0:T(8,128)(2,1)S(1)} %constant_dynamic-slice_fusion.21), channel_id=1, source_target_pairs={{0,4},{2,6},{4,0},{6,2},{8,12},{10,14},{12,8},{14,10},{16,20},{18,... | collective-permute-start | bytes 3145736 | tf_op jit(solution)/shard_map/ppermute | solution.py:375
  133.7 26.3 %collective-permute-start.5 = (bf16[256,2048]{1,0:T(8,128)(2,1)}, bf16[256,2048]{1,0:T(8,128)(2,1)}, u32[]{:S(2)}, u32[]{:S(2)}) collective-permute-start(bf16[256,2048]{1,0:T(8,128)(2,1)} %constant_dynamic-slice_fusion.20), channel_id=1, source_target_pairs={{0,2},{2,0},{4,6},{6,4},{8,10},{10,8},{12,14},{14,12},{16,18},{18,... | collective-permute-start | bytes 3145736 | tf_op jit(solution)/shard_map/ppermute | solution.py:375
  134.0 26.3 %collective-permute-start.6 = (bf16[256,2048]{1,0:T(8,128)(2,1)}, bf16[256,2048]{1,0:T(8,128)(2,1)}, u32[]{:S(2)}, u32[]{:S(2)}) collective-permute-start(bf16[256,2048]{1,0:T(8,128)(2,1)} %constant_dynamic-slice_fusion.19), channel_id=1, source_target_pairs={{0,4},{2,6},{4,0},{6,2},{8,12},{10,14},{12,8},{14,10},{16,20},{18,... | collective-permute-start | bytes 3145736 | tf_op jit(solution)/shard_map/ppermute | solution.py:375
  135.8 35.1 %collective-permute-start.7 = (bf16[256,1024]{1,0:T(8,128)(2,1)}, bf16[256,1024]{1,0:T(8,128)(2,1)}, u32[]{:S(2)}, u32[]{:S(2)}) collective-permute-start(bf16[256,1024]{1,0:T(8,128)(2,1)} %constant_dynamic-slice_fusion.18), channel_id=1, source_target_pairs={{0,4},{2,6},{4,0},{6,2},{8,12},{10,14},{12,8},{14,10},{16,20},{18,... | collective-permute-start | bytes 1572872 | tf_op jit(solution)/shard_map/ppermute | solution.py:375
  136.0 34.8 %collective-permute-start.8 = (bf16[256,1024]{1,0:T(8,128)(2,1)}, bf16[256,1024]{1,0:T(8,128)(2,1)}, u32[]{:S(2)}, u32[]{:S(2)}) collective-permute-start(bf16[256,1024]{1,0:T(8,128)(2,1)} %constant_dynamic-slice_fusion.17), channel_id=1, source_target_pairs={{0,2},{2,0},{4,6},{6,4},{8,10},{10,8},{12,14},{14,12},{16,18},{18,... | collective-permute-start | bytes 1572872 | tf_op jit(solution)/shard_map/ppermute | solution.py:375
  180.6 19.3 %collective-permute-start.10 = (bf16[128,2048]{1,0:T(8,128)(2,1)}, bf16[128,2048]{1,0:T(8,128)(2,1)}, u32[]{:S(2)}, u32[]{:S(2)}) collective-permute-start(bf16[128,2048]{1,0:T(8,128)(2,1)} %constant_dynamic-slice_fusion.15), channel_id=1, source_target_pairs={{0,2},{2,0},{4,6},{6,4},{8,10},{10,8},{12,14},{14,12},{16,18},{18,... | collective-permute-start | bytes 1572872 | tf_op jit(solution)/shard_map/ppermute | solution.py:375
  182.3 17.6 %collective-permute-start.9 = (bf16[128,2048]{1,0:T(8,128)(2,1)}, bf16[128,2048]{1,0:T(8,128)(2,1)}, u32[]{:S(2)}, u32[]{:S(2)}) collective-permute-start(bf16[128,2048]{1,0:T(8,128)(2,1)} %constant_dynamic-slice_fusion.16), channel_id=1, source_target_pairs={{0,4},{2,6},{4,0},{6,2},{8,12},{10,14},{12,8},{14,10},{16,20},{18,... | collective-permute-start | bytes 1572872 | tf_op jit(solution)/shard_map/ppermute | solution.py:375
  183.8 16.1 %collective-permute-start.11 = (bf16[128,1024]{1,0:T(8,128)(2,1)}, bf16[128,1024]{1,0:T(8,128)(2,1)}, u32[]{:S(2)}, u32[]{:S(2)}) collective-permute-start(bf16[128,1024]{1,0:T(8,128)(2,1)} %constant_dynamic-slice_fusion.14), channel_id=1, source_target_pairs={{0,8},{2,10},{4,12},{6,14},{8,0},{10,2},{12,4},{14,6},{16,24},{18,... | collective-permute-start | bytes 786440 | tf_op jit(solution)/shard_map/ppermute | solution.py:375
  185.4 14.5 %collective-permute-start.12 = (bf16[128,1024]{1,0:T(8,128)(2,1)S(1)}, bf16[128,1024]{1,0:T(8,128)(2,1)}, u32[]{:S(2)}, u32[]{:S(2)}) collective-permute-start(bf16[128,1024]{1,0:T(8,128)(2,1)S(1)} %constant_dynamic-slice_fusion.13), channel_id=1, source_target_pairs={{0,8},{2,10},{4,12},{6,14},{8,0},{10,2},{12,4},{14,6},{16,24},{18,... | collective-permute-start | bytes 786440 | tf_op jit(solution)/shard_map/ppermute | solution.py:375
  207.1 17.5 %collective-permute-start.13 = (bf16[64,2048]{1,0:T(8,128)(2,1)}, bf16[64,2048]{1,0:T(8,128)(2,1)}, u32[]{:S(2)}, u32[]{:S(2)}) collective-permute-start(bf16[64,2048]{1,0:T(8,128)(2,1)} %constant_dynamic-slice_fusion.12), channel_id=1, source_target_pairs={{0,8},{2,10},{4,12},{6,14},{8,0},{10,2},{12,4},{14,6},{16,24},{18,... | collective-permute-start | bytes 786440 | tf_op jit(solution)/shard_map/ppermute | solution.py:375
  208.6 16.4 %collective-permute-start.14 = (bf16[64,2048]{1,0:T(8,128)(2,1)}, bf16[64,2048]{1,0:T(8,128)(2,1)}, u32[]{:S(2)}, u32[]{:S(2)}) collective-permute-start(bf16[64,2048]{1,0:T(8,128)(2,1)} %constant_dynamic-slice_fusion.11), channel_id=1, source_target_pairs={{0,8},{2,10},{4,12},{6,14},{8,0},{10,2},{12,4},{14,6},{16,24},{18,... | collective-permute-start | bytes 786440 | tf_op jit(solution)/shard_map/ppermute | solution.py:375
  210.2 14.4 %collective-permute-start.15 = (bf16[64,1024]{1,0:T(8,128)(2,1)}, bf16[64,1024]{1,0:T(8,128)(2,1)}, u32[]{:S(2)}, u32[]{:S(2)}) collective-permute-start(bf16[64,1024]{1,0:T(8,128)(2,1)} %constant_dynamic-slice_fusion.10), channel_id=1, source_target_pairs={{0,16},{2,18},{4,20},{6,22},{8,24},{10,26},{12,28},{14,30},{16,0},... | collective-permute-start | bytes 393224 | tf_op jit(solution)/shard_map/ppermute | solution.py:375
  212.7 11.8 %collective-permute-start.16 = (bf16[64,1024]{1,0:T(8,128)(2,1)S(1)}, bf16[64,1024]{1,0:T(8,128)(2,1)}, u32[]{:S(2)}, u32[]{:S(2)}) collective-permute-start(bf16[64,1024]{1,0:T(8,128)(2,1)S(1)} %constant_dynamic-slice_fusion.9), channel_id=1, source_target_pairs={{0,16},{2,18},{4,20},{6,22},{8,24},{10,26},{12,28},{14,30},{16,0},... | collective-permute-start | bytes 393224 | tf_op jit(solution)/shard_map/ppermute | solution.py:375
  241.3 17.1 %collective-permute-start.17 = (bf16[32,2048]{1,0:T(8,128)(2,1)S(1)}, bf16[32,2048]{1,0:T(8,128)(2,1)S(1)}, u32[]{:S(2)}, u32[]{:S(2)}) collective-permute-start(bf16[32,2048]{1,0:T(8,128)(2,1)S(1)} %constant_dynamic-slice_fusion.8), channel_id=1, source_target_pairs={{0,16},{2,18},{4,20},{6,22},{8,24},{10,26},{12,28},{14,30},{16,0},... | collective-permute-start | bytes 393224 | tf_op jit(solution)/shard_map/ppermute | solution.py:375
  243.8 17.4 %collective-permute-start.18 = (bf16[32,2048]{1,0:T(8,128)(2,1)S(1)}, bf16[32,2048]{1,0:T(8,128)(2,1)S(1)}, u32[]{:S(2)}, u32[]{:S(2)}) collective-permute-start(bf16[32,2048]{1,0:T(8,128)(2,1)S(1)} %constant_dynamic-slice_fusion.7), channel_id=1, source_target_pairs={{0,16},{2,18},{4,20},{6,22},{8,24},{10,26},{12,28},{14,30},{16,0},... | collective-permute-start | bytes 393224 | tf_op jit(solution)/shard_map/ppermute | solution.py:375
  244.3 19.6 %collective-permute-start.19 = (bf16[64,1024]{1,0:T(8,128)(2,1)S(1)}, bf16[64,1024]{1,0:T(8,128)(2,1)S(1)}, u32[]{:S(2)}, u32[]{:S(2)}) collective-permute-start(bf16[64,1024]{1,0:T(8,128)(2,1)S(1)} %add_convert_fusion.25), channel_id=1, source_target_pairs={{0,16},{2,18},{4,20},{6,22},{8,24},{10,26},{12,28},{14,30},{16,0},... | collective-permute-start | bytes 393224 | tf_op jit(solution)/shard_map/ppermute | solution.py:375
  246.8 18.6 %collective-permute-start.20 = (bf16[64,1024]{1,0:T(8,128)(2,1)S(1)}, bf16[64,1024]{1,0:T(8,128)(2,1)S(1)}, u32[]{:S(2)}, u32[]{:S(2)}) collective-permute-start(bf16[64,1024]{1,0:T(8,128)(2,1)S(1)} %add_convert_fusion.24), channel_id=1, source_target_pairs={{0,16},{2,18},{4,20},{6,22},{8,24},{10,26},{12,28},{14,30},{16,0},... | collective-permute-start | bytes 393224 | tf_op jit(solution)/shard_map/ppermute | solution.py:375
  267.7 10.3 %collective-permute-start.21 = (bf16[1024,1024]{1,0:T(8,128)(2,1)S(1)}, bf16[1024,1024]{1,0:T(8,128)(2,1)S(1)}, u32[]{:S(2)}, u32[]{:S(2)}) collective-permute-start(bf16[1024,1024]{1,0:T(8,128)(2,1)S(1)} %add_convert_fusion.1.refs_0_), channel_id=1, source_target_pairs={{0,1},{1,0},{2,3},{3,2},{4,5},{5,4},{6,7},{7,6},{8,9},{9,8},{10,11... | collective-permute-start | bytes 6291464 | tf_op jit(solution)/shard_map/ppermute | solution.py:443
  267.7 26.1 %collective-permute-start.22 = (bf16[1024,512]{1,0:T(8,128)(2,1)}, bf16[1024,512]{1,0:T(8,128)(2,1)}, u32[]{:S(2)}, u32[]{:S(2)}) collective-permute-start(bf16[1024,512]{1,0:T(8,128)(2,1)} %fusion.6), channel_id=1, source_target_pairs={{0,2},{2,0},{4,6},{6,4},{8,10},{10,8},{12,14},{14,12},{16,18},{18,... | collective-permute-start | bytes 3145736 | tf_op jit(solution)/shard_map/ppermute | solution.py:375
  268.3 25.6 %collective-permute-start.23 = (bf16[1024,512]{1,0:T(8,128)(2,1)}, bf16[1024,512]{1,0:T(8,128)(2,1)}, u32[]{:S(2)}, u32[]{:S(2)}) collective-permute-start(bf16[1024,512]{1,0:T(8,128)(2,1)} %constant_dynamic-slice_fusion.6), channel_id=1, source_target_pairs={{0,4},{2,6},{4,0},{6,2},{8,12},{10,14},{12,8},{14,10},{16,20},{18,... | collective-permute-start | bytes 3145736 | tf_op jit(solution)/shard_map/ppermute | solution.py:375
  268.8 9.2 %collective-permute-start.24 = (bf16[32,2048]{1,0:T(8,128)(2,1)S(1)}, bf16[32,2048]{1,0:T(8,128)(2,1)S(1)}, u32[]{:S(2)}, u32[]{:S(2)}) collective-permute-start(bf16[32,2048]{1,0:T(8,128)(2,1)S(1)} %add_convert_fusion.23), channel_id=1, source_target_pairs={{0,16},{2,18},{4,20},{6,22},{8,24},{10,26},{12,28},{14,30},{16,0},... | collective-permute-start | bytes 393224 | tf_op jit(solution)/shard_map/ppermute | solution.py:375
  268.8 22.5 %collective-permute-start.26 = (bf16[128,1024]{1,0:T(8,128)(2,1)}, bf16[128,1024]{1,0:T(8,128)(2,1)}, u32[]{:S(2)}, u32[]{:S(2)}) collective-permute-start(bf16[128,1024]{1,0:T(8,128)(2,1)} %pad_maximum_fusion.15), channel_id=1, source_target_pairs={{0,8},{2,10},{4,12},{6,14},{8,0},{10,2},{12,4},{14,6},{16,24},{18,... | collective-permute-start | bytes 786440 | tf_op jit(solution)/shard_map/ppermute | solution.py:375
  278.0 13.3 %collective-permute-start.27 = (bf16[128,1024]{1,0:T(8,128)(2,1)}, bf16[128,1024]{1,0:T(8,128)(2,1)}, u32[]{:S(2)}, u32[]{:S(2)}) collective-permute-start(bf16[128,1024]{1,0:T(8,128)(2,1)} %pad_maximum_fusion.16), channel_id=1, source_target_pairs={{0,8},{2,10},{4,12},{6,14},{8,0},{10,2},{12,4},{14,6},{16,24},{18,... | collective-permute-start | bytes 786440 | tf_op jit(solution)/shard_map/ppermute | solution.py:375
  279.3 10.4 %collective-permute-start.25 = (bf16[32,2048]{1,0:T(8,128)(2,1)}, bf16[32,2048]{1,0:T(8,128)(2,1)}, u32[]{:S(2)}, u32[]{:S(2)}) collective-permute-start(bf16[32,2048]{1,0:T(8,128)(2,1)} %add_convert_fusion.22), channel_id=1, source_target_pairs={{0,16},{2,18},{4,20},{6,22},{8,24},{10,26},{12,28},{14,30},{16,0},... | collective-permute-start | bytes 393224 | tf_op jit(solution)/shard_map/ppermute | solution.py:375
  309.5 15.8 %collective-permute-start.29 = (bf16[512,512]{1,0:T(8,128)(2,1)}, bf16[512,512]{1,0:T(8,128)(2,1)}, u32[]{:S(2)}, u32[]{:S(2)}) collective-permute-start(bf16[512,512]{1,0:T(8,128)(2,1)} %constant_dynamic-slice_fusion.5), channel_id=1, source_target_pairs={{0,4},{2,6},{4,0},{6,2},{8,12},{10,14},{12,8},{14,10},{16,20},{18,... | collective-permute-start | bytes 1572872 | tf_op jit(solution)/shard_map/ppermute | solution.py:375
  310.4 7.4 %collective-permute-start.31 = (bf16[64,2048]{1,0:T(8,128)(2,1)S(1)}, bf16[64,2048]{1,0:T(8,128)(2,1)S(1)}, u32[]{:S(2)}, u32[]{:S(2)}) collective-permute-start(bf16[64,2048]{1,0:T(8,128)(2,1)S(1)} %pad_maximum_fusion.17), channel_id=1, source_target_pairs={{0,8},{2,10},{4,12},{6,14},{8,0},{10,2},{12,4},{14,6},{16,24},{18,... | collective-permute-start | bytes 786440 | tf_op jit(solution)/shard_map/ppermute | solution.py:375
  310.4 15.1 %collective-permute-start.30 = (bf16[512,512]{1,0:T(8,128)(2,1)}, bf16[512,512]{1,0:T(8,128)(2,1)}, u32[]{:S(2)}, u32[]{:S(2)}) collective-permute-start(bf16[512,512]{1,0:T(8,128)(2,1)} %constant_dynamic-slice_fusion.4), channel_id=1, source_target_pairs={{0,2},{2,0},{4,6},{6,4},{8,10},{10,8},{12,14},{14,12},{16,18},{18,... | collective-permute-start | bytes 1572872 | tf_op jit(solution)/shard_map/ppermute | solution.py:375
  311.8 21.9 %collective-permute-start.33 = (bf16[256,1024]{1,0:T(8,128)(2,1)}, bf16[256,1024]{1,0:T(8,128)(2,1)S(1)}, u32[]{:S(2)}, u32[]{:S(2)}) collective-permute-start(bf16[256,1024]{1,0:T(8,128)(2,1)} %pad_maximum_fusion.9), channel_id=1, source_target_pairs={{0,4},{2,6},{4,0},{6,2},{8,12},{10,14},{12,8},{14,10},{16,20},{18,... | collective-permute-start | bytes 1572872 | tf_op jit(solution)/shard_map/ppermute | solution.py:375
  313.3 21.5 %collective-permute-start.34 = (bf16[256,1024]{1,0:T(8,128)(2,1)}, bf16[256,1024]{1,0:T(8,128)(2,1)S(1)}, u32[]{:S(2)}, u32[]{:S(2)}) collective-permute-start(bf16[256,1024]{1,0:T(8,128)(2,1)} %pad_maximum_fusion.10), channel_id=1, source_target_pairs={{0,2},{2,0},{4,6},{6,4},{8,10},{10,8},{12,14},{14,12},{16,18},{18,... | collective-permute-start | bytes 1572872 | tf_op jit(solution)/shard_map/ppermute | solution.py:375
  318.4 6.9 %collective-permute-start.32 = (bf16[64,2048]{1,0:T(8,128)(2,1)}, bf16[64,2048]{1,0:T(8,128)(2,1)}, u32[]{:S(2)}, u32[]{:S(2)}) collective-permute-start(bf16[64,2048]{1,0:T(8,128)(2,1)} %pad_maximum_fusion.18), channel_id=1, source_target_pairs={{0,8},{2,10},{4,12},{6,14},{8,0},{10,2},{12,4},{14,6},{16,24},{18,... | collective-permute-start | bytes 786440 | tf_op jit(solution)/shard_map/ppermute | solution.py:375
  344.3 35.1 %collective-permute-start.40 = (bf16[512,1024]{1,0:T(8,128)(2,1)S(1)}, bf16[512,1024]{1,0:T(8,128)(2,1)}, u32[]{:S(2)}, u32[]{:S(2)}) collective-permute-start(bf16[512,1024]{1,0:T(8,128)(2,1)S(1)} %pad_maximum_fusion.3.piece), channel_id=1, source_target_pairs={{0,2},{2,0},{4,6},{6,4},{8,10},{10,8},{12,14},{14,12},{16,18},{18,... | collective-permute-start | bytes 3145736 | tf_op jit(solution)/shard_map/ppermute | solution.py:375
  345.3 34.0 %collective-permute-start.41 = (bf16[512,1024]{1,0:T(8,128)(2,1)S(1)}, bf16[512,1024]{1,0:T(8,128)(2,1)}, u32[]{:S(2)}, u32[]{:S(2)}) collective-permute-start(bf16[512,1024]{1,0:T(8,128)(2,1)S(1)} %pad_maximum_fusion.4.piece), channel_id=1, source_target_pairs={{0,4},{2,6},{4,0},{6,2},{8,12},{10,14},{12,8},{14,10},{16,20},{18,... | collective-permute-start | bytes 3145736 | tf_op jit(solution)/shard_map/ppermute | solution.py:375
  348.6 30.7 %collective-permute-start.38 = (bf16[128,2048]{1,0:T(8,128)(2,1)}, bf16[128,2048]{1,0:T(8,128)(2,1)S(1)}, u32[]{:S(2)}, u32[]{:S(2)}) collective-permute-start(bf16[128,2048]{1,0:T(8,128)(2,1)} %pad_maximum_fusion.11), channel_id=1, source_target_pairs={{0,4},{2,6},{4,0},{6,2},{8,12},{10,14},{12,8},{14,10},{16,20},{18,... | collective-permute-start | bytes 1572872 | tf_op jit(solution)/shard_map/ppermute | solution.py:375
  350.3 29.0 %collective-permute-start.39 = (bf16[128,2048]{1,0:T(8,128)(2,1)}, bf16[128,2048]{1,0:T(8,128)(2,1)}, u32[]{:S(2)}, u32[]{:S(2)}) collective-permute-start(bf16[128,2048]{1,0:T(8,128)(2,1)} %pad_maximum_fusion.12), channel_id=1, source_target_pairs={{0,2},{2,0},{4,6},{6,4},{8,10},{10,8},{12,14},{14,12},{16,18},{18,... | collective-permute-start | bytes 1572872 | tf_op jit(solution)/shard_map/ppermute | solution.py:375
  385.6 22.2 %collective-permute-start.45 = (bf16[256,2048]{1,0:T(8,128)(2,1)S(1)}, bf16[256,2048]{1,0:T(8,128)(2,1)S(1)}, u32[]{:S(2)}, u32[]{:S(2)}) collective-permute-start(bf16[256,2048]{1,0:T(8,128)(2,1)S(1)} %pad_maximum_fusion.5.piece), channel_id=1, source_target_pairs={{0,2},{2,0},{4,6},{6,4},{8,10},{10,8},{12,14},{14,12},{16,18},{18,... | collective-permute-start | bytes 3145736 | tf_op jit(solution)/shard_map/ppermute | solution.py:375
  387.0 22.6 %collective-permute-start.46 = (bf16[256,2048]{1,0:T(8,128)(2,1)S(1)}, bf16[256,2048]{1,0:T(8,128)(2,1)}, u32[]{:S(2)}, u32[]{:S(2)}) collective-permute-start(bf16[256,2048]{1,0:T(8,128)(2,1)S(1)} %pad_maximum_fusion.6.piece), channel_id=1, source_target_pairs={{0,4},{2,6},{4,0},{6,2},{8,12},{10,14},{12,8},{14,10},{16,20},{18,... | collective-permute-start | bytes 3145736 | tf_op jit(solution)/shard_map/ppermute | solution.py:375
  388.7 14.0 %collective-permute-start.43 = (bf16[128,512]{1,0:T(8,128)(2,1)}, bf16[128,512]{1,0:T(8,128)(2,1)}, u32[]{:S(2)}, u32[]{:S(2)}) collective-permute-start(bf16[128,512]{1,0:T(8,128)(2,1)} %constant_dynamic-slice_fusion.1), channel_id=1, source_target_pairs={{0,16},{2,18},{4,20},{6,22},{8,24},{10,26},{12,28},{14,30},{16,0},... | collective-permute-start | bytes 393224 | tf_op jit(solution)/shard_map/ppermute | solution.py:375
  390.0 12.7 %collective-permute-start.44 = (bf16[128,512]{1,0:T(8,128)(2,1)S(1)}, bf16[128,512]{1,0:T(8,128)(2,1)}, u32[]{:S(2)}, u32[]{:S(2)}) collective-permute-start(bf16[128,512]{1,0:T(8,128)(2,1)S(1)} %constant_dynamic-slice_fusion), channel_id=1, source_target_pairs={{0,16},{2,18},{4,20},{6,22},{8,24},{10,26},{12,28},{14,30},{16,0},... | collective-permute-start | bytes 393224 | tf_op jit(solution)/shard_map/ppermute | solution.py:375
  391.6 11.0 %collective-permute-start.47 = (bf16[8,1024]{1,0:T(8,128)(2,1)}, bf16[8,1024]{1,0:T(8,128)(2,1)S(1)}, u32[]{:S(2)}, u32[]{:S(2)}) collective-permute-start(bf16[8,1024]{1,0:T(8,128)(2,1)} %add_convert_fusion.27), channel_id=1, source_target_pairs={{0,16},{2,18},{4,20},{6,22},{8,24},{10,26},{12,28},{14,30},{16,0},... | collective-permute-start | bytes 49160 | tf_op jit(solution)/shard_map/ppermute | solution.py:375
  411.5 12.7 %collective-permute-start.48 = (bf16[128,512]{1,0:T(8,128)(2,1)S(1)}, bf16[128,512]{1,0:T(8,128)(2,1)S(1)}, u32[]{:S(2)}, u32[]{:S(2)}) collective-permute-start(bf16[128,512]{1,0:T(8,128)(2,1)S(1)} %add_convert_fusion.21), channel_id=1, source_target_pairs={{0,16},{2,18},{4,20},{6,22},{8,24},{10,26},{12,28},{14,30},{16,0},... | collective-permute-start | bytes 393224 | tf_op jit(solution)/shard_map/ppermute | solution.py:375
  413.6 10.6 %collective-permute-start.49 = (bf16[128,512]{1,0:T(8,128)(2,1)S(1)}, bf16[128,512]{1,0:T(8,128)(2,1)S(1)}, u32[]{:S(2)}, u32[]{:S(2)}) collective-permute-start(bf16[128,512]{1,0:T(8,128)(2,1)S(1)} %add_convert_fusion.20), channel_id=1, source_target_pairs={{0,16},{2,18},{4,20},{6,22},{8,24},{10,26},{12,28},{14,30},{16,0},... | collective-permute-start | bytes 393224 | tf_op jit(solution)/shard_map/ppermute | solution.py:375
  424.3 8.2 %collective-permute-start.50 = (bf16[256,512]{1,0:T(8,128)(2,1)S(1)}, bf16[256,512]{1,0:T(8,128)(2,1)S(1)}, u32[]{:S(2)}, u32[]{:S(2)}) collective-permute-start(bf16[256,512]{1,0:T(8,128)(2,1)S(1)} %pad_maximum_fusion.19), channel_id=1, source_target_pairs={{0,8},{2,10},{4,12},{6,14},{8,0},{10,2},{12,4},{14,6},{16,24},{18,... | collective-permute-start | bytes 786440 | tf_op jit(solution)/shard_map/ppermute | solution.py:375
  425.1 10.1 %collective-permute-start.51 = (bf16[256,512]{1,0:T(8,128)(2,1)S(1)}, bf16[256,512]{1,0:T(8,128)(2,1)S(1)}, u32[]{:S(2)}, u32[]{:S(2)}) collective-permute-start(bf16[256,512]{1,0:T(8,128)(2,1)S(1)} %pad_maximum_fusion.20), channel_id=1, source_target_pairs={{0,8},{2,10},{4,12},{6,14},{8,0},{10,2},{12,4},{14,6},{16,24},{18,... | collective-permute-start | bytes 786440 | tf_op jit(solution)/shard_map/ppermute | solution.py:375
  435.6 10.7 %collective-permute-start.52 = (bf16[512,512]{1,0:T(8,128)(2,1)S(1)}, bf16[512,512]{1,0:T(8,128)(2,1)S(1)}, u32[]{:S(2)}, u32[]{:S(2)}) collective-permute-start(bf16[512,512]{1,0:T(8,128)(2,1)S(1)} %pad_maximum_fusion.13), channel_id=1, source_target_pairs={{0,4},{2,6},{4,0},{6,2},{8,12},{10,14},{12,8},{14,10},{16,20},{18,... | collective-permute-start | bytes 1572872 | tf_op jit(solution)/shard_map/ppermute | solution.py:375
  437.7 11.5 %collective-permute-start.53 = (bf16[512,512]{1,0:T(8,128)(2,1)S(1)}, bf16[512,512]{1,0:T(8,128)(2,1)S(1)}, u32[]{:S(2)}, u32[]{:S(2)}) collective-permute-start(bf16[512,512]{1,0:T(8,128)(2,1)S(1)} %pad_maximum_fusion.14), channel_id=1, source_target_pairs={{0,2},{2,0},{4,6},{6,4},{8,10},{10,8},{12,14},{14,12},{16,18},{18,... | collective-permute-start | bytes 1572872 | tf_op jit(solution)/shard_map/ppermute | solution.py:375
  449.7 20.6 %collective-permute-start.54 = (bf16[1024,512]{1,0:T(8,128)(2,1)S(1)}, bf16[1024,512]{1,0:T(8,128)(2,1)}, u32[]{:S(2)}, u32[]{:S(2)}) collective-permute-start(bf16[1024,512]{1,0:T(8,128)(2,1)S(1)} %pad_maximum_fusion.7.piece), channel_id=1, source_target_pairs={{0,2},{2,0},{4,6},{6,4},{8,10},{10,8},{12,14},{14,12},{16,18},{18,... | collective-permute-start | bytes 3145736 | tf_op jit(solution)/shard_map/ppermute | solution.py:375
  450.6 19.8 %collective-permute-start.55 = (bf16[1024,512]{1,0:T(8,128)(2,1)S(1)}, bf16[1024,512]{1,0:T(8,128)(2,1)}, u32[]{:S(2)}, u32[]{:S(2)}) collective-permute-start(bf16[1024,512]{1,0:T(8,128)(2,1)S(1)} %pad_maximum_fusion.8), channel_id=1, source_target_pairs={{0,4},{2,6},{4,0},{6,2},{8,12},{10,14},{12,8},{14,10},{16,20},{18,... | collective-permute-start | bytes 3145736 | tf_op jit(solution)/shard_map/ppermute | solution.py:375
  (92 other events, 851.7 us)
